TPU v7x, 32 devices: a whole 2x2x4 slice. The times are simulated.
32 devices in a mesh: band: 16 (over z, y, x), head: 2 (over core).
Axes of the slice: x: 2, y: 2, z: 4, core: 2. Of those that a mesh axis runs over, the one named last changes fastest.
Arguments:
- pixels: bfloat16 [16, 16, 196, 256], P(None, 'band'), may hold values from -6 to 6
- band_mask: int32 [16, 16], replicated, may hold values 0 or 1
- wave_ids: int32 [16, 1], replicated, may hold values from 0 to 15
- pos_embed: bfloat16 [196, 768], replicated, may hold values from -3 to 3
- in_proj: bfloat16 [3, 768, 768], P(None, None, 'head'), may hold values from -0.21875 to 0.21875
- out_proj: bfloat16 [768, 768], P('head'), may hold values from -0.4375 to 0.4375
- up_proj: bfloat16 [768, 3072], P(None, 'head'), may hold values from -0.21875 to 0.21875
- down_proj: bfloat16 [3072, 768], P('head'), may hold values from -0.109375 to 0.109375
- gain_one: bfloat16 [768], replicated, may hold values from 0.5 to 1.5
- gain_two: bfloat16 [768], replicated, may hold values from 0.5 to 1.5
- kernel_gen: bfloat16 [128, 256, 768], P(None, 'band', 'head'), may hold values from -0.01171875 to 0.01171875
- bias_gen: bfloat16 [128, 768], P(None, 'head'), may hold values from -0.1875 to 0.1875
- wave_table: float32 [16, 128], replicated, may hold values from -6 to 6
- hyper_in: float32 [128, 384], replicated, may hold values from -0.5 to 0.5
- hyper_out: float32 [128, 128], replicated, may hold values from -0.5 to 0.5
- hyper_up: float32 [128, 2048], replicated, may hold values from -0.5 to 0.5
- hyper_down: float32 [2048, 128], replicated, may hold values from -0.125 to 0.125
- hyper_gain_one: float32 [128], replicated, may hold values from 0.5 to 1.5
- hyper_gain_two: float32 [128], replicated, may hold values from 0.5 to 1.5
- cotangent: bfloat16 [16, 196, 768], P('band'), may hold values from -6 to 6
Outputs:
- layer_out: bfloat16 [16, 196, 768], P('band')
- grad_pixels: bfloat16 [16, 16, 196, 256], P('head', 'band')
- grad_pos: float32 [196, 768], P(None, 'band')
- grad_in_proj: float32 [3, 768, 768], P(None, 'band', 'head')
- grad_out_proj: float32 [768, 768], P('head', 'band')
- grad_up_proj: float32 [768, 3072], P('band', 'head')
- grad_down_proj: float32 [3072, 768], P('head', 'band')
- grad_gain_one: float32 [768], P('band')
- grad_gain_two: float32 [768], P('band')
- grad_kernel_gen: float32 [128, 256, 768], P(None, 'band', 'head')
- grad_bias_gen: float32 [128, 768], P(None, 'head')
- grad_wave_table: float32 [16, 128], replicated
- grad_hyper_in: float32 [128, 384], replicated
- grad_hyper_out: float32 [128, 128], replicated
- grad_hyper_up: float32 [128, 2048], replicated
- grad_hyper_down: float32 [2048, 128], replicated
- grad_hyper_gain_one: float32 [128], replicated
- grad_hyper_gain_two: float32 [128], replicated
Inputs may be any that keep to these rules, and one draw needn't show every extreme that they name: `wave_ids`: every wavelength from 0 to 15 is the wavelength of some band slot.
All inputs are finite; a program needn't handle non-finite values.
Results may differ from a plain program's by a relative error of at most 0.015.
Values may be sent and summed in bfloat16 or wider, within the bound.
No kernel may reach another device: no remote copies, remote signals or barrier semaphores. Data moves between devices by JAX's collectives and lax.ppermute only.
A program may use at most 256 MiB of HBM per device.

v0:
```python
import jax
import jax.numpy as jnp
from jax import lax
from jax.sharding import PartitionSpec as P

HS = 64
HHEADS = 4


highest = lax.Precision.HIGHEST
norm_epsilon = 1e-06
score_scale = 0.125


def layer_norm(values, gain_vec):
    row_mean = jnp.mean(values, axis=-1, keepdims=True)
    centered = values - row_mean
    variance = jnp.mean(centered * centered, axis=-1, keepdims=True)
    return centered * lax.rsqrt(variance + norm_epsilon) * gain_vec


def gelu_exact(values):
    return jax.nn.gelu(values, approximate=False)


def hyper(wave_table, hyper_in, hyper_out, hyper_up, hyper_down, hyper_gain_one, hyper_gain_two):
    wave_count, hyper_width = wave_table.shape
    head_size = hyper_width // HHEADS
    projected = jnp.dot(wave_table, hyper_in, precision=highest).reshape(
        wave_count, 3, HHEADS, head_size
    )
    scores = jnp.einsum(
        "qhe,khe->hqk", projected[:, 0], projected[:, 1], precision=highest
    ) * head_size ** (-0.5)
    weights = jax.nn.softmax(scores, axis=-1)
    attended = jnp.einsum("hqk,khe->qhe", weights, projected[:, 2], precision=highest).reshape(
        wave_count, hyper_width
    )
    first_out = layer_norm(
        wave_table + jnp.dot(attended, hyper_out, precision=highest), hyper_gain_one
    )
    inner_act = gelu_exact(jnp.dot(first_out, hyper_up, precision=highest))
    return layer_norm(first_out + jnp.dot(inner_act, hyper_down, precision=highest), hyper_gain_two)


def contract_first(left, right):
    return lax.dot_general(
        left, right, (((0,), (0,)), ((), ())), preferred_element_type=jnp.float32
    )


def contract_last(left, right):
    return lax.dot_general(
        left, right, (((1,), (1,)), ((), ())), preferred_element_type=jnp.float32
    )


def shards(
    pixels,
    band_mask,
    wave_ids,
    pos_embed,
    in_proj,
    out_proj,
    up_proj,
    down_proj,
    gain_one,
    gain_two,
    kernel_gen,
    bias_gen,
    wave_table,
    hyper_in,
    hyper_out,
    hyper_up,
    hyper_down,
    hyper_gain_one,
    hyper_gain_two,
    cotangent,
):
    band_index = lax.axis_index("band")
    head_index = lax.axis_index("head")
    band_count = lax.axis_size("band")
    images, slot_local, patches, pixel_count = pixels.shape
    model_width = in_proj.shape[1]
    half_width = in_proj.shape[2]
    wave_count, hyper_width = wave_table.shape
    own_images = images // band_count
    row_total = own_images * patches
    heads_local = half_width // HS
    wave_list = wave_ids[:, 0]
    onehot_all = (wave_list[:, None] == jnp.arange(wave_count, dtype=jnp.int32)[None, :]).astype(
        jnp.float32
    )
    onehot_local = lax.dynamic_slice_in_dim(onehot_all, band_index * slot_local, slot_local, 0)
    mask_all = band_mask.astype(jnp.float32)
    mask_local = lax.dynamic_slice_in_dim(mask_all, band_index * slot_local, slot_local, 1)
    mixture, hyper_back = jax.vjp(
        hyper, wave_table, hyper_in, hyper_out, hyper_up, hyper_down, hyper_gain_one, hyper_gain_two
    )
    mix_low = mixture.astype(jnp.bfloat16)
    gen_flat = kernel_gen.reshape(hyper_width, -1)
    kernel_piece = jnp.dot(mix_low, gen_flat, preferred_element_type=jnp.float32).astype(
        jnp.bfloat16
    )
    kernel_piece = kernel_piece.reshape(wave_count, -1, half_width)
    kernel_all = lax.all_gather(kernel_piece, "band", axis=1, tiled=True)
    wave_bias = jnp.dot(mix_low, bias_gen, preferred_element_type=jnp.float32)
    local_kernels = jnp.einsum(
        "sw,wpd->spd",
        onehot_local.astype(jnp.bfloat16),
        kernel_all,
        preferred_element_type=jnp.float32,
    ).astype(jnp.bfloat16)
    local_bias = jnp.dot(onehot_local, wave_bias, precision=highest)
    row_block = pixels
    mask_block = mask_local
    masked = row_block * mask_block.astype(jnp.bfloat16)[:, :, None, None]
    partial_value = jnp.einsum(
        "isnp,spd->ind", masked, local_kernels, preferred_element_type=jnp.float32
    )
    embed_half = lax.psum_scatter(
        partial_value + jnp.dot(mask_block, local_bias, precision=highest)[:, None, :],
        "band",
        scatter_dimension=0,
        tiled=True,
    )
    embed = lax.all_gather(embed_half.astype(jnp.bfloat16), "head", axis=2, tiled=True).astype(
        embed_half.dtype
    )
    tokens = (embed + pos_embed.astype(jnp.float32)[None]).reshape(row_total, model_width)
    normed, norm_back_one = jax.vjp(layer_norm, tokens, gain_one.astype(jnp.float32))
    normed_low = normed.astype(jnp.bfloat16)
    projected = jnp.einsum("rd,jde->jre", normed_low, in_proj, preferred_element_type=jnp.float32)
    projected = projected.astype(jnp.bfloat16).reshape(3, own_images, patches, heads_local, HS)
    query_rows = projected[0]
    key_rows = projected[1]
    value_rows = projected[2]
    scores = (
        jnp.einsum("iqhe,ikhe->ihqk", query_rows, key_rows, preferred_element_type=jnp.float32)
        * score_scale
    )
    softmax_out = jax.nn.softmax(scores, axis=-1)
    probs_low = softmax_out.astype(jnp.bfloat16)
    attended = jnp.einsum(
        "ihqk,ikhe->iqhe", probs_low, value_rows, preferred_element_type=jnp.float32
    )
    attended = attended.astype(jnp.bfloat16).reshape(row_total, half_width)
    attn_part = jnp.dot(attended, out_proj, preferred_element_type=jnp.float32)
    mid_stream = tokens + lax.psum(attn_part.astype(jnp.bfloat16), "head").astype(jnp.float32)
    second, norm_back_two = jax.vjp(layer_norm, mid_stream, gain_two.astype(jnp.float32))
    second_low = second.astype(jnp.bfloat16)
    hidden = jnp.dot(second_low, up_proj, preferred_element_type=jnp.float32)
    active, gelu_back = jax.vjp(gelu_exact, hidden)
    active_low = active.astype(jnp.bfloat16)
    down_part = jnp.dot(active_low, down_proj, preferred_element_type=jnp.float32)
    result = mid_stream + lax.psum(down_part.astype(jnp.bfloat16), "head").astype(jnp.float32)
    layer_out = result.astype(jnp.bfloat16).reshape(own_images, patches, model_width)
    grad_result = cotangent.astype(jnp.float32).reshape(row_total, model_width)
    grad_low = grad_result.astype(jnp.bfloat16)
    grad_active = contract_last(grad_low, down_proj)
    grad_down = contract_first(active_low, grad_low)
    grad_hidden = gelu_back(grad_active)[0].astype(jnp.bfloat16)
    grad_up = contract_first(second_low, grad_hidden)
    grad_second = lax.psum(contract_last(grad_hidden, up_proj).astype(jnp.bfloat16), "head").astype(
        jnp.float32
    )
    grad_mid_norm, grad_gain_two = norm_back_two(grad_second)
    grad_mid = grad_result + grad_mid_norm
    grad_mid_low = grad_mid.astype(jnp.bfloat16)
    grad_out = contract_first(attended, grad_mid_low)
    grad_attended = contract_last(grad_mid_low, out_proj).astype(jnp.bfloat16)
    grad_attended = grad_attended.reshape(own_images, patches, heads_local, HS)
    grad_probs = jnp.einsum(
        "iqhe,ikhe->ihqk", grad_attended, value_rows, preferred_element_type=jnp.float32
    )
    grad_value = jnp.einsum(
        "ihqk,iqhe->ikhe", probs_low, grad_attended, preferred_element_type=jnp.float32
    )
    grad_scores = softmax_out * (
        grad_probs - jnp.sum(grad_probs * softmax_out, axis=-1, keepdims=True)
    )
    grad_scores_low = grad_scores.astype(jnp.bfloat16)
    grad_query = (
        jnp.einsum("ihqk,ikhe->iqhe", grad_scores_low, key_rows, preferred_element_type=jnp.float32)
        * score_scale
    )
    grad_key = (
        jnp.einsum(
            "ihqk,iqhe->ikhe", grad_scores_low, query_rows, preferred_element_type=jnp.float32
        )
        * score_scale
    )
    grad_projected = jnp.stack([grad_query, grad_key, grad_value]).astype(jnp.bfloat16)
    grad_projected = grad_projected.reshape(3, row_total, half_width)
    grad_in = jnp.einsum(
        "rd,jre->jde", normed_low, grad_projected, preferred_element_type=jnp.float32
    )
    grad_normed_part = jnp.einsum(
        "jre,jde->rd", grad_projected, in_proj, preferred_element_type=jnp.float32
    )
    grad_normed = lax.psum(grad_normed_part.astype(jnp.bfloat16), "head").astype(jnp.float32)
    grad_tokens_norm, grad_gain_one = norm_back_one(grad_normed)
    grad_tokens = grad_mid + grad_tokens_norm
    grad_pos_part = jnp.sum(grad_tokens.reshape(own_images, patches, model_width), axis=0)
    grad_embed = grad_tokens.astype(jnp.bfloat16).reshape(own_images, patches, model_width)
    mask_low = mask_local.astype(jnp.bfloat16)
    grad_embed_half = lax.dynamic_slice_in_dim(grad_embed, head_index * half_width, half_width, 2)
    grad_embed_all = lax.all_gather(grad_embed_half, "band", axis=0, tiled=True)
    row_block = grad_embed_all
    mask_block = mask_local
    partial_value = jnp.einsum(
        "ind,spd->isnp", row_block, local_kernels, preferred_element_type=jnp.float32
    )
    grad_pixels = lax.psum_scatter(
        (partial_value * mask_block[:, :, None, None]).astype(jnp.bfloat16),
        "head",
        scatter_dimension=0,
        tiled=True,
    ).astype(jnp.float32)
    grad_pixels = grad_pixels.astype(jnp.bfloat16)
    masked_local = pixels * mask_low[:, :, None, None]
    grad_local_kernels = jnp.einsum(
        "isnp,ind->spd", masked_local, grad_embed_all, preferred_element_type=jnp.float32
    )
    grad_local_bias = jnp.einsum(
        "is,ind->sd", mask_low, grad_embed_all, preferred_element_type=jnp.float32
    )
    grad_wave_kernels = jnp.einsum(
        "sw,spd->wpd", onehot_local, grad_local_kernels, precision=highest
    )
    grad_kernel_sum = lax.psum_scatter(grad_wave_kernels, "band", scatter_dimension=1, tiled=True)
    grad_kernel_piece = grad_kernel_sum.astype(jnp.bfloat16)
    grad_flat = grad_kernel_piece.reshape(wave_count, -1)
    grad_kernel_gen = contract_first(mix_low, grad_flat).reshape(kernel_gen.shape)
    grad_wave_bias = jnp.dot(onehot_local.T, grad_local_bias, precision=highest)
    grad_mix_part = contract_last(grad_flat, gen_flat)
    grad_mix_part = grad_mix_part + jnp.dot(
        grad_wave_bias, bias_gen.astype(jnp.float32).T, precision=highest
    )
    grad_mix = lax.psum(grad_mix_part, ("band", "head"))
    hyper_grads = hyper_back(grad_mix)
    bias_part = jnp.dot(mix_low.astype(jnp.float32).T, grad_wave_bias, precision=highest)
    grad_bias_gen = lax.psum(bias_part, "band")
    summed = (
        lax.psum_scatter(grad_in, "band", scatter_dimension=1, tiled=True),
        lax.psum_scatter(grad_out, "band", scatter_dimension=1, tiled=True),
        lax.psum_scatter(grad_up, "band", scatter_dimension=0, tiled=True),
        lax.psum_scatter(grad_down, "band", scatter_dimension=1, tiled=True),
        lax.psum_scatter(grad_gain_one, "band", scatter_dimension=0, tiled=True),
        lax.psum_scatter(grad_gain_two, "band", scatter_dimension=0, tiled=True),
        lax.psum_scatter(grad_pos_part, "band", scatter_dimension=1, tiled=True),
    )
    return (
        layer_out,
        grad_pixels,
        summed[6],
        summed[0],
        summed[1],
        summed[2],
        summed[3],
        summed[4],
        summed[5],
        grad_kernel_gen,
        grad_bias_gen,
        hyper_grads[0],
        hyper_grads[1],
        hyper_grads[2],
        hyper_grads[3],
        hyper_grads[4],
        hyper_grads[5],
        hyper_grads[6],
    )


def solution(mesh):
    in_specs = (
        P(None, "band", None, None),
        P(),
        P(),
        P(),
        P(None, None, "head"),
        P("head", None),
        P(None, "head"),
        P("head", None),
        P(),
        P(),
        P(None, "band", "head"),
        P(None, "head"),
        P(),
        P(),
        P(),
        P(),
        P(),
        P(),
        P(),
        P("band", None, None),
    )
    out_specs = (
        P("band", None, None),
        P("head", "band", None, None),
        P(None, "band"),
        P(None, "band", "head"),
        P("head", "band"),
        P("band", "head"),
        P("head", "band"),
        P("band"),
        P("band"),
        P(None, "band", "head"),
        P(None, "head"),
        P(),
        P(),
        P(),
        P(),
        P(),
        P(),
        P(),
    )
    return jax.shard_map(shards, mesh=mesh, in_specs=in_specs, out_specs=out_specs, check_vma=False)
```

profile of v0, /device:TPU:0, one launch (start us, length us, event | category | flops | bytes accessed | tf_op | source)
XLA Modules:
  0.0 1293.7 jit_solution(7931495204307640268)
XLA Ops:
  20.6 66.9 %all-gather.5.cloned.1.call-done = bf16[16,256,384]{2,1,0:T(8,128)(2,1)} async-done(((bf16[16,16,384]{2,1,0:T(8,128)(2,1)}), bf16[16,256,384]{2,1,0:T(8,128)(2,1)}) %all-gather.5.cloned.1.call-update) | async-done | bytes 3145744 | tf_op jit(solution)/shard_map/all_gather | solution.py:106
  87.5 3.9 fusion.2
  92.2 3.4 broadcast_add_fusion
  96.3 136.1 %reduce-scatter.24.cloned.1.call-done = f32[1,196,384]{2,1,0:T(8,128)} async-done(((f32[16,196,384]{2,1,0:T(8,128)}), f32[1,196,384]{2,1,0:T(8,128)}) %reduce-scatter.24.cloned.1.call-update) | async-done | bytes 301072
  243.3 17.4 %all-reduce.15.cloned.1.call-done = bf16[196,768]{1,0:T(8,128)(2,1)} async-done(((bf16[196,768]{1,0:T(8,128)(2,1)}), bf16[196,768]{1,0:T(8,128)(2,1)}) %all-reduce.15.cloned.1.call-update) | async-done | bytes 301072 | tf_op jit(solution)/shard_map/psum | solution.py:149
  262.8 3.9 multiply_convert_fusion.1
  270.3 3.2 convolution_convert_fusion.4
  273.5 16.3 %all-reduce.17.cloned.1.call-done = bf16[196,768]{1,0:T(8,128)(2,1)} async-done(((bf16[196,768]{1,0:T(8,128)(2,1)}), bf16[196,768]{1,0:T(8,128)(2,1)}) %all-reduce.17.cloned.1.call-update) | async-done | bytes 301072 | tf_op jit(solution)/shard_map/psum | solution.py:164
  300.3 3.1 fusion.18
  303.6 20.2 %all-reduce.21.cloned.1.call-done = (bf16[196,768]{1,0:T(8,128)(2,1)}, bf16[196,768]{1,0:T(8,128)(2,1)}) async-done(((bf16[196,768]{1,0:T(8,128)(2,1)}, bf16[196,768]{1,0:T(8,128)(2,1)}), (bf16[196,768]{1,0:T(8,128)(2,1)}, bf16[196,768]{1,0:T(8,128)(2,1)})) %all-reduce.21.cloned.1.call-update) | async-done | bytes 602128 | tf_op jit(solution)/shard_map/psum | solution.py:156
  327.7 64.4 %all-gather.7.cloned.1.call-done = bf16[16,196,384]{2,1,0:T(8,128)(2,1)} async-done(((bf16[1,196,384]{2,1,0:T(8,128)(2,1)}), bf16[16,196,384]{2,1,0:T(8,128)(2,1)}) %all-gather.7.cloned.1.call-update) | async-done | bytes 2408464 | tf_op jit(solution)/shard_map/all_gather | solution.py:208
  392.0 4.1 fusion.10
  399.8 6.3 copy.113
  413.5 3.3 broadcast_multiply_fusion
  419.7 3.2 fusion.122
  429.0 42.9 %all-reduce.7 = (f32[768]{0:T(1024)S(1)}, f32[768]{0:T(1024)S(1)}) all-reduce(f32[768]{0:T(1024)S(1)} %get-tuple-element.72, f32[768]{0:T(1024)S(1)} %get-tuple-element.74), channel_id=10, replica_groups=mesh['band'=16,'head'=2] {'band'}, use_global_device_ids=true, to_apply=%region_29.0.clone | all-reduce | flops 1536 | bytes 12288
  476.0 122.1 %all-reduce.19.cloned.1.call-done = (f32[3,768,384]{2,0,1:T(4,128)}, f32[128,384]{1,0:T(8,128)}) async-done(((f32[3,768,384]{2,0,1:T(4,128)}, f32[128,384]{1,0:T(8,128)}), (f32[3,768,384]{2,0,1:T(4,128)}, f32[128,384]{1,0:T(8,128)})) %all-reduce.19.cloned.1.call-update) | async-done | bytes 3735568
  599.9 148.1 %reduce-scatter.20.cloned.1.call-done = f32[16,16,384]{2,1,0:T(8,128)} async-done(((f32[16,256,384]{2,1,0:T(8,128)}), f32[16,16,384]{2,1,0:T(8,128)}) %reduce-scatter.20.cloned.1.call-update) | async-done | bytes 393232 | tf_op jit(solution)/shard_map/reduce_scatter | solution.py:231
  749.8 40.2 %psum.47 = f32[16,128]{1,0:T(8,128)S(1)} all-reduce(f32[16,128]{1,0:T(8,128)S(1)} %convolution_add_fusion.2), channel_id=1, replica_groups=mesh['band'=16,'head'=2] {'band','head'}, use_global_device_ids=true, to_apply=%region_35.0 | all-reduce | flops 2048 | bytes 16384 | tf_op jit(solution)/shard_map/psum | solution.py:240
  798.5 3.5 copy.124
  808.9 65.6 %reduce-scatter.22.cloned.1.call-done = f32[48,196]{1,0:T(8,128)} async-done(((f32[768,196]{1,0:T(8,128)}), f32[48,196]{1,0:T(8,128)}) %reduce-scatter.22.cloned.1.call-update) | async-done | bytes 37648
  874.5 127.9 %reduce-scatter.14.cloned.1.call-done = f32[384,48]{0,1:T(8,128)} async-done(((f32[384,768]{0,1:T(8,128)}), f32[384,48]{0,1:T(8,128)}) %reduce-scatter.14.cloned.1.call-update) | async-done | bytes 73744 | tf_op jit(solution)/shard_map/reduce_scatter | solution.py:246
  1002.5 141.6 %reduce-scatter.16.cloned.1.call-done = f32[48,1536]{1,0:T(8,128)} async-done(((f32[768,1536]{1,0:T(8,128)}), f32[48,1536]{1,0:T(8,128)}) %reduce-scatter.16.cloned.1.call-update) | async-done | bytes 294928 | tf_op jit(solution)/shard_map/reduce_scatter | solution.py:247
  1144.0 142.1 %reduce-scatter.18.cloned.1.call-done = f32[1536,48]{0,1:T(8,128)} async-done(((f32[1536,768]{0,1:T(8,128)}), f32[1536,48]{0,1:T(8,128)}) %reduce-scatter.18.cloned.1.call-update) | async-done | bytes 294928 | tf_op jit(solution)/shard_map/reduce_scatter | solution.py:248
  (335 shorter events, 87.9 us)
Async XLA Ops:
  7.2 255.6 %copy-start = (bf16[768,1536]{1,0:T(8,128)(2,1)S(1)}, bf16[768,1536]{1,0:T(8,128)(2,1)}, u32[]{:S(2)}) copy-start(bf16[768,1536]{1,0:T(8,128)(2,1)} %param.26) | copy-start | bytes 7077892
  7.2 80.3 %all-gather.5.cloned.1.call-start = ((), (), s32[]{:S(2)}) async-start(), calls=%async_computation.7 | async-start | bytes 3342336 | tf_op jit(solution)/shard_map/all_gather | solution.py:106
  16.9 215.5 %reduce-scatter.24.cloned.1.call-start = ((), (), s32[]{:S(2)}) async-start(), calls=%async_computation.17 | async-start | bytes 5222400
  95.6 140.0 %copy-start.2 = (bf16[196,768]{1,0:T(8,128)(2,1)S(1)}, bf16[196,768]{1,0:T(8,128)(2,1)}, u32[]{:S(2)}) copy-start(bf16[196,768]{1,0:T(8,128)(2,1)} %param.23) | copy-start | bytes 903172
  95.7 165.0 %all-reduce.15.cloned.1.call-start = ((), (), s32[]{:S(2)}) async-start(), calls=%async_computation.8 | async-start | bytes 614400 | tf_op jit(solution)/shard_map/psum | solution.py:149
  243.1 46.8 %all-reduce.17.cloned.1.call-start = ((), (), s32[]{:S(2)}) async-start(), calls=%async_computation.9 | async-start | bytes 614400 | tf_op jit(solution)/shard_map/psum | solution.py:164
  270.2 53.5 %all-reduce.21.cloned.1.call-start = ((), (), s32[]{:S(2)}) async-start(), calls=%async_computation.19 | async-start | bytes 1228800 | tf_op jit(solution)/shard_map/psum | solution.py:156
  303.5 88.5 %all-gather.7.cloned.1.call-start = ((), (), s32[]{:S(2)}) async-start(), calls=%async_computation.15 | async-start | bytes 2611200 | tf_op jit(solution)/shard_map/all_gather | solution.py:208
  327.6 146.2 %reduce-scatter.12.cloned.1.call-start = ((), (), s32[]{:S(2)}) async-start(), calls=%async_computation.10 | async-start | bytes 2457600 | tf_op jit(solution)/shard_map/reduce_scatter | solution.py:214
  396.1 202.0 %all-reduce.19.cloned.1.call-start = ((), (), s32[]{:S(2)}) async-start(), calls=%async_computation.18 | async-start | bytes 9830400
  409.3 338.7 %reduce-scatter.20.cloned.1.call-start = ((), (), s32[]{:S(2)}) async-start(), calls=%async_computation.14 | async-start | bytes 6684672 | tf_op jit(solution)/shard_map/reduce_scatter | solution.py:231
  416.8 457.7 %reduce-scatter.22.cloned.1.call-start = ((), (), s32[]{:S(2)}) async-start(), calls=%async_computation.16 | async-start | bytes 835584
  418.1 584.4 %reduce-scatter.14.cloned.1.call-start = ((), (), s32[]{:S(2)}) async-start(), calls=%async_computation.11 | async-start | bytes 1253376 | tf_op jit(solution)/shard_map/reduce_scatter | solution.py:246
  419.7 724.3 %reduce-scatter.16.cloned.1.call-start = ((), (), s32[]{:S(2)}) async-start(), calls=%async_computation.12 | async-start | bytes 5013504 | tf_op jit(solution)/shard_map/reduce_scatter | solution.py:247
  423.0 863.1 %reduce-scatter.18.cloned.1.call-start = ((), (), s32[]{:S(2)}) async-start(), calls=%async_computation.13 | async-start | bytes 5013504 | tf_op jit(solution)/shard_map/reduce_scatter | solution.py:248
  476.0 272.9 %copy-start.21 = (bf16[128,16,384]{2,1,0:T(8,128)(2,1)S(1)}, bf16[128,16,384]{2,1,0:T(8,128)(2,1)}, u32[]{:S(2)}) copy-start(bf16[128,16,384]{2,1,0:T(8,128)(2,1)} %param.30) | copy-start | bytes 4718596
  599.8 149.7 %copy-start.48 = (bf16[128,384]{1,0:T(8,128)(2,1)S(1)}, bf16[128,384]{1,0:T(8,128)(2,1)}, u32[]{:S(2)}) copy-start(bf16[128,384]{1,0:T(8,128)(2,1)} %param.31) | copy-start | bytes 294916
  599.8 190.2 %copy-start.72 = (f32[16]{0:T(128)S(1)}, f32[16]{0:T(128)}, u32[]{:S(2)}) copy-start(f32[16]{0:T(128)} %copy-done.71) | copy-start | bytes 196
  599.8 190.2 %copy-start.79 = (f32[128]{0:T(128)S(1)}, f32[128]{0:T(128)}, u32[]{:S(2)}) copy-start(f32[128]{0:T(128)} %param.38) | copy-start | bytes 1540
  599.8 190.2 %copy-start.81 = (f32[16]{0:T(128)S(1)}, f32[16]{0:T(128)}, u32[]{:S(2)}) copy-start(f32[16]{0:T(128)} %copy-done.80) | copy-start | bytes 196
  599.8 190.9 %copy-start.90 = (f32[16]{0:T(128)S(1)}, f32[16]{0:T(128)}, u32[]{:S(2)}) copy-start(f32[16]{0:T(128)} %copy-done.89) | copy-start | bytes 196
  599.9 191.1 %copy-start.40 = (f32[16,2048]{1,0:T(8,128)S(1)}, f32[16,2048]{1,0:T(8,128)}, u32[]{:S(2)}) copy-start(f32[16,2048]{1,0:T(8,128)} %copy-done.39) | copy-start | bytes 393220
  803.9 482.9 %copy-start.1 = (bf16[768,1536]{1,0:T(8,128)(2,1)S(1)}, bf16[768,1536]{1,0:T(8,128)(2,1)}, u32[]{:S(2)}) copy-start(bf16[768,1536]{1,0:T(8,128)(2,1)} %param.26) | copy-start | bytes 7077892
  806.8 479.3 %copy-start.37 = (f32[128,384]{1,0:T(8,128)S(1)}, f32[128,384]{1,0:T(8,128)}, u32[]{:S(2)}) copy-start(f32[128,384]{1,0:T(8,128)} %get-tuple-element.126) | copy-start | bytes 589828
  (84 other events, 521.9 us)
Sparse Core Ops, SparseCore 0:
  17.0 70.4 all-gather.4
  95.8 136.6 reduce-scatter.23
  243.2 17.4 all-reduce.14
  270.3 19.5 all-reduce.16
  303.6 20.0 all-reduce.20
  327.7 64.2 all-gather.6
  396.2 7.9 reduce-scatter.11
  411.6 186.5 all-reduce.18
  603.4 144.5 reduce-scatter.19
  753.1 121.4 reduce-scatter.21
  879.9 122.5 reduce-scatter.13
  1008.1 135.9 reduce-scatter.15
  1150.6 135.4 reduce-scatter.17
where the time goes:
time: 1300 us; the launch traced here: 1290 us
  waiting for transfers between devices  1070 us (82%)
  blocking collectives  85.1 us (7%)
  matrix products  68.8 us (5%)
  local copies, waits for them, and re-layouts  31.9 us (2%)
  other arithmetic  21.9 us (2%)
  between operations  16.2 us (1%)
    unnamed x16, waiting for transfers between devices  324 us
    reduce_scatter x1, waiting for transfers between devices, shards(): lax.psum_scatter(grad_wave_kernels, 'band', scatter_dimension=1, tiled=True)  148 us
    reduce_scatter x1, waiting for transfers between devices, shards(): lax.psum_scatter(grad_down, 'band', scatter_dimension=1, tiled=True)  142 us
    reduce_scatter x1, waiting for transfers between devices, shards(): lax.psum_scatter(grad_up, 'band', scatter_dimension=0, tiled=True)  142 us
    reduce_scatter x1, waiting for transfers between devices, shards(): lax.psum_scatter(grad_out, 'band', scatter_dimension=1, tiled=True)  128 us
    all_gather x1, waiting for transfers between devices, shards(): kernel_all = lax.all_gather(kernel_piece, 'band', axis=1, tiled=True)  66.9 us
    all_gather x1, waiting for transfers between devices, shards(): grad_embed_all = lax.all_gather(grad_embed_half, 'band', axis=0, tiled=True)  64.4 us
    unnamed x1, blocking collectives  42.9 us
  transfers between devices with their start and end apart: 13, of which 12 were waited for; matrix products, arithmetic and copies ran while one was open for 5% of the time, Pallas kernels for 0%

commit v1 on v0

v1 whole, which is shorter than its diff:
```python
import jax
import jax.numpy as jnp
import numpy as np
from jax import lax
from jax.experimental import pallas as pl
from jax.experimental.pallas import tpu as pltpu
from jax.sharding import PartitionSpec as P

HS = 64
HHEADS = 4
LANES = 128
EXTRA = 256

highest = lax.Precision.HIGHEST
norm_epsilon = 1e-06
score_scale = 0.125
root_half = 0.7071067811865476
density_scale = 0.3989422804014327
f32 = jnp.float32
bf16 = jnp.bfloat16


def norm_parts(values):
    centered = values - jnp.mean(values, axis=-1, keepdims=True)
    variance = jnp.mean(centered * centered, axis=-1, keepdims=True)
    scale = lax.rsqrt(variance + norm_epsilon)
    return centered * scale, scale


def norm_grad(grad, normal, scale):
    inner = jnp.mean(grad, axis=-1, keepdims=True)
    along = jnp.mean(grad * normal, axis=-1, keepdims=True)
    return scale * (grad - inner - normal * along)


def gelu_parts(values):
    cumulative = 0.5 * (1.0 + lax.erf(values * root_half))
    density = jnp.exp(-0.5 * values * values) * density_scale
    return cumulative, cumulative + values * density


def contract_first(left, right):
    return lax.dot_general(left, right, (((0,), (0,)), ((), ())), preferred_element_type=f32)


def contract_last(left, right):
    return lax.dot_general(left, right, (((1,), (1,)), ((), ())), preferred_element_type=f32)


def exact(left, right, dims=((1,), (0,))):
    return lax.dot_general(
        left, right, (dims, ((), ())), precision=highest, preferred_element_type=f32
    )


FIRST = ((0,), (0,))
LAST = ((1,), (1,))


def low_dot(left, right):
    return jnp.dot(left, right, preferred_element_type=f32)


def equal_index(rows, columns, row_shift, column_shift, row_mask, column_mask):
    row = lax.broadcasted_iota(jnp.int32, (rows, columns), 0)
    column = lax.broadcasted_iota(jnp.int32, (rows, columns), 1)
    return ((row >> row_shift) & row_mask) == ((column >> column_shift) & column_mask)


def onehot_of(wave_column, wave_count):
    slots = wave_column.shape[0]
    return wave_column == lax.broadcasted_iota(jnp.int32, (slots, wave_count), 1)


def spread(mix, piece):
    rows, width = mix.shape
    shift = piece.bit_length() - 1
    all_bits = 2**30 - 1
    repeat_rows = equal_index(rows * piece, rows, shift, 0, all_bits, all_bits)
    repeat_columns = equal_index(width, width * piece, 0, shift, all_bits, all_bits)
    tall = low_dot(repeat_rows.astype(bf16), mix).astype(bf16)
    return low_dot(tall, repeat_columns.astype(bf16))


def kron_identity(mix, piece):
    rows, width = mix.shape
    same = equal_index(rows * piece, width * piece, 0, 0, piece - 1, piece - 1)
    return jnp.where(same, spread(mix, piece), 0.0).astype(bf16)


def head_lanes(width, head_size, head):
    lane = lax.broadcasted_iota(jnp.int32, (1, width), 1)
    return (lane >> (head_size.bit_length() - 1)) == head


def hop(values, step):
    count = lax.axis_size("band")
    return lax.ppermute(values, "band", [(i, i ^ step) for i in range(count)])


def swap(values):
    return lax.ppermute(values, "head", [(0, 1), (1, 0)])


def head_sum(part):
    low = part.astype(bf16)
    return low.astype(f32) + swap(low).astype(f32)


def gather_orders(count):
    steps = []
    step = count // 2
    while step:
        steps.append(step)
        step //= 2
    if len(steps) < 4:
        return [tuple(steps)] * 3
    head, (c, b, a) = tuple(steps[:-3]), steps[-3:]
    return [head + (c, b, a), head + (a, c, b), head + (b, a, c)]


def relative_index(position, order):
    index = 0
    for t, step in enumerate(order):
        index = index + ((position >> t) & 1) * step
    return index


def position_of(index, order):
    position = 0
    for t, step in enumerate(order):
        position = position + (((index >> (step.bit_length() - 1)) & 1) << t)
    return position


def scatter_sum(keeps, sends, orders, arriving=None):
    if arriving is None:
        arriving = [hop(send, order[-1]) for send, order in zip(sends, orders)]
    for t in range(len(orders[0]) - 2, -1, -1):
        sends, kept = [], []
        for k, a in zip(keeps, arriving):
            half = k.shape[0] // 2
            sends.append((k[half:].astype(f32) + a[half:].astype(f32)).astype(bf16))
            kept.append(k[:half].astype(f32) + a[:half].astype(f32))
        keeps = kept
        if t == 0 and len({order[0] for order in orders}) == 1:
            merged = hop(jnp.concatenate(sends, axis=-1), orders[0][0])
            arriving, start = [], 0
            for send in sends:
                arriving.append(merged[..., start : start + send.shape[-1]])
                start += send.shape[-1]
        else:
            arriving = [hop(send, order[t]) for send, order in zip(sends, orders)]
    return [k.astype(f32) + a.astype(f32) for k, a in zip(keeps, arriving)]


def loop(count, body):
    if count <= 16:
        for q in range(count):
            body(q)
    else:

        def step(q, carry):
            body(q)
            return carry

        lax.fori_loop(0, count, step, 0)


def span(c):
    return slice(c * LANES, (c + 1) * LANES)


def local_call(kernel, where, tables, args, out_shape, scratch=(), name=None, flops=0):
    vmem = pl.BlockSpec(memory_space=pltpu.VMEM)
    smem = pl.BlockSpec(memory_space=pltpu.SMEM)
    moved = sum(x.size * x.dtype.itemsize for x in args)
    moved += sum(int(np.prod(s.shape)) * s.dtype.itemsize for s in out_shape)
    return pl.pallas_call(
        kernel,
        in_specs=[smem] * (1 + len(tables)) + [vmem] * len(args),
        out_specs=[vmem] * len(out_shape),
        out_shape=list(out_shape),
        scratch_shapes=list(scratch),
        cost_estimate=pl.CostEstimate(flops=flops, bytes_accessed=moved, transcendentals=0),
        compiler_params=pltpu.CompilerParams(vmem_limit_bytes=56 * 2**20),
        name=name,
    )(where, *tables, *args)


def hyper_forward(where, wave_ids, band_mask, table, weights, gains, gen_rows, bias_gen, count):
    slots = wave_ids.shape[0]
    wave_count, width = table.shape
    piece = gen_rows.shape[0] // width
    half_width = gen_rows.shape[1]
    inner = weights[2].shape[1]
    head_size = width // HHEADS

    def kernel(
        where_ref, ids_ref, mask_ref, table_ref, in_ref, out_ref, up_ref, down_ref, one_ref,
        two_ref, gen_ref, bias_ref, piece_out, image_bias_out, mix_out, projected_out, probs_out,
        attended_out, normal_one_out, scale_one_out, hidden_out, normal_two_out, scale_two_out,
    ):
        values = table_ref[...]
        projected = exact(values, in_ref[...])
        projected_out[...] = projected
        query, key, value = (projected[:, i * width : (i + 1) * width] for i in range(3))
        attended = jnp.zeros((wave_count, width), f32)
        for head in range(HHEADS):
            lanes = head_lanes(width, head_size, head)
            scores = exact(jnp.where(lanes, query, 0.0), key, LAST) * head_size ** (-0.5)
            scores = jnp.exp(scores - jnp.max(scores, axis=-1, keepdims=True))
            probs = scores / jnp.sum(scores, axis=-1, keepdims=True)
            probs_out[head] = probs
            attended += exact(probs, jnp.where(lanes, value, 0.0))
        attended_out[...] = attended
        normal_one, scale_one = norm_parts(values + exact(attended, out_ref[...]))
        first = normal_one * one_ref[...]
        hidden = exact(first, up_ref[...])
        factor, _ = gelu_parts(hidden)
        normal_two, scale_two = norm_parts(first + exact(hidden * factor, down_ref[...]))
        mix = (normal_two * two_ref[...]).astype(bf16)
        normal_one_out[...] = normal_one
        scale_one_out[...] = scale_one
        hidden_out[...] = hidden
        normal_two_out[...] = normal_two
        scale_two_out[...] = scale_two
        mix_out[...] = mix
        onehot = onehot_of(ids_ref[...], wave_count)
        slot_mix = low_dot(onehot.astype(bf16), mix).astype(bf16)
        piece_out[...] = low_dot(kron_identity(slot_mix, piece), gen_ref[...]).astype(bf16)
        image = lax.broadcasted_iota(jnp.int32, mask_ref.shape, 0) == where_ref[0]
        bands = jnp.sum(jnp.where(image, mask_ref[...], 0).astype(f32), axis=0, keepdims=True)
        waves = exact(bands, onehot.astype(f32))
        image_bias_out[...] = exact(waves, low_dot(mix, bias_ref[...]))

    def shape(*dims):
        return jax.ShapeDtypeStruct(dims, f32)

    return local_call(
        kernel,
        where,
        [],
        [wave_ids, band_mask, table, *weights, *gains, gen_rows, bias_gen],
        [
            jax.ShapeDtypeStruct((slots * piece, half_width), bf16),
            shape(1, half_width),
            jax.ShapeDtypeStruct((wave_count, width), bf16),
            shape(wave_count, 3 * width),
            shape(HHEADS, wave_count, wave_count),
            shape(wave_count, width),
            shape(wave_count, width),
            shape(wave_count, 1),
            shape(wave_count, inner),
            shape(wave_count, width),
            shape(wave_count, 1),
        ],
        name="hyper_forward",
        flops=8 * slots * piece * gen_rows.size,
    )


def hyper_backward(where, grad_mix, table, weights, gains, kept):
    wave_count, width = table.shape
    head_size = width // HHEADS

    def kernel(
        where_ref, grad_ref, table_ref, in_ref, out_ref, up_ref, down_ref, one_ref, two_ref,
        projected_ref, probs_ref, attended_ref, normal_one_ref, scale_one_ref, hidden_ref,
        normal_two_ref, scale_two_ref, table_out, in_out, out_out, up_out, down_out, one_out,
        two_out,
    ):
        grad = grad_ref[...]
        normal_two = normal_two_ref[...]
        two_out[...] = jnp.sum(grad * normal_two, axis=0, keepdims=True)
        grad_two = norm_grad(grad * two_ref[...], normal_two, scale_two_ref[...])
        hidden = hidden_ref[...]
        factor, slope = gelu_parts(hidden)
        normal_one = normal_one_ref[...]
        first = normal_one * one_ref[...]
        grad_hidden = exact(grad_two, down_ref[...], LAST) * slope
        down_out[...] = exact(hidden * factor, grad_two, FIRST)
        up_out[...] = exact(first, grad_hidden, FIRST)
        grad_first = grad_two + exact(grad_hidden, up_ref[...], LAST)
        one_out[...] = jnp.sum(grad_first * normal_one, axis=0, keepdims=True)
        grad_one = norm_grad(grad_first * one_ref[...], normal_one, scale_one_ref[...])
        out_out[...] = exact(attended_ref[...], grad_one, FIRST)
        grad_attended = exact(grad_one, out_ref[...], LAST)
        projected = projected_ref[...]
        query, key, value = (projected[:, i * width : (i + 1) * width] for i in range(3))
        grads = [jnp.zeros((wave_count, width), f32) for _ in range(3)]
        for head in range(HHEADS):
            lanes = head_lanes(width, head_size, head)
            own = jnp.where(lanes, grad_attended, 0.0)
            probs = probs_ref[head]
            grad_probs = exact(own, value, LAST)
            grads[2] += exact(probs, own, FIRST)
            scores = probs * (grad_probs - jnp.sum(grad_probs * probs, axis=-1, keepdims=True))
            scores = scores * head_size ** (-0.5)
            grads[0] += exact(scores, jnp.where(lanes, key, 0.0))
            grads[1] += exact(scores, jnp.where(lanes, query, 0.0), FIRST)
        grad_projected = jnp.concatenate(grads, axis=1)
        in_out[...] = exact(table_ref[...], grad_projected, FIRST)
        table_out[...] = grad_one + exact(grad_projected, in_ref[...], LAST)

    arrays = [table, *weights, *gains]
    return local_call(
        kernel,
        where,
        [],
        [grad_mix, *arrays, *kept],
        [jax.ShapeDtypeStruct(a.shape, f32) for a in arrays],
        name="hyper_backward",
        flops=80 * wave_count * weights[2].size,
    )


def attention_forward(where, own, other, pos, gain, in_proj, out_proj):
    patches, half_width = own.shape
    width = 2 * half_width
    heads = half_width // HS

    def kernel(
        where_ref, own_ref, other_ref, pos_ref, gain_ref, in_ref, out_ref, tokens_out, normed_out,
        query_out, key_out, value_out, probs_out, attended_out, part_out,
    ):
        own_half, other_half = own_ref[...].astype(f32), other_ref[...].astype(f32)
        first = where_ref[1] == 0
        embed = jnp.concatenate(
            [jnp.where(first, own_half, other_half), jnp.where(first, other_half, own_half)], axis=1
        )
        tokens = embed + pos_ref[...].astype(f32)
        tokens_out[...] = tokens
        normal, _ = norm_parts(tokens)
        normed = (normal * gain_ref[...].astype(f32)).astype(bf16)
        normed_out[...] = normed
        projected = [low_dot(normed, in_ref[j]).astype(bf16) for j in range(3)]
        query_out[...], key_out[...], value_out[...] = projected
        for pair in range(heads // 2):
            lanes = slice(pair * 2 * HS, (pair + 1) * 2 * HS)
            query, key, value = (p[:, lanes] for p in projected)
            total = None
            for side in range(2):
                mine = head_lanes(2 * HS, HS, side)
                scores = contract_last(jnp.where(mine, query, 0), key) * score_scale
                scores = jnp.exp(scores - jnp.max(scores, axis=-1, keepdims=True))
                probs = scores / jnp.sum(scores, axis=-1, keepdims=True)
                probs_out[2 * pair + side] = probs
                part = low_dot(probs.astype(bf16), jnp.where(mine, value, 0))
                total = part if total is None else total + part
            attended_out[:, lanes] = total.astype(bf16)
        part_out[...] = low_dot(attended_out[...], out_ref[...]).astype(bf16)

    def low(*dims):
        return jax.ShapeDtypeStruct(dims, bf16)

    return local_call(
        kernel,
        where,
        [],
        [own, other, pos, gain, in_proj, out_proj],
        [
            jax.ShapeDtypeStruct((patches, width), f32),
            low(patches, width),
            low(patches, half_width),
            low(patches, half_width),
            low(patches, half_width),
            jax.ShapeDtypeStruct((heads, patches, patches), f32),
            low(patches, half_width),
            low(patches, width),
        ],
        name="attention_forward",
        flops=2 * patches * (in_proj.size + out_proj.size + 4 * patches * half_width),
    )


def feed_forward(where, tokens, own, other, gain, up, down, cotangent):
    patches, width = tokens.shape
    local = up.shape[1]
    tile = local // 3

    def kernel(
        where_ref, tokens_ref, own_ref, other_ref, gain_ref, up_ref, down_ref, cotangent_ref,
        mid_out, second_out, active_out, grad_hidden_out, parts_out,
    ):
        mid = tokens_ref[...] + (own_ref[...].astype(f32) + other_ref[...].astype(f32))
        mid_out[...] = mid
        normal, _ = norm_parts(mid)
        second = (normal * gain_ref[...].astype(f32)).astype(bf16)
        second_out[...] = second
        for t in range(3):
            columns = slice(t * tile, (t + 1) * tile)
            hidden = low_dot(second, up_ref[:, columns])
            factor, slope = gelu_parts(hidden)
            active_out[:, columns] = (hidden * factor).astype(bf16)
            grad_active = contract_last(cotangent_ref[...], down_ref[columns, :])
            grad_hidden_out[:, columns] = (grad_active * slope).astype(bf16)
        parts_out[0] = low_dot(active_out[...], down_ref[...]).astype(bf16)
        parts_out[1] = contract_last(grad_hidden_out[...], up_ref[...]).astype(bf16)

    return local_call(
        kernel,
        where,
        [],
        [tokens, own, other, gain, up, down, cotangent],
        [
            jax.ShapeDtypeStruct((patches, width), f32),
            jax.ShapeDtypeStruct((patches, width), bf16),
            jax.ShapeDtypeStruct((patches, local), bf16),
            jax.ShapeDtypeStruct((patches, local), bf16),
            jax.ShapeDtypeStruct((2, patches, width), bf16),
        ],
        name="feed_forward",
        flops=8 * patches * up.size,
    )


def attention_backward(
    where, mid, own, other, cotangent, gain, in_proj, out_proj, query, key, value, probs
):
    patches, width = mid.shape
    half_width = width // 2
    heads = half_width // HS

    def kernel(
        where_ref, mid_ref, own_ref, other_ref, cotangent_ref, gain_ref, in_ref, out_ref,
        query_ref, key_ref, value_ref, probs_ref, layer_out, gain_out, grad_mid_out, low_out,
        query_out, key_out, value_out, part_out,
    ):
        mid_values = mid_ref[...]
        down = own_ref[0].astype(f32) + other_ref[0].astype(f32)
        layer_out[...] = (mid_values + down).astype(bf16)
        grad_second = own_ref[1].astype(f32) + other_ref[1].astype(f32)
        normal, scale = norm_parts(mid_values)
        gain_out[...] = jnp.sum(grad_second * normal, axis=0, keepdims=True)
        grad_mid = cotangent_ref[...].astype(f32) + norm_grad(
            grad_second * gain_ref[...].astype(f32), normal, scale
        )
        grad_mid_out[...] = grad_mid
        grad_low = grad_mid.astype(bf16)
        low_out[...] = grad_low
        grad_attended = contract_last(grad_low, out_ref[...]).astype(bf16)
        for pair in range(heads // 2):
            lanes = slice(pair * 2 * HS, (pair + 1) * 2 * HS)
            query, key, value = query_ref[:, lanes], key_ref[:, lanes], value_ref[:, lanes]
            totals = [None] * 3
            for side in range(2):
                mine = head_lanes(2 * HS, HS, side)
                own_grad = jnp.where(mine, grad_attended[:, lanes], 0)
                probs = probs_ref[2 * pair + side]
                grad_probs = contract_last(own_grad, value)
                inner = jnp.sum(grad_probs * probs, axis=-1, keepdims=True)
                scores = (probs * (grad_probs - inner)).astype(bf16)
                parts = (
                    low_dot(scores, jnp.where(mine, key, 0)),
                    contract_first(scores, jnp.where(mine, query, 0)),
                    contract_first(probs.astype(bf16), own_grad),
                )
                totals = [p if t is None else t + p for t, p in zip(totals, parts)]
            query_out[:, lanes] = (totals[0] * score_scale).astype(bf16)
            key_out[:, lanes] = (totals[1] * score_scale).astype(bf16)
            value_out[:, lanes] = totals[2].astype(bf16)
        part = contract_last(query_out[...], in_ref[0])
        part += contract_last(key_out[...], in_ref[1])
        part += contract_last(value_out[...], in_ref[2])
        part_out[...] = part.astype(bf16)

    def low(*dims):
        return jax.ShapeDtypeStruct(dims, bf16)

    return local_call(
        kernel,
        where,
        [],
        [mid, own, other, cotangent, gain, in_proj, out_proj, query, key, value, probs],
        [
            low(patches, width),
            jax.ShapeDtypeStruct((1, width), f32),
            jax.ShapeDtypeStruct((patches, width), f32),
            low(patches, width),
            low(patches, half_width),
            low(patches, half_width),
            low(patches, half_width),
            low(patches, width),
        ],
        name="attention_backward",
        flops=2 * patches * (in_proj.size + out_proj.size + 8 * patches * half_width),
    )


def token_grad(where, tokens, grad_mid, own, other, gain, gain_two_grad):
    patches, width = tokens.shape
    half_width = width // 2

    def kernel(
        where_ref, tokens_ref, grad_mid_ref, own_ref, other_ref, gain_ref, two_ref, half_out,
        small_out,
    ):
        grad_normed = own_ref[...].astype(f32) + other_ref[...].astype(f32)
        normal, scale = norm_parts(tokens_ref[...])
        grad_one = jnp.sum(grad_normed * normal, axis=0, keepdims=True)
        grad = grad_mid_ref[...] + norm_grad(
            grad_normed * gain_ref[...].astype(f32), normal, scale
        )
        low = grad.astype(bf16)
        half_out[...] = jnp.where(where_ref[1] == 0, low[:, :half_width], low[:, half_width:])
        small_out[...] = jnp.zeros_like(small_out)
        small_out[:patches, :] = low
        small_out[patches : patches + 1, :] = grad_one.astype(bf16)
        small_out[patches + 1 : patches + 2, :] = two_ref[...].astype(bf16)

    return local_call(
        kernel,
        where,
        [],
        [tokens, grad_mid, own, other, gain, gain_two_grad],
        [
            jax.ShapeDtypeStruct((patches, half_width), bf16),
            jax.ShapeDtypeStruct((EXTRA, width), bf16),
        ],
        name="token_grad",
    )


def wave_grads(wave_column, blocks_ref, rows_ref, wave_count, piece):
    slots = wave_column.shape[0]
    for s in range(slots):
        rows_ref[s * piece : (s + 1) * piece, :] = blocks_ref[s, :piece, :]
    onehot = onehot_of(wave_column, wave_count)
    bits = 2**30 - 1
    shift = piece.bit_length() - 1
    tall = low_dot(
        equal_index(slots * piece, slots, shift, 0, bits, bits).astype(bf16), onehot.astype(bf16)
    ).astype(bf16)
    wide = low_dot(
        tall, equal_index(wave_count, wave_count * piece, 0, shift, bits, bits).astype(bf16)
    )
    same = equal_index(slots * piece, wave_count * piece, 0, 0, piece - 1, piece - 1)
    select = jnp.where(same, wide, 0.0).astype(bf16)
    kernels = contract_first(select, rows_ref[...]).astype(bf16)
    biases = jnp.concatenate(
        [
            blocks_ref[s, piece : piece + 1, :].astype(f32)
            + blocks_ref[s, piece + 1 : piece + 2, :].astype(f32)
            for s in range(slots)
        ],
        axis=0,
    )
    return kernels, exact(onehot.astype(f32), biases, FIRST)


def mix_grad(where, wave_ids, blocks, gen_rows, bias_gen, wave_count, count):
    width, half_width = bias_gen.shape
    piece = gen_rows.shape[0] // width

    def kernel(
        where_ref, ids_ref, blocks_ref, gen_ref, bias_ref, mix_out, kernels_out, biases_out, rows_ref
    ):
        kernels, biases = wave_grads(ids_ref[...], blocks_ref, rows_ref, wave_count, piece)
        kernels_out[...] = kernels
        biases_out[...] = biases
        products = contract_last(kernels, gen_ref[...])
        same = equal_index(*products.shape, 0, 0, piece - 1, piece - 1)
        products = jnp.where(same, products, 0.0)
        rows = jnp.sum(products.reshape(wave_count, piece, -1), axis=1)
        bits = 2**30 - 1
        gather = equal_index(
            width * piece, width, piece.bit_length() - 1, 0, bits, bits
        ).astype(f32)
        mix = exact(rows, gather)
        mix_out[...] = mix + exact(biases, bias_ref[...].astype(f32), LAST) * (1.0 / count)

    return local_call(
        kernel,
        where,
        [],
        [wave_ids, blocks, gen_rows, bias_gen],
        [
            jax.ShapeDtypeStruct((wave_count, width), f32),
            jax.ShapeDtypeStruct((wave_count * piece, half_width), bf16),
            jax.ShapeDtypeStruct((wave_count, half_width), f32),
        ],
        scratch=[pltpu.VMEM((wave_ids.shape[0] * piece, half_width), bf16)],
        name="mix_grad",
        flops=2 * wave_count * piece * gen_rows.size,
    )


def generator_grads(where, mix_low, kernels, biases):
    wave_count, width = mix_low.shape
    piece = kernels.shape[0] // wave_count
    half_width = kernels.shape[1]

    def kernel(where_ref, mix_ref, kernels_ref, biases_ref, gen_out, bias_out):
        mix = mix_ref[...]
        gen_out[...] = contract_first(kron_identity(mix, piece), kernels_ref[...])
        bias_out[...] = exact(mix.astype(f32), biases_ref[...], FIRST)

    return local_call(
        kernel,
        where,
        [],
        [mix_low, kernels, biases],
        [
            jax.ShapeDtypeStruct((width * piece, half_width), f32),
            jax.ShapeDtypeStruct((width, half_width), f32),
        ],
        name="generator_grads",
        flops=2 * wave_count * piece * width * piece * half_width,
    )


def embed_part(upper, orders, where, mask, pixels, kernels):
    images, patches, pixel_count = pixels.shape
    half = images // 2

    def kernel(where_ref, mask_ref, pixel_ref, kernel_ref, *outs):
        band = where_ref[0]

        def body(q):
            for c, order in enumerate(orders):
                image = band ^ relative_index(q + half * upper, order)
                scale = mask_ref[image, band].astype(f32)
                product = jnp.dot(
                    pixel_ref[image], kernel_ref[:, span(c)], preferred_element_type=f32
                )
                outs[c][q] = (product * scale).astype(bf16)

        loop(half, body)

    return local_call(
        kernel,
        where,
        [mask],
        [pixels, kernels],
        [jax.ShapeDtypeStruct((half, patches, LANES), bf16)] * 3,
        name="embed_part",
        flops=images * patches * pixel_count * 3 * LANES,
    )


def kernel_grad(upper, orders, where, mask, pixels, grads, total, bias):
    images, patches, pixel_count = pixels.shape
    half = images // 2
    piece = pixel_count // images
    width = 3 * LANES

    def kernel(where_ref, mask_ref, pixel_ref, *refs):
        band = where_ref[0]
        grad_refs = refs[:3]
        if upper:
            old_total, old_bias, out_ref, total_ref, bias_ref = refs[3:]
            total_ref[...] = old_total[...]
            bias_ref[...] = old_bias[...]
        else:
            total_ref, bias_ref = refs[3:]
            total_ref[...] = jnp.zeros_like(total_ref)
            bias_ref[...] = jnp.zeros_like(bias_ref)

        def body(q):
            for c, order in enumerate(orders):
                image = band ^ relative_index(q + half * upper, order)

                @pl.when(mask_ref[image, band] != 0)
                def _(c=c, image=image):
                    grad = grad_refs[c][q]
                    total_ref[span(c), :] += contract_first(grad, pixel_ref[image])
                    bias_ref[:, span(c)] += jnp.sum(grad.astype(f32), axis=0, keepdims=True)

        loop(half, body)
        if upper:
            high = bias_ref[...].astype(bf16)
            low = (bias_ref[...] - high.astype(f32)).astype(bf16)
            whole = total_ref[...].T.astype(bf16)
            for k in range(images):
                out_ref[k, :piece, :] = whole[k * piece : (k + 1) * piece]
                out_ref[k, piece : piece + 1, :] = high
                out_ref[k, piece + 1 : piece + 2, :] = low

    accumulators = [
        jax.ShapeDtypeStruct((width, pixel_count), f32),
        jax.ShapeDtypeStruct((1, width), f32),
    ]
    flops = images * patches * pixel_count * width
    if not upper:
        return local_call(
            kernel, where, [mask], [pixels, *grads], accumulators, name="kernel_grad", flops=flops
        )
    return local_call(
        kernel,
        where,
        [mask],
        [pixels, *grads, total, bias],
        [jax.ShapeDtypeStruct((images, piece + 2, width), bf16)],
        scratch=[pltpu.VMEM(s.shape, f32) for s in accumulators],
        name="kernel_grad_end",
        flops=flops,
    )[0]


def pixel_grad(orders, where, mask, early, late, kernels):
    half, patches, _ = early[0].shape
    pixel_count = kernels.shape[0]

    def kernel(where_ref, mask_ref, *refs):
        early_refs, late_refs, kernel_ref, outs = refs[:3], refs[3:6], refs[6], refs[7:]
        band, head = where_ref[0], where_ref[1]

        def body(q):
            for side in range(2):
                first = head if side == 0 else 1 - head
                image = first * half + q
                parts = []
                for c, order in enumerate(orders):
                    position = position_of(image ^ band, order)
                    low = jnp.minimum(position, half - 1)
                    high = jnp.maximum(position - half, 0)
                    parts.append(
                        jnp.where(position < half, early_refs[c][low], late_refs[c][high])
                    )
                total = contract_last(jnp.concatenate(parts, axis=1), kernel_ref[...])
                outs[side][q] = (total * mask_ref[image, band].astype(f32)).astype(bf16)

        loop(half, body)

    return local_call(
        kernel,
        where,
        [mask],
        [*early, *late, kernels],
        [jax.ShapeDtypeStruct((half, patches, pixel_count), bf16)] * 2,
        name="pixel_grad",
        flops=4 * half * patches * pixel_count * 3 * LANES,
    )


def row_products(orders, count, where, lefts, rights, portions, name):
    rows = lefts[0].shape[1] // count
    half = count // 2 * rows
    widths = [sum(piece[3] for piece in portion) for portion in portions]
    if rows % 16:
        keeps, sends = [], []
        for portion, order in zip(portions, orders):
            places = jnp.asarray([relative_index(p, order) for p in range(count)], jnp.int32)
            columns = ((where[0] ^ places) * rows)[:, None] + jnp.arange(rows, dtype=jnp.int32)
            select = jnp.arange(count * rows, dtype=jnp.int32)[:, None] == columns.reshape(1, -1)
            turned = [jnp.dot(left, select.astype(bf16)) for left in lefts]
            whole = jnp.concatenate(
                [contract_first(turned[i], rights[j][:, s : s + w]) for i, j, s, w in portion],
                axis=1,
            ).astype(bf16)
            keeps.append(whole[:half])
            sends.append(whole[half:])
        return keeps, sends
    uses = sorted({(piece[0], c) for c, portion in enumerate(portions) for piece in portion})

    def kernel(where_ref, *refs):
        left_refs = refs[: len(lefts)]
        right_refs = refs[len(lefts) : len(lefts) + len(rights)]
        outs = refs[len(lefts) + len(rights) : len(lefts) + len(rights) + 2 * len(portions)]
        turned_refs = refs[-len(uses) - len(lefts) : -len(uses)]
        ordered = dict(zip(uses, refs[-len(uses) :]))
        band = where_ref[0]
        for left_ref, turned_ref in zip(left_refs, turned_refs):
            turned_ref[...] = left_ref[...].T
        for (i, c), ordered_ref in ordered.items():
            for p in range(count):
                block = (band ^ relative_index(p, orders[c])) * rows
                ordered_ref[p * rows : (p + 1) * rows, :] = turned_refs[i][
                    pl.ds(pl.multiple_of(block, 16), rows), :
                ]
        for side in (1, 0):
            for c, portion in enumerate(portions):
                place = 0
                for i, j, start, width in portion:
                    left = ordered[i, c][side * half : (side + 1) * half, :]
                    for column in range(0, width, 256):
                        wide = min(256, width - column)
                        outs[2 * c + side][:, place : place + wide] = jnp.dot(
                            left,
                            right_refs[j][:, start + column : start + column + wide],
                            preferred_element_type=f32,
                        ).astype(bf16)
                        place += wide

    shapes = []
    for width in widths:
        shapes += [jax.ShapeDtypeStruct((half, width), bf16)] * 2
    turned = [pltpu.VMEM((left.shape[1], left.shape[0]), bf16) for left in lefts]
    ordered = [pltpu.VMEM((lefts[i].shape[1], lefts[i].shape[0]), bf16) for i, _ in uses]
    outs = local_call(
        kernel,
        where,
        [],
        [*lefts, *rights],
        shapes,
        scratch=turned + ordered,
        name=name,
        flops=2 * lefts[0].size * sum(widths),
    )
    return outs[0::2], outs[1::2]


def shards(
    pixels,
    band_mask,
    wave_ids,
    pos_embed,
    in_proj,
    out_proj,
    up_proj,
    down_proj,
    gain_one,
    gain_two,
    kernel_gen,
    bias_gen,
    wave_table,
    hyper_in,
    hyper_out,
    hyper_up,
    hyper_down,
    hyper_gain_one,
    hyper_gain_two,
    cotangent,
):
    band_index = lax.axis_index("band")
    head_index = lax.axis_index("head")
    count = lax.axis_size("band")
    images, slot_local, patches, pixel_count = pixels.shape
    model_width = in_proj.shape[1]
    half_width = in_proj.shape[2]
    wave_count, hyper_width = wave_table.shape
    assert images == count and slot_local == 1
    orders = gather_orders(count)
    where = jnp.stack([band_index, head_index]).astype(jnp.int32)
    pixels = pixels.reshape(images, patches, pixel_count)

    gen_rows = kernel_gen.reshape(-1, half_width)
    hyper_weights = [hyper_in, hyper_out, hyper_up, hyper_down]
    hyper_gains = [hyper_gain_one[None], hyper_gain_two[None]]
    slot_piece, image_bias, mix_low, *hyper_kept = hyper_forward(
        where,
        wave_ids,
        band_mask,
        wave_table,
        hyper_weights,
        hyper_gains,
        gen_rows,
        bias_gen,
        count,
    )
    slot_piece = slot_piece.reshape(count, -1, half_width)
    kernels = lax.all_to_all(slot_piece, "band", 0, 0, tiled=True).reshape(pixel_count, half_width)

    sends = embed_part(1, orders, where, band_mask, pixels, kernels)
    arriving = [hop(send, order[-1]) for send, order in zip(sends, orders)]
    keeps = embed_part(0, orders, where, band_mask, pixels, kernels)
    embed_half = jnp.concatenate(
        [part[0] for part in scatter_sum(keeps, None, orders, arriving)], axis=1
    )
    embed_low = (embed_half + image_bias).astype(bf16)
    gain_one = gain_one[None]
    gain_two = gain_two[None]
    tokens, normed_low, query, key, value, probs, attended, attn_part = attention_forward(
        where, embed_low, swap(embed_low), pos_embed, gain_one, in_proj, out_proj
    )
    grad_low = cotangent[0]
    mid_stream, second_low, active_low, grad_hidden, ff_parts = feed_forward(
        where, tokens, attn_part, swap(attn_part), gain_two, up_proj, down_proj, grad_low
    )
    ff_other = swap(ff_parts)

    ff_local = up_proj.shape[1]
    third = ff_local * 2 // 3
    ff_keeps, ff_sends = row_products(
        orders,
        count,
        where,
        [second_low, grad_low],
        [grad_hidden, active_low],
        [
            [(0, 0, 0, third)],
            [(0, 0, third, ff_local - third), (1, 1, 0, 2 * third - ff_local)],
            [(1, 1, 2 * third - ff_local, third)],
        ],
        "ff_grads",
    )
    ff_sends, ff_other = lax.optimization_barrier((ff_sends, ff_other))
    ff_arriving = [hop(send, order[-1]) for send, order in zip(ff_sends, orders)]

    layer_out, gain_two_grad, grad_mid, grad_mid_low, *grad_projected, normed_part = (
        attention_backward(
            where,
            mid_stream,
            ff_parts,
            ff_other,
            grad_low,
            gain_two,
            in_proj,
            out_proj,
            query,
            key,
            value,
            probs,
        )
    )
    grad_embed_half, small = token_grad(
        where, tokens, grad_mid, normed_part, swap(normed_part), gain_one, gain_two_grad
    )

    first = hop(grad_embed_half, orders[0][0])
    early, late = [], []
    for c, order in enumerate(orders):
        block = jnp.stack([grad_embed_half[:, span(c)], first[:, span(c)]])
        for step in order[1:-1]:
            block = jnp.concatenate([block, hop(block, step)], axis=0)
        early.append(block)
        late.append(hop(block, order[-1]))
    total, bias = kernel_grad(0, orders, where, band_mask, pixels, early, None, None)
    blocks = kernel_grad(1, orders, where, band_mask, pixels, late, total, bias)
    own_pixels, other_pixels = pixel_grad(orders, where, band_mask, early, late, kernels)
    grad_pixels = (own_pixels.astype(f32) + swap(other_pixels).astype(f32)).astype(bf16)
    grad_pixels = grad_pixels[:, None]

    blocks = lax.all_to_all(blocks, "band", 0, 0, tiled=True)
    grad_mix, wave_kernels, wave_biases = mix_grad(
        where, wave_ids, blocks, gen_rows, bias_gen, wave_count, count
    )
    grad_kernel_gen, grad_bias_gen = generator_grads(where, mix_low, wave_kernels, wave_biases)
    grad_mix = grad_mix + swap(grad_mix)
    step = 1
    while step < count:
        if step * 4 <= count:
            grad_mix = (grad_mix + hop(grad_mix, step)) + (
                hop(grad_mix, 2 * step) + hop(grad_mix, 3 * step)
            )
            step *= 4
        else:
            grad_mix = grad_mix + hop(grad_mix, step)
            step *= 2
    hyper_grads = hyper_backward(
        where, grad_mix, wave_table, hyper_weights, hyper_gains, hyper_kept
    )

    at_keeps, at_sends = row_products(
        orders,
        count,
        where,
        [normed_low, grad_mid_low, small],
        [*grad_projected, attended, jnp.eye(EXTRA, dtype=bf16)],
        [
            [(0, 0, 0, half_width), (0, 1, 0, 256)],
            [(0, 1, 256, half_width - 256), (0, 2, 0, half_width), (1, 3, 0, 128)],
            [(1, 3, 128, half_width - 128), (2, 4, 0, EXTRA)],
        ],
        "attention_grads",
    )
    ff_keeps, ff_arriving, at_sends, _ = lax.optimization_barrier(
        (ff_keeps, ff_arriving, at_sends, late)
    )
    ff_sums = jnp.concatenate(scatter_sum(ff_keeps, None, orders, ff_arriving), axis=1)
    at_sums = jnp.concatenate(scatter_sum(at_keeps, at_sends, orders), axis=1)
    grad_up, grad_down = ff_sums[:, :ff_local], ff_sums[:, ff_local:]
    grad_in_proj = jnp.stack(
        [at_sums[:, i * half_width : (i + 1) * half_width] for i in range(3)]
    )
    grad_out_proj = at_sums[:, 3 * half_width : 4 * half_width].T
    tail = at_sums[:, 4 * half_width :].T
    return (
        layer_out[None],
        grad_pixels,
        tail[:patches],
        grad_in_proj,
        grad_out_proj,
        grad_up,
        grad_down.T,
        tail[patches],
        tail[patches + 1],
        grad_kernel_gen.reshape(kernel_gen.shape),
        grad_bias_gen,
        *hyper_grads[:5],
        hyper_grads[5][0],
        hyper_grads[6][0],
    )


def solution(mesh):
    in_specs = (
        P(None, "band", None, None),
        P(),
        P(),
        P(),
        P(None, None, "head"),
        P("head", None),
        P(None, "head"),
        P("head", None),
        P(),
        P(),
        P(None, "band", "head"),
        P(None, "head"),
        P(),
        P(),
        P(),
        P(),
        P(),
        P(),
        P(),
        P("band", None, None),
    )
    out_specs = (
        P("band", None, None),
        P("head", "band", None, None),
        P(None, "band"),
        P(None, "band", "head"),
        P("head", "band"),
        P("band", "head"),
        P("head", "band"),
        P("band"),
        P("band"),
        P(None, "band", "head"),
        P(None, "head"),
        P(),
        P(),
        P(),
        P(),
        P(),
        P(),
        P(),
    )
    return jax.shard_map(shards, mesh=mesh, in_specs=in_specs, out_specs=out_specs, check_vma=False)
```

time: 1300 us -> 251 us (0.19)
  waiting for transfers between devices: 1070 us -> 84.7 us
  blocking collectives: 85.1 us -> 0 us
  Pallas kernels: 0 us -> 70.7 us
  matrix products: 68.8 us -> 0 us
  starting transfers between devices: 0.92 us -> 63.3 us
  local copies, waits for them, and re-layouts: 31.9 us -> 15.2 us
  between operations: 16.2 us -> 1.29 us
    reduce_scatter x5 -> x0, waiting for transfers between devices: 560 us -> none  [the longest x1 148 us: shards(): lax.psum_scatter(grad_wave_kernels, 'band', scatter_dimension=1, tiled=True)]
    unnamed x16 -> x0, waiting for transfers between devices: 324 us -> none
    all_gather x2 -> x0, waiting for transfers between devices: 131 us -> none  [the longest x1 66.9 us: shards(): kernel_all = lax.all_gather(kernel_piece, 'band', axis=1, tiled=True)]
    ppermute x0 -> x52, waiting for transfers between devices: none -> 78 us  [the longest x46 74.7 us: hop(): return lax.ppermute(values, 'band', [(i, i ^ step) for i in range(count)])]
    pallas_call x0 -> x15, Pallas kernels: none -> 70.7 us  [local_call(): pl.pallas_call(kernel, in_specs=[smem] * (1 + len(tables)) + [vmem] * len...]
    dot_general x47 -> x0, matrix products: 67.2 us -> none  [the longest x4 8.35 us: contract_first(): lax.dot_general(left, right, (((0,), (0,)), ((), ())), preferred_element_...]
    psum x3 -> x0, waiting for transfers between devices: 53.9 us -> none  [the longest x1 20.2 us: shards(): lax.psum(down_part.astype(jnp.bfloat16), 'head').astype(jnp.float32)]
    ppermute x0 -> x52, starting transfers between devices: none -> 48.7 us  [the longest x46 47.8 us: hop(): return lax.ppermute(values, 'band', [(i, i ^ step) for i in range(count)])]
  transfers between devices with their start and end apart: 13 -> 54, of which waited for: 12 -> 29; matrix products, arithmetic and copies ran while one was open for 5% -> 7% of each run, Pallas kernels for 0% -> 16%
where the time goes in v1:
time: 251 us; the launch traced here: 250 us
  waiting for transfers between devices  84.7 us (34%)
  Pallas kernels  70.7 us (28%)
  starting transfers between devices  63.3 us (25%)
  local copies, waits for them, and re-layouts  15.2 us (6%)
  other arithmetic  14.4 us (6%)
    ppermute x46, waiting for transfers between devices, hop(): return lax.ppermute(values, 'band', [(i, i ^ step) for i in range(count)])  74.7 us
    pallas_call x15, Pallas kernels, local_call(): pl.pallas_call(kernel, in_specs=[smem] * (1 + len(tables)) + [vmem] * len...  70.7 us
    ppermute x46, starting transfers between devices, hop(): return lax.ppermute(values, 'band', [(i, i ^ step) for i in range(count)])  47.8 us
    convert_element_type x27, other arithmetic, scatter_sum(): sends.append((k[half:].astype(f32) + a[half:].astype(f32)).astype(bf16))  9.44 us
    unnamed x63, local copies, waits for them, and re-layouts  8.63 us
    all_to_all x1, starting transfers between devices, shards(): lax.all_to_all(slot_piece, 'band', 0, 0, tiled=True)  8.5 us
    all_to_all x1, waiting for transfers between devices, shards(): lax.all_to_all(slot_piece, 'band', 0, 0, tiled=True)  6.74 us
    all_to_all x1, starting transfers between devices, shards(): blocks = lax.all_to_all(blocks, 'band', 0, 0, tiled=True)  6.08 us
  transfers between devices with their start and end apart: 54, of which 29 were waited for; matrix products, arithmetic and copies ran while one was open for 7% of the time, Pallas kernels for 16%

profile of v1, /device:TPU:0, one launch (start us, length us, event | category | flops | bytes accessed | tf_op | source)
XLA Modules:
  0.0 249.6 jit_solution(3981797437810663162)
XLA Ops:
  2.6 6.6 %hyper_forward.1 = (bf16[256,384]{1,0:T(8,128)(2,1)}, f32[1,384]{1,0:T(1,128)}, bf16[16,128]{1,0:T(8,128)(2,1)}, f32[16,384]{1,0:T(8,128)}, f32[4,16,16]{2,1,0:T...) custom-call(s32[2]{0:T(128)} %pad_add_fusion.where_ref, ...), custom_call_target="tpu_custom_call" | custom-call | flops 1610612736 | bytes 4427456 | tf_op jit(solution)/shard_map/hyper_forward/pallas_call | solution.py:179
  9.2 8.5 %all-to-all-start = ((bf16[16,16,384]{2,1,0:T(8,128)(2,1)}), bf16[16,16,384]{2,1,0:T(8,128)(2,1)S(1)}, u32[]{:S(2)}, u32[]{:S(2)}) async-start(bf16[16,16,384]{2,1,0:T(8,128)(2,1)} %bitcast.60), calls=%async_computation | async-start | bytes 393216 | tf_op jit(solution)/shard_map/all_to_all | solution.py:853
  19.4 6.7 %all-to-all-done = bf16[16,16,384]{2,1,0:T(8,128)(2,1)S(1)} async-done(((bf16[16,16,384]{2,1,0:T(8,128)(2,1)}), bf16[16,16,384]{2,1,0:T(8,128)(2,1)S(1)}, u32[]{:S(2)}, u32[]{:S(2)}) %all-to-all-start) | async-done | bytes 196640 | tf_op jit(solution)/shard_map/all_to_all | solution.py:853
  35.6 4.0 %collective-permute-done.6 = bf16[8,196,128]{2,1,0:T(8,128)(2,1)S(1)} collective-permute-done((bf16[8,196,128]{2,1,0:T(8,128)(2,1)}, bf16[8,196,128]{2,1,0:T(8,128)(2,1)S(1)}, u32[]{:S(2)}, u32[]{:S(2)}) %collective-permute-start.6) | collective-permute-done | bytes 401440 | tf_op jit(solution)/shard_map/ppermute | solution.py:98
  57.2 5.4 %collective-permute-done.9 = bf16[1,196,384]{2,1,0:T(8,128)(2,1)S(1)} collective-permute-done((bf16[1,196,384]{2,1,0:T(8,128)(2,1)S(1)}, bf16[1,196,384]{2,1,0:T(8,128)(2,1)S(1)}, u32[]{:S(2)}, u32[]{:S(2)}) %collective-permute-start.9) | collective-permute-done | bytes 150560 | tf_op jit(solution)/shard_map/ppermute | solution.py:98
  64.8 4.6 %attention_forward.1 = (f32[196,768]{1,0:T(8,128)}, bf16[196,768]{1,0:T(8,128)(2,1)}, bf16[196,384]{1,0:T(8,128)(2,1)}, bf16[196,384]{1,0:T(8,128)(2,1)}, bf16[1...) custom-call(s32[2]{0:T(128)} %pad_add_fusion.where_ref, ...), custom_call_target="tpu_custom_call" | custom-call | flops 580435968 | bytes 5691264 | tf_op jit(solution)/shard_map/attention_forward/pallas_call | solution.py:179
  72.0 6.5 %feed_forward.1 = (f32[196,768]{1,0:T(8,128)}, bf16[196,768]{1,0:T(8,128)(2,1)}, bf16[196,1536]{1,0:T(8,128)(2,1)}, bf16[196,1536]{1,0:T(8,128)(2,1)}, bf16[2,196,768]{2,1,0:T(8,128)(2,1)}) custom-call(s32[2]{0:T(128)} %pad_add_fusion.where_ref, f32[196,768]{1,0:T(8,128)} %get-tuple-element.107.tokens_ref, bf16[196,768]{1,0:T(8,128)(2,1)} %get-tuple-element.108.own_ref, ...), custom_call_target="tpu_custom_call" | custom-call | flops 1849688064 | bytes 8934912 | tf_op jit(solution)/shard_map/feed_forward/pallas_call | solution.py:179
  80.2 4.2 %ff_grads.1 = (bf16[384,1024]{1,0:T(8,128)(2,1)}, bf16[384,1024]{1,0:T(8,128)(2,1)}, bf16[384,1024]{1,0:T(8,128)(2,1)}, bf16[384,1024]{1,0:T(8,128)(2,1)}, bf16[...) custom-call(s32[2]{0:T(128)} %pad_add_fusion.where_ref, bf16[196,768]{1,0:T(8,128)(2,1)} %get-tuple-element.111.refs_0_, ...), custom_call_target="tpu_custom_call" | custom-call | flops 924844032 | bytes 6524928 | tf_op jit(solution)/shard_map/ff_grads/pallas_call | solution.py:179
  85.4 6.8 %attention_backward.1 = (bf16[196,768]{1,0:T(8,128)(2,1)}, f32[1,768]{1,0:T(1,128)}, f32[196,768]{1,0:T(8,128)}, bf16[196,768]{1,0:T(8,128)(2,1)}, bf16[196,384]...) custom-call(s32[2]{0:T(128)} %pad_add_fusion.where_ref, ...), custom_call_target="tpu_custom_call" | custom-call | flops 698449920 | bytes 7801728 | tf_op jit(solution)/shard_map/attention_backward/pallas_call | solution.py:179
  99.2 9.0 %collective-permute-done.14 = bf16[196,384]{1,0:T(8,128)(2,1)S(1)} collective-permute-done((bf16[196,384]{1,0:T(8,128)(2,1)}, bf16[196,384]{1,0:T(8,128)(2,1)S(1)}, u32[]{:S(2)}, u32[]{:S(2)}) %collective-permute-start.14) | collective-permute-done | bytes 150560 | tf_op jit(solution)/shard_map/ppermute | solution.py:98
  109.5 3.5 %collective-permute-done.19 = bf16[2,196,128]{2,1,0:T(8,128)(2,1)S(1)} collective-permute-done((bf16[2,196,128]{2,1,0:T(8,128)(2,1)S(1)}, bf16[2,196,128]{2,1,0:T(8,128)(2,1)S(1)}, u32[]{:S(2)}, u32[]{:S(2)}) %collective-permute-start.19) | collective-permute-done | bytes 100384 | tf_op jit(solution)/shard_map/ppermute | solution.py:98
  124.4 3.5 %collective-permute-done.16 = bf16[4,196,128]{2,1,0:T(8,128)(2,1)S(1)} collective-permute-done((bf16[4,196,128]{2,1,0:T(8,128)(2,1)S(1)}, bf16[4,196,128]{2,1,0:T(8,128)(2,1)S(1)}, u32[]{:S(2)}, u32[]{:S(2)}) %collective-permute-start.16) | collective-permute-done | bytes 200736 | tf_op jit(solution)/shard_map/ppermute | solution.py:98
  128.1 5.0 %collective-permute-done.23.refs_5_.refs_2_ = bf16[8,196,128]{2,1,0:T(8,128)(2,1)S(1)} collective-permute-done((bf16[8,196,128]{2,1,0:T(8,128)(2,1)S(1)}, bf16[8,196,128]{2,1,0:T(8,128)(2,1)S(1)}, u32[]{:S(2)}, u32[]{:S(2)}) %collective-permute-start.23) | collective-permute-done | bytes 401440 | tf_op jit(solution)/shard_map/ppermute | solution.py:98
  134.5 3.6 %attention_grads.1 = (bf16[384,640]{1,0:T(8,128)(2,1)}, bf16[384,640]{1,0:T(8,128)(2,1)}, bf16[384,640]{1,0:T(8,128)(2,1)}, bf16[384,640]{1,0:T(8,128)(2,1)}, bf...) custom-call(s32[2]{0:T(128)} %pad_add_fusion.where_ref, bf16[196,768]{1,0:T(8,128)(2,1)} %get-tuple-element.129.refs_0_, ...), custom_call_target="tpu_custom_call" | custom-call | flops 539492352 | bytes 4481024 | tf_op jit(solution)/shard_map/attention_grads/pallas_call | solution.py:179
  138.2 4.0 %kernel_grad.1 = (f32[384,256]{1,0:T(8,128)}, f32[1,384]{1,0:T(1,128)}) custom-call(s32[2]{0:T(128)} %pad_add_fusion.where_ref, s32[16,16]{1,0:T(8,128)} %mask_ref.11, bf16[16,196,256]{2,1,0:T(8,128)(2,1)} %bitcast.50, bf16[8,196,128]{2,1,0:T(8,128)(2,1)} %copy-done.2, bf16[8,196,128]{2,1,0:T(8,128)(2,1)} %copy-done.1, bf16[8,196,128]{2,1,0:T(8,128)(2,1)} %copy-done), custom_call_target="tpu_custom_call" | custom-call | flops 308281344 | bytes 3204608 | tf_op jit(solution)/shard_map/kernel_grad/pallas_call | solution.py:179
  142.2 7.2 %collective-permute-done.22.refs_4_.refs_1_ = bf16[8,196,128]{2,1,0:T(8,128)(2,1)S(1)} collective-permute-done((bf16[8,196,128]{2,1,0:T(8,128)(2,1)S(1)}, bf16[8,196,128]{2,1,0:T(8,128)(2,1)S(1)}, u32[]{:S(2)}, u32[]{:S(2)}) %collective-permute-start.22) | collective-permute-done | bytes 401440 | tf_op jit(solution)/shard_map/ppermute | solution.py:98
  150.3 5.1 %kernel_grad_end.1 = bf16[16,18,384]{2,1,0:T(8,128)(2,1)} custom-call(s32[2]{0:T(128)} %pad_add_fusion.where_ref, s32[16,16]{1,0:T(8,128)} %mask_ref.11, bf16[16,196,256]{2,1,0:T(8,128)(2,1)} %bitcast.51, bf16[8,196,128]{2,1,0:T(8,128)(2,1)} %copy-done.6, bf16[8,196,128]{2,1,0:T(8,128)(2,1)} %copy-done.5, bf16[8,196,128]{2,1,0:T(8,128)(2,1)} %copy-done.4, ...), custom_call_target="tpu_custom_call" | custom-call | flops 308281344 | bytes 3425792 | tf_op jit(solution)/shard_map/kernel_grad_end/pallas_call | solution.py:179
  155.3 6.1 %all-to-all-start.1 = ((bf16[16,18,384]{2,1,0:T(8,128)(2,1)}), bf16[16,18,384]{2,1,0:T(8,128)(2,1)S(1)}, u32[]{:S(2)}, u32[]{:S(2)}) async-start(bf16[16,18,384]{2,1,0:T(8,128)(2,1)} %kernel_grad_end.1), calls=%async_computation.1 | async-start | bytes 589824 | tf_op jit(solution)/shard_map/all_to_all | solution.py:925
  161.4 4.3 %pixel_grad.1 = (bf16[8,196,256]{2,1,0:T(8,128)(2,1)}, bf16[8,196,256]{2,1,0:T(8,128)(2,1)}) custom-call(s32[2]{0:T(128)} %pad_add_fusion.where_ref, s32[16,16]{1,0:T(8,128)} %mask_ref.11, bf16[8,196,128]{2,1,0:T(8,128)(2,1)} %copy-done.2, bf16[8,196,128]{2,1,0:T(8,128)(2,1)} %copy-done.1, bf16[8,196,128]{2,1,0:T(8,128)(2,1)} %copy-done, ...), custom_call_target="tpu_custom_call" | custom-call | flops 616562688 | bytes 4210688 | tf_op jit(solution)/shard_map/pixel_grad/pallas_call | solution.py:179
  175.2 7.5 %collective-permute-done.38 = bf16[192,1024]{1,0:T(8,128)(2,1)S(1)} collective-permute-done((bf16[192,1024]{1,0:T(8,128)(2,1)S(1)}, bf16[192,1024]{1,0:T(8,128)(2,1)S(1)}, u32[]{:S(2)}, u32[]{:S(2)}) %collective-permute-start.38) | collective-permute-done | bytes 393248 | tf_op jit(solution)/shard_map/ppermute | solution.py:98
  188.9 4.1 %mix_grad.1 = (f32[16,128]{1,0:T(8,128)}, bf16[256,384]{1,0:T(8,128)(2,1)}, f32[16,384]{1,0:T(8,128)}) custom-call(s32[2]{0:T(128)} %pad_add_fusion.where_ref, s32[16,1]{1,0:T(8,128)} %copy.47.ids_ref, bf16[16,18,384]{2,1,0:T(8,128)(2,1)} %copy-done.8, bf16[2048,384]{1,0:T(8,128)(2,1)} %bitcast.56, bf16[128,384]{1,0:T(8,128)(2,1)} %bias_ref.3), custom_call_target="tpu_custom_call" | custom-call | flops 402653184 | bytes 2121792 | tf_op jit(solution)/shard_map/mix_grad/pallas_call | solution.py:179
  205.6 3.8 %generator_grads.1 = (f32[2048,384]{1,0:T(8,128)}, f32[128,384]{1,0:T(8,128)}) custom-call(s32[2]{0:T(128)} %pad_add_fusion.where_ref, bf16[16,128]{1,0:T(8,128)(2,1)} %get-tuple-element.157.mix_ref, bf16[256,384]{1,0:T(8,128)(2,1)} %get-tuple-element.160.kernels_ref, f32[16,384]{1,0:T(8,128)} %get-tuple-element.161.biases_ref), custom_call_target="tpu_custom_call" | custom-call | flops 402653184 | bytes 3567616 | tf_op jit(solution)/shard_map/generator_grads/pallas_call | solution.py:179
  213.0 7.8 %hyper_backward.1 = (f32[16,128]{1,0:T(8,128)}, f32[128,384]{1,0:T(8,128)}, f32[128,128]{1,0:T(8,128)}, f32[128,2048]{1,0:T(8,128)}, f32[2048,128]{1,0:T(8,128)}, /*index=5*/f32[1,128]{1,0:T(1,128)}, f32[1,128]{1,0:T(1,128)}) custom-call(s32[2]{0:T(128)} %pad_add_fusion.where_ref, f32[16,128]{1,0:T(8,128)} %add_add_fusion.grad_ref, f32[16,128]{1,0:T(8,128)} %table_ref.3, ...), custom_call_target="tpu_custom_call" | custom-call | flops 335544320 | bytes 4929664 | tf_op jit(solution)/shard_map/hyper_backward/pallas_call | solution.py:179
  227.7 3.3 %collective-permute-done.43 = bf16[96,1024]{1,0:T(8,128)(2,1)S(1)} collective-permute-done((bf16[96,1024]{1,0:T(8,128)(2,1)S(1)}, bf16[96,1024]{1,0:T(8,128)(2,1)S(1)}, u32[]{:S(2)}, u32[]{:S(2)}) %collective-permute-start.43) | collective-permute-done | bytes 196640 | tf_op jit(solution)/shard_map/ppermute | solution.py:98
  (225 shorter events, 117.2 us)
Async XLA Ops:
  9.2 17.0 %all-to-all-start = ((bf16[16,16,384]{2,1,0:T(8,128)(2,1)}), bf16[16,16,384]{2,1,0:T(8,128)(2,1)S(1)}, u32[]{:S(2)}, u32[]{:S(2)}) async-start(bf16[16,16,384]{2,1,0:T(8,128)(2,1)} %bitcast.60), calls=%async_computation | async-start | bytes 393216 | tf_op jit(solution)/shard_map/all_to_all | solution.py:853
  31.1 11.3 %collective-permute-start.3 = (bf16[8,196,128]{2,1,0:T(8,128)(2,1)}, bf16[8,196,128]{2,1,0:T(8,128)(2,1)S(1)}, u32[]{:S(2)}, u32[]{:S(2)}) collective-permute-start(bf16[8,196,128]{2,1,0:T(8,128)(2,1)} %get-tuple-element.103), channel_id=1, source_target_pairs={{0,4},{2,6},{4,0},{6,2},{8,12},{10,14},{12,8},{14,10},{16,20},{18,... | collective-permute-start | bytes 1204232 | tf_op jit(solution)/shard_map/ppermute | solution.py:98
  31.8 11.1 %collective-permute-start = (bf16[8,196,128]{2,1,0:T(8,128)(2,1)}, bf16[8,196,128]{2,1,0:T(8,128)(2,1)S(1)}, u32[]{:S(2)}, u32[]{:S(2)}) collective-permute-start(bf16[8,196,128]{2,1,0:T(8,128)(2,1)} %get-tuple-element.101), channel_id=1, source_target_pairs={{0,2},{2,0},{4,6},{6,4},{8,10},{10,8},{12,14},{14,12},{16,18},{18,... | collective-permute-start | bytes 1204232 | tf_op jit(solution)/shard_map/ppermute | solution.py:98
  97.5 10.7 %collective-permute-start.14 = (bf16[196,384]{1,0:T(8,128)(2,1)}, bf16[196,384]{1,0:T(8,128)(2,1)S(1)}, u32[]{:S(2)}, u32[]{:S(2)}) collective-permute-start(bf16[196,384]{1,0:T(8,128)(2,1)} %get-tuple-element.126), channel_id=1, source_target_pairs={{0,16},{2,18},{4,20},{6,22},{8,24},{10,26},{12,28},{14,30},{16,0},... | collective-permute-start | bytes 451592 | tf_op jit(solution)/shard_map/ppermute | solution.py:98
  114.3 10.0 %collective-permute-start.18 = (bf16[4,196,128]{2,1,0:T(8,128)(2,1)S(1)}, bf16[4,196,128]{2,1,0:T(8,128)(2,1)S(1)}, u32[]{:S(2)}, u32[]{:S(2)}) collective-permute-start(bf16[4,196,128]{2,1,0:T(8,128)(2,1)S(1)} %pad_maximum_fusion.8), channel_id=1, source_target_pairs={{0,8},{2,10},{4,12},{6,14},{8,0},{10,2},{12,4},{14,6},{16,24},{18,... | collective-permute-start | bytes 602120 | tf_op jit(solution)/shard_map/ppermute | solution.py:98
  118.9 14.2 %collective-permute-start.23 = (bf16[8,196,128]{2,1,0:T(8,128)(2,1)S(1)}, bf16[8,196,128]{2,1,0:T(8,128)(2,1)S(1)}, u32[]{:S(2)}, u32[]{:S(2)}) collective-permute-start(bf16[8,196,128]{2,1,0:T(8,128)(2,1)S(1)} %pad_maximum_fusion.2.refs_2_), channel_id=1, source_target_pairs={{0,8},{2,10},{4,12},{6,14},{8,0},{10,2},{12,4},{14,6},{16,24},{18,... | collective-permute-start | bytes 1204232 | tf_op jit(solution)/shard_map/ppermute | solution.py:98
  120.0 47.1 %collective-permute-start.25 = (bf16[384,1024]{1,0:T(8,128)(2,1)}, bf16[384,1024]{1,0:T(8,128)(2,1)}, u32[]{:S(2)}, u32[]{:S(2)}) collective-permute-start(bf16[384,1024]{1,0:T(8,128)(2,1)} %get-tuple-element.140), channel_id=1, source_target_pairs={{0,2},{2,0},{4,6},{6,4},{8,10},{10,8},{12,14},{14,12},{16,18},{18,... | collective-permute-start | bytes 2359304 | tf_op jit(solution)/shard_map/ppermute | solution.py:98
  121.2 45.9 %collective-permute-start.26 = (bf16[384,1024]{1,0:T(8,128)(2,1)}, bf16[384,1024]{1,0:T(8,128)(2,1)S(1)}, u32[]{:S(2)}, u32[]{:S(2)}) collective-permute-start(bf16[384,1024]{1,0:T(8,128)(2,1)} %get-tuple-element.141), channel_id=1, source_target_pairs={{0,4},{2,6},{4,0},{6,2},{8,12},{10,14},{12,8},{14,10},{16,20},{18,... | collective-permute-start | bytes 2359304 | tf_op jit(solution)/shard_map/ppermute | solution.py:98
  124.3 42.9 %collective-permute-start.27 = (bf16[384,1024]{1,0:T(8,128)(2,1)}, bf16[384,1024]{1,0:T(8,128)(2,1)S(1)}, u32[]{:S(2)}, u32[]{:S(2)}) collective-permute-start(bf16[384,1024]{1,0:T(8,128)(2,1)} %get-tuple-element.142), channel_id=1, source_target_pairs={{0,8},{2,10},{4,12},{6,14},{8,0},{10,2},{12,4},{14,6},{16,24},{18,... | collective-permute-start | bytes 2359304 | tf_op jit(solution)/shard_map/ppermute | solution.py:98
  128.0 21.4 %collective-permute-start.22 = (bf16[8,196,128]{2,1,0:T(8,128)(2,1)S(1)}, bf16[8,196,128]{2,1,0:T(8,128)(2,1)S(1)}, u32[]{:S(2)}, u32[]{:S(2)}) collective-permute-start(bf16[8,196,128]{2,1,0:T(8,128)(2,1)S(1)} %pad_maximum_fusion.1.refs_1_), channel_id=1, source_target_pairs={{0,4},{2,6},{4,0},{6,2},{8,12},{10,14},{12,8},{14,10},{16,20},{18,... | collective-permute-start | bytes 1204232 | tf_op jit(solution)/shard_map/ppermute | solution.py:98
  133.1 16.3 %collective-permute-start.21 = (bf16[8,196,128]{2,1,0:T(8,128)(2,1)S(1)}, bf16[8,196,128]{2,1,0:T(8,128)(2,1)S(1)}, u32[]{:S(2)}, u32[]{:S(2)}) collective-permute-start(bf16[8,196,128]{2,1,0:T(8,128)(2,1)S(1)} %pad_maximum_fusion.refs_0_), channel_id=1, source_target_pairs={{0,2},{2,0},{4,6},{6,4},{8,10},{10,8},{12,14},{14,12},{16,18},{18,... | collective-permute-start | bytes 1204232 | tf_op jit(solution)/shard_map/ppermute | solution.py:98
  155.3 32.8 %all-to-all-start.1 = ((bf16[16,18,384]{2,1,0:T(8,128)(2,1)}), bf16[16,18,384]{2,1,0:T(8,128)(2,1)S(1)}, u32[]{:S(2)}, u32[]{:S(2)}) async-start(bf16[16,18,384]{2,1,0:T(8,128)(2,1)} %kernel_grad_end.1), calls=%async_computation.1 | async-start | bytes 589824 | tf_op jit(solution)/shard_map/all_to_all | solution.py:925
  167.0 69.6 %collective-permute-start.24 = (bf16[8,196,256]{2,0,1:T(8,128)(2,1)S(1)}, bf16[8,196,256]{2,0,1:T(8,128)(2,1)S(1)}, u32[]{:S(2)}, u32[]{:S(2)}) collective-permute-start(bf16[8,196,256]{2,0,1:T(8,128)(2,1)S(1)} %copy.50), channel_id=1, source_target_pairs={{0,1},{1,0},{2,3},{3,2},{4,5},{5,4},{6,7},{7,6},{8,9},{9,8},{10,11... | collective-permute-start | bytes 2408456 | tf_op jit(solution)/shard_map/ppermute | solution.py:102
  167.2 30.4 %collective-permute-start.28 = (bf16[384,512]{1,0:T(8,128)(2,1)}, bf16[384,512]{1,0:T(8,128)(2,1)}, u32[]{:S(2)}, u32[]{:S(2)}) collective-permute-start(bf16[384,512]{1,0:T(8,128)(2,1)} %get-tuple-element.146), channel_id=1, source_target_pairs={{0,8},{2,10},{4,12},{6,14},{8,0},{10,2},{12,4},{14,6},{16,24},{18,... | collective-permute-start | bytes 1179656 | tf_op jit(solution)/shard_map/ppermute | solution.py:98
  169.0 51.8 %collective-permute-start.31 = (bf16[384,640]{1,0:T(8,128)(2,1)}, bf16[384,640]{1,0:T(8,128)(2,1)}, u32[]{:S(2)}, u32[]{:S(2)}) collective-permute-start(bf16[384,640]{1,0:T(8,128)(2,1)} %get-tuple-element.148), channel_id=1, source_target_pairs={{0,2},{2,0},{4,6},{6,4},{8,10},{10,8},{12,14},{14,12},{16,18},{18,... | collective-permute-start | bytes 1474568 | tf_op jit(solution)/shard_map/ppermute | solution.py:98
  171.8 11.0 %collective-permute-start.38 = (bf16[192,1024]{1,0:T(8,128)(2,1)S(1)}, bf16[192,1024]{1,0:T(8,128)(2,1)S(1)}, u32[]{:S(2)}, u32[]{:S(2)}) collective-permute-start(bf16[192,1024]{1,0:T(8,128)(2,1)S(1)} %get-tuple-element.236), channel_id=1, source_target_pairs={{0,4},{2,6},{4,0},{6,2},{8,12},{10,14},{12,8},{14,10},{16,20},{18,... | collective-permute-start | bytes 1179656 | tf_op jit(solution)/shard_map/ppermute | solution.py:98
  173.6 13.8 %collective-permute-start.40 = (bf16[192,1024]{1,0:T(8,128)(2,1)S(1)}, bf16[192,1024]{1,0:T(8,128)(2,1)S(1)}, u32[]{:S(2)}, u32[]{:S(2)}) collective-permute-start(bf16[192,1024]{1,0:T(8,128)(2,1)S(1)} %get-tuple-element.240), channel_id=1, source_target_pairs={{0,8},{2,10},{4,12},{6,14},{8,0},{10,2},{12,4},{14,6},{16,24},{18,... | collective-permute-start | bytes 1179656 | tf_op jit(solution)/shard_map/ppermute | solution.py:98
  182.8 10.5 %collective-permute-start.42 = (bf16[192,1024]{1,0:T(8,128)(2,1)}, bf16[192,1024]{1,0:T(8,128)(2,1)}, u32[]{:S(2)}, u32[]{:S(2)}) collective-permute-start(bf16[192,1024]{1,0:T(8,128)(2,1)} %get-tuple-element.238), channel_id=1, source_target_pairs={{0,2},{2,0},{4,6},{6,4},{8,10},{10,8},{12,14},{14,12},{16,18},{18,... | collective-permute-start | bytes 1179656 | tf_op jit(solution)/shard_map/ppermute | solution.py:98
  209.4 14.1 %collective-permute-start.34 = (bf16[384,640]{1,0:T(8,128)(2,1)S(1)}, bf16[384,640]{1,0:T(8,128)(2,1)S(1)}, u32[]{:S(2)}, u32[]{:S(2)}) collective-permute-start(bf16[384,640]{1,0:T(8,128)(2,1)S(1)} %copy-done.28), channel_id=1, source_target_pairs={{0,4},{2,6},{4,0},{6,2},{8,12},{10,14},{12,8},{14,10},{16,20},{18,... | collective-permute-start | bytes 1474568 | tf_op jit(solution)/shard_map/ppermute | solution.py:98
  210.9 13.3 %collective-permute-start.29 = (bf16[192,512]{1,0:T(8,128)(2,1)S(1)}, bf16[192,512]{1,0:T(8,128)(2,1)S(1)}, u32[]{:S(2)}, u32[]{:S(2)}) collective-permute-start(bf16[192,512]{1,0:T(8,128)(2,1)S(1)} %get-tuple-element.258), channel_id=1, source_target_pairs={{0,2},{2,0},{4,6},{6,4},{8,10},{10,8},{12,14},{14,12},{16,18},{18,... | collective-permute-start | bytes 589832 | tf_op jit(solution)/shard_map/ppermute | solution.py:98
  211.5 14.3 %collective-permute-start.39 = (bf16[96,1024]{1,0:T(8,128)(2,1)S(1)}, bf16[96,1024]{1,0:T(8,128)(2,1)S(1)}, u32[]{:S(2)}, u32[]{:S(2)}) collective-permute-start(bf16[96,1024]{1,0:T(8,128)(2,1)S(1)} %copy-done.20), channel_id=1, source_target_pairs={{0,8},{2,10},{4,12},{6,14},{8,0},{10,2},{12,4},{14,6},{16,24},{18,... | collective-permute-start | bytes 589832 | tf_op jit(solution)/shard_map/ppermute | solution.py:98
  224.2 10.5 %collective-permute-start.32 = (bf16[192,640]{1,0:T(8,128)(2,1)S(1)}, bf16[192,640]{1,0:T(8,128)(2,1)S(1)}, u32[]{:S(2)}, u32[]{:S(2)}) collective-permute-start(bf16[192,640]{1,0:T(8,128)(2,1)S(1)} %get-tuple-element.248), channel_id=1, source_target_pairs={{0,4},{2,6},{4,0},{6,2},{8,12},{10,14},{12,8},{14,10},{16,20},{18,... | collective-permute-start | bytes 737288 | tf_op jit(solution)/shard_map/ppermute | solution.py:98
  225.8 9.8 %collective-permute-start.35 = (bf16[192,640]{1,0:T(8,128)(2,1)S(1)}, bf16[192,640]{1,0:T(8,128)(2,1)S(1)}, u32[]{:S(2)}, u32[]{:S(2)}) collective-permute-start(bf16[192,640]{1,0:T(8,128)(2,1)S(1)} %get-tuple-element.250), channel_id=1, source_target_pairs={{0,8},{2,10},{4,12},{6,14},{8,0},{10,2},{12,4},{14,6},{16,24},{18,... | collective-permute-start | bytes 737288 | tf_op jit(solution)/shard_map/ppermute | solution.py:98
  231.1 13.3 %collective-permute-start.44 = (bf16[48,3072]{1,0:T(8,128)(2,1)S(1)}, bf16[48,3072]{1,0:T(8,128)(2,1)S(1)}, u32[]{:S(2)}, u32[]{:S(2)}) collective-permute-start(bf16[48,3072]{1,0:T(8,128)(2,1)S(1)} %pad_maximum_fusion.5), channel_id=1, source_target_pairs={{0,16},{2,18},{4,20},{6,22},{8,24},{10,26},{12,28},{14,30},{16,0},... | collective-permute-start | bytes 884744 | tf_op jit(solution)/shard_map/ppermute | solution.py:98
  (60 other events, 387.2 us)

commit v2 on v1

--- a/solution.py
+++ b/solution.py
@@ -10,6 +10,7 @@
 HHEADS = 4
 LANES = 128
 EXTRA = 256
+PART = 208
 
 highest = lax.Precision.HIGHEST
 norm_epsilon = 1e-06
@@ -171,7 +172,9 @@
     return slice(c * LANES, (c + 1) * LANES)
 
 
-def local_call(kernel, where, tables, args, out_shape, scratch=(), name=None, flops=0):
+def local_call(
+    kernel, where, tables, args, out_shape, scratch=(), name=None, flops=0, mebibytes=24
+):
     vmem = pl.BlockSpec(memory_space=pltpu.VMEM)
     smem = pl.BlockSpec(memory_space=pltpu.SMEM)
     moved = sum(x.size * x.dtype.itemsize for x in args)
@@ -183,7 +186,7 @@
         out_shape=list(out_shape),
         scratch_shapes=list(scratch),
         cost_estimate=pl.CostEstimate(flops=flops, bytes_accessed=moved, transcendentals=0),
-        compiler_params=pltpu.CompilerParams(vmem_limit_bytes=56 * 2**20),
+        compiler_params=pltpu.CompilerParams(vmem_limit_bytes=mebibytes * 2**20),
         name=name,
     )(where, *tables, *args)
 
@@ -256,6 +259,7 @@
             shape(wave_count, 1),
         ],
         name="hyper_forward",
+        mebibytes=56,
         flops=8 * slots * piece * gen_rows.size,
     )
 
@@ -270,7 +274,7 @@
         normal_two_ref, scale_two_ref, table_out, in_out, out_out, up_out, down_out, one_out,
         two_out,
     ):
-        grad = grad_ref[...]
+        grad = jnp.sum(grad_ref[...], axis=0)
         normal_two = normal_two_ref[...]
         two_out[...] = jnp.sum(grad * normal_two, axis=0, keepdims=True)
         grad_two = norm_grad(grad * two_ref[...], normal_two, scale_two_ref[...])
@@ -395,8 +399,10 @@
             active_out[:, columns] = (hidden * factor).astype(bf16)
             grad_active = contract_last(cotangent_ref[...], down_ref[columns, :])
             grad_hidden_out[:, columns] = (grad_active * slope).astype(bf16)
-        parts_out[0] = low_dot(active_out[...], down_ref[...]).astype(bf16)
-        parts_out[1] = contract_last(grad_hidden_out[...], up_ref[...]).astype(bf16)
+        parts_out[:patches, :] = low_dot(active_out[...], down_ref[...]).astype(bf16)
+        parts_out[PART : PART + patches, :] = contract_last(
+            grad_hidden_out[...], up_ref[...]
+        ).astype(bf16)
 
     return local_call(
         kernel,
@@ -408,7 +414,7 @@
             jax.ShapeDtypeStruct((patches, width), bf16),
             jax.ShapeDtypeStruct((patches, local), bf16),
             jax.ShapeDtypeStruct((patches, local), bf16),
-            jax.ShapeDtypeStruct((2, patches, width), bf16),
+            jax.ShapeDtypeStruct((PART + patches, width), bf16),
         ],
         name="feed_forward",
         flops=8 * patches * up.size,
@@ -428,9 +434,10 @@
         query_out, key_out, value_out, part_out,
     ):
         mid_values = mid_ref[...]
-        down = own_ref[0].astype(f32) + other_ref[0].astype(f32)
+        down = own_ref[:patches, :].astype(f32) + other_ref[:patches, :].astype(f32)
         layer_out[...] = (mid_values + down).astype(bf16)
-        grad_second = own_ref[1].astype(f32) + other_ref[1].astype(f32)
+        back = slice(PART, PART + patches)
+        grad_second = own_ref[back, :].astype(f32) + other_ref[back, :].astype(f32)
         normal, scale = norm_parts(mid_values)
         gain_out[...] = jnp.sum(grad_second * normal, axis=0, keepdims=True)
         grad_mid = cotangent_ref[...].astype(f32) + norm_grad(
@@ -734,7 +741,7 @@
     )
 
 
-def row_products(orders, count, where, lefts, rights, portions, name):
+def row_products(orders, count, where, lefts, rights, portions, name, sides=(1, 0)):
     rows = lefts[0].shape[1] // count
     half = count // 2 * rows
     widths = [sum(piece[3] for piece in portion) for portion in portions]
@@ -751,13 +758,13 @@
             ).astype(bf16)
             keeps.append(whole[:half])
             sends.append(whole[half:])
-        return keeps, sends
+        return [keeps, sends]
     uses = sorted({(piece[0], c) for c, portion in enumerate(portions) for piece in portion})
 
     def kernel(where_ref, *refs):
         left_refs = refs[: len(lefts)]
         right_refs = refs[len(lefts) : len(lefts) + len(rights)]
-        outs = refs[len(lefts) + len(rights) : len(lefts) + len(rights) + 2 * len(portions)]
+        outs = refs[len(lefts) + len(rights) :]
         turned_refs = refs[-len(uses) - len(lefts) : -len(uses)]
         ordered = dict(zip(uses, refs[-len(uses) :]))
         band = where_ref[0]
@@ -765,27 +772,27 @@
             turned_ref[...] = left_ref[...].T
         for (i, c), ordered_ref in ordered.items():
             for p in range(count):
+                if p // (count // 2) not in sides:
+                    continue
                 block = (band ^ relative_index(p, orders[c])) * rows
                 ordered_ref[p * rows : (p + 1) * rows, :] = turned_refs[i][
                     pl.ds(pl.multiple_of(block, 16), rows), :
                 ]
-        for side in (1, 0):
+        for side in sides:
             for c, portion in enumerate(portions):
                 place = 0
                 for i, j, start, width in portion:
                     left = ordered[i, c][side * half : (side + 1) * half, :]
                     for column in range(0, width, 256):
                         wide = min(256, width - column)
-                        outs[2 * c + side][:, place : place + wide] = jnp.dot(
+                        outs[sides.index(side) * len(portions) + c][:, place : place + wide] = jnp.dot(
                             left,
                             right_refs[j][:, start + column : start + column + wide],
                             preferred_element_type=f32,
                         ).astype(bf16)
                         place += wide
 
-    shapes = []
-    for width in widths:
-        shapes += [jax.ShapeDtypeStruct((half, width), bf16)] * 2
+    shapes = [jax.ShapeDtypeStruct((half, width), bf16) for width in widths] * len(sides)
     turned = [pltpu.VMEM((left.shape[1], left.shape[0]), bf16) for left in lefts]
     ordered = [pltpu.VMEM((lefts[i].shape[1], lefts[i].shape[0]), bf16) for i, _ in uses]
     outs = local_call(
@@ -796,9 +803,172 @@
         shapes,
         scratch=turned + ordered,
         name=name,
+        flops=len(sides) * lefts[0].size * sum(widths),
+    )
+    return [outs[i * len(portions) : (i + 1) * len(portions)] for i in range(len(sides))]
+
+
+def merged_products(orders, where, lefts, rights, portions, ff_keeps, ff_arriving):
+    count = 16
+    rows = lefts[0].shape[1] // count
+    quarter = 4 * rows
+    widths = [sum(piece[3] for piece in portion) for portion in portions]
+    ff_widths = [keep.shape[1] for keep in ff_keeps]
+    turns = [orders[(c + 1) % 3] for c in range(3)]
+    uses = sorted({(piece[0], c) for c, portion in enumerate(portions) for piece in portion})
+    inputs = len(lefts) + len(rights)
+
+    def kernel(where_ref, *refs):
+        left_refs, right_refs = refs[: len(lefts)], refs[len(lefts) : inputs]
+        keep_refs, arriving_refs = refs[inputs : inputs + 3], refs[inputs + 3 : inputs + 6]
+        sends, keeps = refs[inputs + 6 : inputs + 9], refs[inputs + 9 : inputs + 12]
+        turned_refs = refs[inputs + 12 : inputs + 12 + len(lefts)]
+        ordered = dict(zip(uses, refs[inputs + 12 + len(lefts) :]))
+        band = where_ref[0]
+        for c in range(3):
+            total = keep_refs[c][...].astype(f32) + arriving_refs[c][...].astype(f32)
+            keeps[c][:, : ff_widths[c]] = total[:quarter].astype(bf16)
+            sends[c][:, : ff_widths[c]] = total[quarter:].astype(bf16)
+        for left_ref, turned_ref in zip(left_refs, turned_refs):
+            turned_ref[...] = left_ref[...].T
+        for (i, c), ordered_ref in ordered.items():
+            for p in range(count):
+                block = (band ^ relative_index(p, turns[c])) * rows
+                ordered_ref[p * rows : (p + 1) * rows, :] = turned_refs[i][
+                    pl.ds(pl.multiple_of(block, 16), rows), :
+                ]
+        for c, portion in enumerate(portions):
+            place = 0
+            for i, j, start, width in portion:
+                for column in range(0, width, 256):
+                    wide = min(256, width - column)
+                    product = jnp.dot(
+                        ordered[i, c][...],
+                        right_refs[j][:, start + column : start + column + wide],
+                        preferred_element_type=f32,
+                    ).astype(bf16)
+                    for k in range(4):
+                        out = keeps[c] if k < 2 else sends[c]
+                        at = ff_widths[c] + (k % 2) * widths[c] + place
+                        out[:, at : at + wide] = product[k * quarter : (k + 1) * quarter]
+                    place += wide
+
+    shapes = [
+        jax.ShapeDtypeStruct((quarter, f + 2 * w), bf16) for f, w in zip(ff_widths, widths)
+    ] * 2
+    outs = local_call(
+        kernel,
+        where,
+        [],
+        [*lefts, *rights, *ff_keeps, *ff_arriving],
+        shapes,
+        scratch=[pltpu.VMEM((left.shape[1], left.shape[0]), bf16) for left in lefts]
+        + [pltpu.VMEM((lefts[i].shape[1], lefts[i].shape[0]), bf16) for i, _ in uses],
+        name="attention_grads",
         flops=2 * lefts[0].size * sum(widths),
     )
-    return outs[0::2], outs[1::2]
+    return outs[:3], outs[3:]
+
+
+def second_sum(where, keeps, arriving, ff_widths, widths):
+    quarter = keeps[0].shape[0]
+    pair = quarter // 2
+
+    def kernel(where_ref, *refs):
+        keep_refs, arriving_refs, sends, kept = refs[:3], refs[3:6], refs[6:9], refs[9:12]
+        for c in range(3):
+            total = keep_refs[c][...].astype(f32) + arriving_refs[c][...].astype(f32)
+            f, w = ff_widths[c], widths[c]
+            kept[c][:, :f] = total[:pair, :f]
+            sends[c][:, :f] = total[pair:, :f].astype(bf16)
+            for k in range(2):
+                rows = slice(k * pair, (k + 1) * pair)
+                at = slice(f + k * w, f + (k + 1) * w)
+                kept[c][:, at] = total[rows, f : f + w]
+                sends[c][:, at] = total[rows, f + w : f + 2 * w].astype(bf16)
+
+    shapes = [(pair, f + 2 * w) for f, w in zip(ff_widths, widths)]
+    outs = local_call(
+        kernel,
+        where,
+        [],
+        [*keeps, *arriving],
+        [jax.ShapeDtypeStruct(s, bf16) for s in shapes]
+        + [jax.ShapeDtypeStruct(s, f32) for s in shapes],
+        name="second_sum",
+    )
+    return outs[:3], outs[3:]
+
+
+def third_sum(where, keeps, arriving, ff_widths, widths):
+    pair = keeps[0].shape[0]
+    rows = pair // 2
+    ff_total = sum(ff_widths)
+
+    def kernel(where_ref, *refs):
+        keep_refs, arriving_refs = refs[:3], refs[3:6]
+        ff_send, ff_kept, sends, kept = refs[6], refs[7], refs[8:11], refs[11:14]
+        place = 0
+        for c in range(3):
+            total = keep_refs[c][...] + arriving_refs[c][...].astype(f32)
+            f, w = ff_widths[c], widths[c]
+            ff_kept[:, place : place + f] = total[:rows, :f]
+            ff_send[:, place : place + f] = total[rows:, :f].astype(bf16)
+            kept[c][...] = total[:, f : f + w]
+            sends[c][...] = total[:, f + w :].astype(bf16)
+            place += f
+
+    outs = local_call(
+        kernel,
+        where,
+        [],
+        [*keeps, *arriving],
+        [jax.ShapeDtypeStruct((rows, ff_total), bf16), jax.ShapeDtypeStruct((rows, ff_total), f32)]
+        + [jax.ShapeDtypeStruct((pair, w), bf16) for w in widths]
+        + [jax.ShapeDtypeStruct((pair, w), f32) for w in widths],
+        name="third_sum",
+    )
+    return outs[0], outs[1], outs[2:5], outs[5:]
+
+
+def fourth_sum(where, ff_kept, ff_arriving, keeps, arriving, large):
+    rows = ff_kept.shape[0]
+    widths = [keep.shape[1] for keep in keeps]
+    half = ff_kept.shape[1] // 2
+    rest = half - large
+
+    def kernel(where_ref, *refs):
+        ff_ref, ff_arriving_ref, keep_refs, arriving_refs = refs[0], refs[1], refs[2:5], refs[5:8]
+        up_out, down_out, send, kept = refs[8:12]
+        for k, out in enumerate((up_out, down_out)):
+            for source, place, wide in ((k * large, 0, large), (2 * large + k * rest, large, rest)):
+                at = slice(source, source + wide)
+                out[:, place : place + wide] = ff_ref[:, at] + ff_arriving_ref[:, at].astype(f32)
+        place = 0
+        for c in range(3):
+            total = keep_refs[c][...] + arriving_refs[c][...].astype(f32)
+            at = slice(place, place + widths[c])
+            kept[:, at] = total[:rows]
+            send[:, at] = total[rows:].astype(bf16)
+            place += widths[c]
+
+    return local_call(
+        kernel,
+        where,
+        [],
+        [ff_kept, ff_arriving, *keeps, *arriving],
+        [
+            jax.ShapeDtypeStruct((rows, half), f32),
+            jax.ShapeDtypeStruct((rows, half), f32),
+            jax.ShapeDtypeStruct((rows, sum(widths)), bf16),
+            jax.ShapeDtypeStruct((rows, sum(widths)), f32),
+        ],
+        name="fourth_sum",
+    )
+
+
+def after(values, *others):
+    return lax.optimization_barrier((values, others))[0]
 
 
 def shards(
@@ -870,22 +1040,24 @@
     )
     ff_other = swap(ff_parts)
 
+    staged = count == 16
     ff_local = up_proj.shape[1]
-    third = ff_local * 2 // 3
-    ff_keeps, ff_sends = row_products(
-        orders,
-        count,
-        where,
-        [second_low, grad_low],
-        [grad_hidden, active_low],
-        [
-            [(0, 0, 0, third)],
-            [(0, 0, third, ff_local - third), (1, 1, 0, 2 * third - ff_local)],
-            [(1, 1, 2 * third - ff_local, third)],
-        ],
-        "ff_grads",
-    )
-    ff_sends, ff_other = lax.optimization_barrier((ff_sends, ff_other))
+    large = ff_local * 5 // 6
+    small_part = ff_local - large
+    ff_portions = [
+        [(0, 0, 0, large)],
+        [(1, 1, 0, large)],
+        [(0, 0, large, small_part), (1, 1, large, small_part)],
+    ]
+    ff_lefts, ff_rights = [second_low, grad_low], [grad_hidden, active_low]
+    ff_args = (orders, count, where)
+    if staged:
+        (ff_sends,) = row_products(
+            *ff_args, ff_lefts, ff_rights, ff_portions, "ff_grads_send", (1,)
+        )
+        ff_other = after(ff_other, ff_sends)
+    else:
+        ff_keeps, ff_sends = row_products(*ff_args, ff_lefts, ff_rights, ff_portions, "ff_grads")
     ff_arriving = [hop(send, order[-1]) for send, order in zip(ff_sends, orders)]
 
     layer_out, gain_two_grad, grad_mid, grad_mid_low, *grad_projected, normed_part = (
@@ -908,7 +1080,24 @@
         where, tokens, grad_mid, normed_part, swap(normed_part), gain_one, gain_two_grad
     )
 
+    if staged:
+        ff_lefts = after(ff_lefts, grad_embed_half)
+        (ff_keeps,) = row_products(
+            *ff_args, ff_lefts, ff_rights, ff_portions, "ff_grads_keep", (0,)
+        )
+        grad_embed_half = after(grad_embed_half, ff_arriving[2])
     first = hop(grad_embed_half, orders[0][0])
+    if staged:
+        first = after(first, (ff_keeps, ff_arriving))
+    at_portions = [
+        [(0, 0, 0, half_width)],
+        [(0, 1, 0, half_width)],
+        [(0, 2, 0, half_width), (1, 3, 0, half_width), (2, 4, 0, EXTRA)],
+    ]
+    at_lefts = [normed_low, grad_mid_low, small]
+    at_rights = [*grad_projected, attended, jnp.eye(EXTRA, dtype=bf16)]
+    at_widths = [sum(piece[3] for piece in portion) for portion in at_portions]
+    ff_widths = [sum(piece[3] for piece in portion) for portion in ff_portions]
     early, late = [], []
     for c, order in enumerate(orders):
         block = jnp.stack([grad_embed_half[:, span(c)], first[:, span(c)]])
@@ -917,50 +1106,52 @@
         early.append(block)
         late.append(hop(block, order[-1]))
     total, bias = kernel_grad(0, orders, where, band_mask, pixels, early, None, None)
+    if staged:
+        sends, keeps = merged_products(
+            orders, where, after(at_lefts, early), at_rights, at_portions, ff_keeps, ff_arriving
+        )
+        sends, late, total = lax.optimization_barrier((sends, late, total))
+        arriving = [hop(send, order[-2]) for send, order in zip(sends, orders)]
     blocks = kernel_grad(1, orders, where, band_mask, pixels, late, total, bias)
+    spread_blocks = lax.all_to_all(blocks, "band", 0, 0, tiled=True)
     own_pixels, other_pixels = pixel_grad(orders, where, band_mask, early, late, kernels)
+    if staged:
+        arriving = after(arriving, (blocks, own_pixels))
+        sends, keeps = second_sum(where, keeps, arriving, ff_widths, at_widths)
+        arriving = [hop(send, order[-3]) for send, order in zip(sends, orders)]
+        spread_blocks = after(spread_blocks, sends)
+    grad_mix, wave_kernels, wave_biases = mix_grad(
+        where, wave_ids, spread_blocks, gen_rows, bias_gen, wave_count, count
+    )
+    grad_mix = grad_mix + swap(grad_mix)
+    grad_mix = jnp.broadcast_to(grad_mix[None], (count, *grad_mix.shape))
+    grad_mix = lax.all_to_all(grad_mix, "band", 0, 0, tiled=True)
+    if staged:
+        arriving = after(arriving, grad_mix)
+        ff_send, ff_kept, sends, keeps = third_sum(where, keeps, arriving, ff_widths, at_widths)
+        ff_last = hop(ff_send, orders[0][0])
+        arriving = [hop(send, orders[(c + 1) % 3][-3]) for c, send in enumerate(sends)]
+        grad_mix = after(grad_mix, ff_send)
+    hyper_grads = hyper_backward(
+        where, grad_mix, wave_table, hyper_weights, hyper_gains, hyper_kept
+    )
+    grad_kernel_gen, grad_bias_gen = generator_grads(where, mix_low, wave_kernels, wave_biases)
     grad_pixels = (own_pixels.astype(f32) + swap(other_pixels).astype(f32)).astype(bf16)
     grad_pixels = grad_pixels[:, None]
-
-    blocks = lax.all_to_all(blocks, "band", 0, 0, tiled=True)
-    grad_mix, wave_kernels, wave_biases = mix_grad(
-        where, wave_ids, blocks, gen_rows, bias_gen, wave_count, count
-    )
-    grad_kernel_gen, grad_bias_gen = generator_grads(where, mix_low, wave_kernels, wave_biases)
-    grad_mix = grad_mix + swap(grad_mix)
-    step = 1
-    while step < count:
-        if step * 4 <= count:
-            grad_mix = (grad_mix + hop(grad_mix, step)) + (
-                hop(grad_mix, 2 * step) + hop(grad_mix, 3 * step)
-            )
-            step *= 4
-        else:
-            grad_mix = grad_mix + hop(grad_mix, step)
-            step *= 2
-    hyper_grads = hyper_backward(
-        where, grad_mix, wave_table, hyper_weights, hyper_gains, hyper_kept
-    )
-
-    at_keeps, at_sends = row_products(
-        orders,
-        count,
-        where,
-        [normed_low, grad_mid_low, small],
-        [*grad_projected, attended, jnp.eye(EXTRA, dtype=bf16)],
-        [
-            [(0, 0, 0, half_width), (0, 1, 0, 256)],
-            [(0, 1, 256, half_width - 256), (0, 2, 0, half_width), (1, 3, 0, 128)],
-            [(1, 3, 128, half_width - 128), (2, 4, 0, EXTRA)],
-        ],
-        "attention_grads",
-    )
-    ff_keeps, ff_arriving, at_sends, _ = lax.optimization_barrier(
-        (ff_keeps, ff_arriving, at_sends, late)
-    )
-    ff_sums = jnp.concatenate(scatter_sum(ff_keeps, None, orders, ff_arriving), axis=1)
-    at_sums = jnp.concatenate(scatter_sum(at_keeps, at_sends, orders), axis=1)
-    grad_up, grad_down = ff_sums[:, :ff_local], ff_sums[:, ff_local:]
+    if staged:
+        arriving = after(arriving, (hyper_grads[0], grad_bias_gen))
+        grad_up, grad_down, send, kept = fourth_sum(
+            where, ff_kept, ff_last, keeps, arriving, large
+        )
+        at_sums = kept + hop(send, orders[0][0]).astype(f32)
+    else:
+        at_keeps, at_sends = row_products(
+            orders, count, where, at_lefts, at_rights, at_portions, "attention_grads"
+        )
+        up_sum, down_sum, both = scatter_sum(ff_keeps, None, orders, ff_arriving)
+        grad_up = jnp.concatenate([up_sum, both[:, :small_part]], axis=1)
+        grad_down = jnp.concatenate([down_sum, both[:, small_part:]], axis=1)
+        at_sums = jnp.concatenate(scatter_sum(at_keeps, at_sends, orders), axis=1)
     grad_in_proj = jnp.stack(
         [at_sums[:, i * half_width : (i + 1) * half_width] for i in range(3)]
     )

time: 251 us -> 205 us (0.82)
  waiting for transfers between devices: 84.7 us -> 61.2 us
  starting transfers between devices: 63.3 us -> 49.2 us
  Pallas kernels: 70.7 us -> 58.2 us
  blocking collectives: 0 us -> 11.3 us
  other arithmetic: 14.4 us -> 5.4 us
    ppermute x46 -> x34, waiting for transfers between devices: 74.7 us -> 47.7 us  [hop(): return lax.ppermute(values, 'band', [(i, i ^ step) for i in range(count)])]
    ppermute x46 -> x34, starting transfers between devices: 47.8 us -> 34.6 us  [hop(): return lax.ppermute(values, 'band', [(i, i ^ step) for i in range(count)])]
    pallas_call x15 -> x19, Pallas kernels: 70.7 us -> 58.2 us  [local_call(): pl.pallas_call(kernel, in_specs=[smem] * (1 + len(tables)) + [vmem] * len...]
    all_to_all x0 -> x1, blocking collectives: none -> 11.3 us  [shards(): grad_mix = lax.all_to_all(grad_mix, 'band', 0, 0, tiled=True)]
    convert_element_type x27 -> x9, other arithmetic: 9.44 us -> 0.48 us  [scatter_sum(): sends.append((k[half:].astype(f32) + a[half:].astype(f32)).astype(bf16))]
    unnamed x63 -> x113, local copies, waits for them, and re-layouts: 8.63 us -> 14.5 us
  transfers between devices with their start and end apart: 54 -> 42, of which waited for: 29 -> 24; matrix products, arithmetic and copies ran while one was open for 7% -> 2% of each run, Pallas kernels for 16% -> 22%
where the time goes in v2:
time: 205 us; the launch traced here: 204 us
  waiting for transfers between devices  61.2 us (30%)
  Pallas kernels  58.2 us (28%)
  starting transfers between devices  49.2 us (24%)
  local copies, waits for them, and re-layouts  17.1 us (8%)
  blocking collectives  11.3 us (6%)
  other arithmetic  5.4 us (3%)
    pallas_call x19, Pallas kernels, local_call(): pl.pallas_call(kernel, in_specs=[smem] * (1 + len(tables)) + [vmem] * len...  58.2 us
    ppermute x34, waiting for transfers between devices, hop(): return lax.ppermute(values, 'band', [(i, i ^ step) for i in range(count)])  47.7 us
    ppermute x34, starting transfers between devices, hop(): return lax.ppermute(values, 'band', [(i, i ^ step) for i in range(count)])  34.6 us
    unnamed x113, local copies, waits for them, and re-layouts  14.5 us
    all_to_all x1, blocking collectives, shards(): grad_mix = lax.all_to_all(grad_mix, 'band', 0, 0, tiled=True)  11.3 us
    all_to_all x1, starting transfers between devices, shards(): lax.all_to_all(slot_piece, 'band', 0, 0, tiled=True)  8.5 us
    all_to_all x1, waiting for transfers between devices, shards(): lax.all_to_all(slot_piece, 'band', 0, 0, tiled=True)  7.89 us
    ppermute x6, waiting for transfers between devices, swap(): return lax.ppermute(values, 'head', [(0, 1), (1, 0)])  5.55 us
  transfers between devices with their start and end apart: 42, of which 24 were waited for; matrix products, arithmetic and copies ran while one was open for 2% of the time, Pallas kernels for 22%

profile of v2, /device:TPU:0, one launch (start us, length us, event | category | flops | bytes accessed | tf_op | source)
XLA Modules:
  0.0 203.8 jit_solution(10958483028855832503)
XLA Ops:
  2.6 6.6 %hyper_forward.1 = (bf16[256,384]{1,0:T(8,128)(2,1)}, f32[1,384]{1,0:T(1,128)}, bf16[16,128]{1,0:T(8,128)(2,1)}, f32[16,384]{1,0:T(8,128)}, f32[4,16,16]{2,1,0:T...) custom-call(s32[2]{0:T(128)} %pad_add_fusion.where_ref, ...), custom_call_target="tpu_custom_call" | custom-call | flops 1610612736 | bytes 4427456 | tf_op jit(solution)/shard_map/hyper_forward/pallas_call | solution.py:182
  9.2 8.5 %all-to-all-start = ((bf16[16,16,384]{2,1,0:T(8,128)(2,1)}), bf16[16,16,384]{2,1,0:T(8,128)(2,1)S(1)}, u32[]{:S(2)}, u32[]{:S(2)}) async-start(bf16[16,16,384]{2,1,0:T(8,128)(2,1)} %bitcast.64), calls=%async_computation | async-start | bytes 393216 | tf_op jit(solution)/shard_map/all_to_all | solution.py:1023
  18.3 7.9 %all-to-all-done = bf16[16,16,384]{2,1,0:T(8,128)(2,1)S(1)} async-done(((bf16[16,16,384]{2,1,0:T(8,128)(2,1)}), bf16[16,16,384]{2,1,0:T(8,128)(2,1)S(1)}, u32[]{:S(2)}, u32[]{:S(2)}) %all-to-all-start) | async-done | bytes 196640 | tf_op jit(solution)/shard_map/all_to_all | solution.py:1023
  31.5 5.6 %collective-permute-done.6 = bf16[8,196,128]{2,1,0:T(8,128)(2,1)S(1)} collective-permute-done((bf16[8,196,128]{2,1,0:T(8,128)(2,1)S(1)}, bf16[8,196,128]{2,1,0:T(8,128)(2,1)S(1)}, u32[]{:S(2)}, u32[]{:S(2)}) %collective-permute-start.6) | collective-permute-done | bytes 401440 | tf_op jit(solution)/shard_map/ppermute | solution.py:99
  40.9 2.1 %collective-permute-done.7 = bf16[4,196,128]{2,1,0:T(8,128)(2,1)S(1)} collective-permute-done((bf16[4,196,128]{2,1,0:T(8,128)(2,1)S(1)}, bf16[4,196,128]{2,1,0:T(8,128)(2,1)S(1)}, u32[]{:S(2)}, u32[]{:S(2)}) %collective-permute-start.7) | collective-permute-done | bytes 200736 | tf_op jit(solution)/shard_map/ppermute | solution.py:99
  52.2 2.9 %collective-permute-start.9 = (bf16[1,196,384]{2,1,0:T(8,128)(2,1)}, bf16[1,196,384]{2,1,0:T(8,128)(2,1)}, u32[]{:S(2)}, u32[]{:S(2)}) collective-permute-start(bf16[1,196,384]{2,1,0:T(8,128)(2,1)} %pad_maximum_fusion.7), channel_id=1, source_target_pairs={{0,16},{2,18},{4,20},{6,22},{8,24},{10,26},{12,28},{14,30},{16,0},... | collective-permute-start | bytes 451592 | tf_op jit(solution)/shard_map/ppermute | solution.py:99
  55.1 5.2 %collective-permute-done.9 = bf16[1,196,384]{2,1,0:T(8,128)(2,1)} collective-permute-done((bf16[1,196,384]{2,1,0:T(8,128)(2,1)}, bf16[1,196,384]{2,1,0:T(8,128)(2,1)}, u32[]{:S(2)}, u32[]{:S(2)}) %collective-permute-start.9) | collective-permute-done | bytes 150560 | tf_op jit(solution)/shard_map/ppermute | solution.py:99
  64.0 2.5 %attention_forward.1 = (f32[196,768]{1,0:T(8,128)S(1)}, bf16[196,768]{1,0:T(8,128)(2,1)S(1)}, bf16[196,384]{1,0:T(8,128)(2,1)S(1)}, bf16[196,384]{1,0:T(8,128)(2...) custom-call(s32[2]{0:T(128)S(1)} %copy-done.27, ...), custom_call_target="tpu_custom_call" | custom-call | flops 580435968 | bytes 5691264 | tf_op jit(solution)/shard_map/attention_forward/pallas_call | solution.py:182
  69.8 3.5 %feed_forward.1 = (f32[196,768]{1,0:T(8,128)S(1)}, bf16[196,768]{1,0:T(8,128)(2,1)S(1)}, bf16[196,1536]{1,0:T(8,128)(2,1)S(1)}, bf16[196,1536]{1,0:T(8,128)(2,1)S(1)}, bf16[404,768]{1,0:T(8,128)(2,1)S(1)}) custom-call(s32[2]{0:T(128)S(1)} %copy-done.27, f32[196,768]{1,0:T(8,128)S(1)} %get-tuple-element.138.tokens_ref, ...), custom_call_target="tpu_custom_call" | custom-call | flops 1849688064 | bytes 8953344 | tf_op jit(solution)/shard_map/feed_forward/pallas_call | solution.py:182
  77.7 4.2 %attention_backward.1 = (bf16[196,768]{1,0:T(8,128)(2,1)}, f32[1,768]{1,0:T(1,128)S(1)}, f32[196,768]{1,0:T(8,128)S(1)}, bf16[196,768]{1,0:T(8,128)(2,1)S(1)}, b...) custom-call(s32[2]{0:T(128)S(1)} %copy-done.27, ...), custom_call_target="tpu_custom_call" | custom-call | flops 698449920 | bytes 7838592 | tf_op jit(solution)/shard_map/attention_backward/pallas_call | solution.py:182
  84.8 3.1 %collective-permute-done.14.refs_13_ = bf16[384,512]{1,0:T(8,128)(2,1)S(1)} collective-permute-done((bf16[384,512]{1,0:T(8,128)(2,1)S(1)}, bf16[384,512]{1,0:T(8,128)(2,1)S(1)}, u32[]{:S(2)}, u32[]{:S(2)}) %collective-permute-start.14) | collective-permute-done | bytes 393248 | tf_op jit(solution)/shard_map/ppermute | solution.py:99
  87.9 2.2 %collective-permute-start.15 = (bf16[196,384]{1,0:T(8,128)(2,1)S(1)}, bf16[196,384]{1,0:T(8,128)(2,1)S(1)}, u32[]{:S(2)}, u32[]{:S(2)}) collective-permute-start(bf16[196,384]{1,0:T(8,128)(2,1)S(1)} %get-tuple-element.158), channel_id=1, source_target_pairs={{0,16},{2,18},{4,20},{6,22},{8,24},{10,26},{12,28},{14,30},{16,0},... | collective-permute-start | bytes 451592 | tf_op jit(solution)/shard_map/ppermute | solution.py:99
  91.7 7.4 %collective-permute-done.16.refs_11_ = bf16[384,1280]{1,0:T(8,128)(2,1)S(1)} collective-permute-done((bf16[384,1280]{1,0:T(8,128)(2,1)S(1)}, bf16[384,1280]{1,0:T(8,128)(2,1)S(1)}, u32[]{:S(2)}, u32[]{:S(2)}) %collective-permute-start.16) | collective-permute-done | bytes 983072 | tf_op jit(solution)/shard_map/ppermute | solution.py:99
  102.7 2.2 %collective-permute-done.22 = bf16[2,196,128]{2,1,0:T(8,128)(2,1)S(1)} collective-permute-done((bf16[2,196,128]{2,1,0:T(8,128)(2,1)S(1)}, bf16[2,196,128]{2,1,0:T(8,128)(2,1)S(1)}, u32[]{:S(2)}, u32[]{:S(2)}) %collective-permute-start.22) | collective-permute-done | bytes 100384 | tf_op jit(solution)/shard_map/ppermute | solution.py:99
  116.9 4.5 %kernel_grad.1 = (f32[384,256]{1,0:T(8,128)S(1)}, f32[1,384]{1,0:T(1,128)S(1)}) custom-call(s32[2]{0:T(128)S(1)} %copy-done.27, s32[16,16]{1,0:T(8,128)S(1)} %copy-done.24, bf16[16,196,256]{2,1,0:T(8,128)(2,1)S(1)} %bitcast.49, bf16[8,196,128]{2,1,0:T(8,128)(2,1)S(1)} %pad_maximum_fusion.refs_0_, bf16[8,196,128]{2,1,0:T(8,128)(2,1)S(1)} %pad_maximum_fusion.1.refs_1_, ...), custom_call_target="tpu_custom_call" | custom-call | flops 308281344 | bytes 3204608 | tf_op jit(solution)/shard_map/kernel_grad/pallas_call | solution.py:182
  121.4 3.9 %attention_grads.1 = (bf16[192,2048]{1,0:T(8,128)(2,1)}, bf16[192,2048]{1,0:T(8,128)(2,1)}, bf16[192,2560]{1,0:T(8,128)(2,1)}, bf16[192,2048]{1,0:T(8,128)(2,1)S...) custom-call(s32[2]{0:T(128)S(1)} %copy-done.27, bf16[196,768]{1,0:T(8,128)(2,1)S(1)} %get-tuple-element.168.refs_0_, ...), custom_call_target="tpu_custom_call" | custom-call | flops 539492352 | bytes 11558912 | tf_op jit(solution)/shard_map/attention_grads/pallas_call | solution.py:182
  129.7 4.9 %kernel_grad_end.1 = bf16[16,18,384]{2,1,0:T(8,128)(2,1)S(1)} custom-call(s32[2]{0:T(128)S(1)} %copy-done.27, s32[16,16]{1,0:T(8,128)S(1)} %copy-done.24, bf16[16,196,256]{2,1,0:T(8,128)(2,1)S(1)} %bitcast.50, bf16[8,196,128]{2,1,0:T(8,128)(2,1)S(1)} %collective-permute-done.24.refs_3_.refs_0_, ...), custom_call_target="tpu_custom_call" | custom-call | flops 308281344 | bytes 3425792 | tf_op jit(solution)/shard_map/kernel_grad_end/pallas_call | solution.py:182
  136.8 5.5 %all-to-all-start.1 = ((bf16[16,18,384]{2,1,0:T(8,128)(2,1)}), bf16[16,18,384]{2,1,0:T(8,128)(2,1)}, u32[]{:S(2)}, u32[]{:S(2)}) async-start(bf16[16,18,384]{2,1,0:T(8,128)(2,1)} %copy-done.10), calls=%async_computation.1 | async-start | bytes 589824 | tf_op jit(solution)/shard_map/all_to_all | solution.py:1116
  148.7 3.2 %second_sum.1 = (bf16[96,2048]{1,0:T(8,128)(2,1)}, bf16[96,2048]{1,0:T(8,128)(2,1)}, bf16[96,2560]{1,0:T(8,128)(2,1)}, f32[96,2048]{1,0:T(8,128)S(1)}, f32[96,2048]{1,0:T(8,128)S(1)}, /*index=5*/f32[96,2560]{1,0:T(8,128)S(1)}) custom-call(s32[2]{0:T(128)S(1)} %copy-done.27, bf16[192,2048]{1,0:T(8,128)(2,1)S(1)} %copy-done.18, ...), custom_call_target="tpu_custom_call" | custom-call | bytes 8945664 | tf_op jit(solution)/shard_map/second_sum/pallas_call | solution.py:182
  157.5 3.0 %mix_grad.1 = (f32[16,128]{1,0:T(8,128)S(1)}, bf16[256,384]{1,0:T(8,128)(2,1)S(1)}, f32[16,384]{1,0:T(8,128)S(1)}) custom-call(s32[2]{0:T(128)S(1)} %copy-done.27, s32[16,1]{1,0:T(8,128)S(1)} %copy-done.31, bf16[16,18,384]{2,1,0:T(8,128)(2,1)} %all-to-all-done.1.blocks_ref, bf16[2048,384]{1,0:T(8,128)(2,1)S(1)} %bitcast.59, bf16[128,384]{1,0:T(8,128)(2,1)S(1)} %copy-done.28), custom_call_target="tpu_custom_call" | custom-call | flops 402653184 | bytes 2121792 | tf_op jit(solution)/shard_map/mix_grad/pallas_call | solution.py:182
  161.8 11.3 %all_to_all.15.grad_ref = f32[16,16,128]{2,1,0:T(8,128)S(1)} all-to-all(f32[16,16,128]{2,1,0:T(8,128)S(1)} %broadcast_in_dim.30), channel_id=1, replica_groups=mesh['band'=16,'head'=2] {'band'}, dimensions={0} | all-to-all | bytes 262144 | tf_op jit(solution)/shard_map/all_to_all | solution.py:1128
  178.3 3.4 %generator_grads.1 = (f32[2048,384]{1,0:T(8,128)}, f32[128,384]{1,0:T(8,128)}) custom-call(s32[2]{0:T(128)S(1)} %copy-done.27, bf16[16,128]{1,0:T(8,128)(2,1)S(1)} %copy-done.43, bf16[256,384]{1,0:T(8,128)(2,1)S(1)} %get-tuple-element.225.kernels_ref, f32[16,384]{1,0:T(8,128)S(1)} %get-tuple-element.226.biases_ref), custom_call_target="tpu_custom_call" | custom-call | flops 402653184 | bytes 3567616 | tf_op jit(solution)/shard_map/generator_grads/pallas_call | solution.py:182
  181.8 6.2 %hyper_backward.1 = (f32[16,128]{1,0:T(8,128)}, f32[128,384]{1,0:T(8,128)}, f32[128,128]{1,0:T(8,128)}, f32[128,2048]{1,0:T(8,128)}, f32[2048,128]{1,0:T(8,128)}, /*index=5*/f32[1,128]{1,0:T(1,128)}, f32[1,128]{1,0:T(1,128)}) custom-call(s32[2]{0:T(128)S(1)} %copy-done.27, f32[16,16,128]{2,1,0:T(8,128)S(1)} %all_to_all.15.grad_ref, ...), custom_call_target="tpu_custom_call" | custom-call | flops 335544320 | bytes 5052544 | tf_op jit(solution)/shard_map/hyper_backward/pallas_call | solution.py:182
  193.7 7.9 %collective-permute-done.39 = bf16[48,1792]{1,0:T(8,128)(2,1)S(1)} collective-permute-done((bf16[48,1792]{1,0:T(8,128)(2,1)S(1)}, bf16[48,1792]{1,0:T(8,128)(2,1)S(1)}, u32[]{:S(2)}, u32[]{:S(2)}) %collective-permute-start.39) | collective-permute-done | bytes 172064 | tf_op jit(solution)/shard_map/ppermute | solution.py:99
  (230 shorter events, 84.7 us)
Async XLA Ops:
  9.2 17.0 %all-to-all-start = ((bf16[16,16,384]{2,1,0:T(8,128)(2,1)}), bf16[16,16,384]{2,1,0:T(8,128)(2,1)S(1)}, u32[]{:S(2)}, u32[]{:S(2)}) async-start(bf16[16,16,384]{2,1,0:T(8,128)(2,1)} %bitcast.64), calls=%async_computation | async-start | bytes 393216 | tf_op jit(solution)/shard_map/all_to_all | solution.py:1023
  27.7 9.3 %collective-permute-start.6 = (bf16[8,196,128]{2,1,0:T(8,128)(2,1)S(1)}, bf16[8,196,128]{2,1,0:T(8,128)(2,1)S(1)}, u32[]{:S(2)}, u32[]{:S(2)}) collective-permute-start(bf16[8,196,128]{2,1,0:T(8,128)(2,1)S(1)} %get-tuple-element.136), channel_id=1, source_target_pairs={{0,8},{2,10},{4,12},{6,14},{8,0},{10,2},{12,4},{14,6},{16,24},{18,... | collective-permute-start | bytes 1204232 | tf_op jit(solution)/shard_map/ppermute | solution.py:99
  28.7 10.1 %collective-permute-start.3 = (bf16[8,196,128]{2,1,0:T(8,128)(2,1)S(1)}, bf16[8,196,128]{2,1,0:T(8,128)(2,1)S(1)}, u32[]{:S(2)}, u32[]{:S(2)}) collective-permute-start(bf16[8,196,128]{2,1,0:T(8,128)(2,1)S(1)} %get-tuple-element.134), channel_id=1, source_target_pairs={{0,4},{2,6},{4,0},{6,2},{8,12},{10,14},{12,8},{14,10},{16,20},{18,... | collective-permute-start | bytes 1204232 | tf_op jit(solution)/shard_map/ppermute | solution.py:99
  29.4 9.8 %collective-permute-start = (bf16[8,196,128]{2,1,0:T(8,128)(2,1)S(1)}, bf16[8,196,128]{2,1,0:T(8,128)(2,1)S(1)}, u32[]{:S(2)}, u32[]{:S(2)}) collective-permute-start(bf16[8,196,128]{2,1,0:T(8,128)(2,1)S(1)} %get-tuple-element.132), channel_id=1, source_target_pairs={{0,2},{2,0},{4,6},{6,4},{8,10},{10,8},{12,14},{14,12},{16,18},{18,... | collective-permute-start | bytes 1204232 | tf_op jit(solution)/shard_map/ppermute | solution.py:99
  75.0 24.1 %collective-permute-start.16 = (bf16[384,1280]{1,0:T(8,128)(2,1)S(1)}, bf16[384,1280]{1,0:T(8,128)(2,1)S(1)}, u32[]{:S(2)}, u32[]{:S(2)}) collective-permute-start(bf16[384,1280]{1,0:T(8,128)(2,1)S(1)} %get-tuple-element.145), channel_id=1, source_target_pairs={{0,2},{2,0},{4,6},{6,4},{8,10},{10,8},{12,14},{14,12},{16,18},{18,... | collective-permute-start | bytes 2949128 | tf_op jit(solution)/shard_map/ppermute | solution.py:99
  76.2 23.8 %collective-permute-start.17 = (bf16[384,1280]{1,0:T(8,128)(2,1)S(1)}, bf16[384,1280]{1,0:T(8,128)(2,1)S(1)}, u32[]{:S(2)}, u32[]{:S(2)}) collective-permute-start(bf16[384,1280]{1,0:T(8,128)(2,1)S(1)} %get-tuple-element.146), channel_id=1, source_target_pairs={{0,4},{2,6},{4,0},{6,2},{8,12},{10,14},{12,8},{14,10},{16,20},{18,... | collective-permute-start | bytes 2949128 | tf_op jit(solution)/shard_map/ppermute | solution.py:99
  77.1 10.8 %collective-permute-start.14 = (bf16[384,512]{1,0:T(8,128)(2,1)S(1)}, bf16[384,512]{1,0:T(8,128)(2,1)S(1)}, u32[]{:S(2)}, u32[]{:S(2)}) collective-permute-start(bf16[384,512]{1,0:T(8,128)(2,1)S(1)} %get-tuple-element.147), channel_id=1, source_target_pairs={{0,8},{2,10},{4,12},{6,14},{8,0},{10,2},{12,4},{14,6},{16,24},{18,... | collective-permute-start | bytes 1179656 | tf_op jit(solution)/shard_map/ppermute | solution.py:99
  87.9 12.1 %collective-permute-start.15 = (bf16[196,384]{1,0:T(8,128)(2,1)S(1)}, bf16[196,384]{1,0:T(8,128)(2,1)S(1)}, u32[]{:S(2)}, u32[]{:S(2)}) collective-permute-start(bf16[196,384]{1,0:T(8,128)(2,1)S(1)} %get-tuple-element.158), channel_id=1, source_target_pairs={{0,16},{2,18},{4,20},{6,22},{8,24},{10,26},{12,28},{14,30},{16,0},... | collective-permute-start | bytes 451592 | tf_op jit(solution)/shard_map/ppermute | solution.py:99
  110.8 17.3 %collective-permute-start.26 = (bf16[8,196,128]{2,1,0:T(8,128)(2,1)S(1)}, bf16[8,196,128]{2,1,0:T(8,128)(2,1)S(1)}, u32[]{:S(2)}, u32[]{:S(2)}) collective-permute-start(bf16[8,196,128]{2,1,0:T(8,128)(2,1)S(1)} %pad_maximum_fusion.2.refs_2_), channel_id=1, source_target_pairs={{0,8},{2,10},{4,12},{6,14},{8,0},{10,2},{12,4},{14,6},{16,24},{18,... | collective-permute-start | bytes 1204232 | tf_op jit(solution)/shard_map/ppermute | solution.py:99
  114.9 13.2 %collective-permute-start.25 = (bf16[8,196,128]{2,1,0:T(8,128)(2,1)S(1)}, bf16[8,196,128]{2,1,0:T(8,128)(2,1)S(1)}, u32[]{:S(2)}, u32[]{:S(2)}) collective-permute-start(bf16[8,196,128]{2,1,0:T(8,128)(2,1)S(1)} %pad_maximum_fusion.1.refs_1_), channel_id=1, source_target_pairs={{0,4},{2,6},{4,0},{6,2},{8,12},{10,14},{12,8},{14,10},{16,20},{18,... | collective-permute-start | bytes 1204232 | tf_op jit(solution)/shard_map/ppermute | solution.py:99
  115.8 12.3 %collective-permute-start.24 = (bf16[8,196,128]{2,1,0:T(8,128)(2,1)S(1)}, bf16[8,196,128]{2,1,0:T(8,128)(2,1)S(1)}, u32[]{:S(2)}, u32[]{:S(2)}) collective-permute-start(bf16[8,196,128]{2,1,0:T(8,128)(2,1)S(1)} %pad_maximum_fusion.refs_0_), channel_id=1, source_target_pairs={{0,2},{2,0},{4,6},{6,4},{8,10},{10,8},{12,14},{14,12},{16,18},{18,... | collective-permute-start | bytes 1204232 | tf_op jit(solution)/shard_map/ppermute | solution.py:99
  128.1 20.6 %collective-permute-start.30 = (bf16[192,2560]{1,0:T(8,128)(2,1)}, bf16[192,2560]{1,0:T(8,128)(2,1)}, u32[]{:S(2)}, u32[]{:S(2)}) collective-permute-start(bf16[192,2560]{1,0:T(8,128)(2,1)} %get-tuple-element.189), channel_id=1, source_target_pairs={{0,2},{2,0},{4,6},{6,4},{8,10},{10,8},{12,14},{14,12},{16,18},{18,... | collective-permute-start | bytes 2949128 | tf_op jit(solution)/shard_map/ppermute | solution.py:99
  128.2 19.5 %collective-permute-start.28 = (bf16[192,2048]{1,0:T(8,128)(2,1)}, bf16[192,2048]{1,0:T(8,128)(2,1)}, u32[]{:S(2)}, u32[]{:S(2)}) collective-permute-start(bf16[192,2048]{1,0:T(8,128)(2,1)} %get-tuple-element.187), channel_id=1, source_target_pairs={{0,4},{2,6},{4,0},{6,2},{8,12},{10,14},{12,8},{14,10},{16,20},{18,... | collective-permute-start | bytes 2359304 | tf_op jit(solution)/shard_map/ppermute | solution.py:99
  129.7 17.9 %collective-permute-start.29 = (bf16[192,2048]{1,0:T(8,128)(2,1)}, bf16[192,2048]{1,0:T(8,128)(2,1)}, u32[]{:S(2)}, u32[]{:S(2)}) collective-permute-start(bf16[192,2048]{1,0:T(8,128)(2,1)} %get-tuple-element.188), channel_id=1, source_target_pairs={{0,8},{2,10},{4,12},{6,14},{8,0},{10,2},{12,4},{14,6},{16,24},{18,... | collective-permute-start | bytes 2359304 | tf_op jit(solution)/shard_map/ppermute | solution.py:99
  136.8 19.8 %all-to-all-start.1 = ((bf16[16,18,384]{2,1,0:T(8,128)(2,1)}), bf16[16,18,384]{2,1,0:T(8,128)(2,1)}, u32[]{:S(2)}, u32[]{:S(2)}) async-start(bf16[16,18,384]{2,1,0:T(8,128)(2,1)} %copy-done.10), calls=%async_computation.1 | async-start | bytes 589824 | tf_op jit(solution)/shard_map/all_to_all | solution.py:1116
  147.6 43.7 %collective-permute-start.27 = (bf16[8,196,256]{2,0,1:T(8,128)(2,1)}, bf16[8,196,256]{2,0,1:T(8,128)(2,1)}, u32[]{:S(2)}, u32[]{:S(2)}) collective-permute-start(bf16[8,196,256]{2,0,1:T(8,128)(2,1)} %copy.48), channel_id=1, source_target_pairs={{0,1},{1,0},{2,3},{3,2},{4,5},{5,4},{6,7},{7,6},{8,9},{9,8},{10,11... | collective-permute-start | bytes 2408456 | tf_op jit(solution)/shard_map/ppermute | solution.py:103
  152.8 20.4 %collective-permute-start.33 = (bf16[96,2560]{1,0:T(8,128)(2,1)}, bf16[96,2560]{1,0:T(8,128)(2,1)}, u32[]{:S(2)}, u32[]{:S(2)}) collective-permute-start(bf16[96,2560]{1,0:T(8,128)(2,1)} %get-tuple-element.200), channel_id=1, source_target_pairs={{0,4},{2,6},{4,0},{6,2},{8,12},{10,14},{12,8},{14,10},{16,20},{18,... | collective-permute-start | bytes 1474568 | tf_op jit(solution)/shard_map/ppermute | solution.py:99
  153.7 19.4 %collective-permute-start.31 = (bf16[96,2048]{1,0:T(8,128)(2,1)}, bf16[96,2048]{1,0:T(8,128)(2,1)}, u32[]{:S(2)}, u32[]{:S(2)}) collective-permute-start(bf16[96,2048]{1,0:T(8,128)(2,1)} %get-tuple-element.198), channel_id=1, source_target_pairs={{0,8},{2,10},{4,12},{6,14},{8,0},{10,2},{12,4},{14,6},{16,24},{18,... | collective-permute-start | bytes 1179656 | tf_op jit(solution)/shard_map/ppermute | solution.py:99
  155.1 18.0 %collective-permute-start.32 = (bf16[96,2048]{1,0:T(8,128)(2,1)}, bf16[96,2048]{1,0:T(8,128)(2,1)}, u32[]{:S(2)}, u32[]{:S(2)}) collective-permute-start(bf16[96,2048]{1,0:T(8,128)(2,1)} %get-tuple-element.199), channel_id=1, source_target_pairs={{0,2},{2,0},{4,6},{6,4},{8,10},{10,8},{12,14},{14,12},{16,18},{18,... | collective-permute-start | bytes 1179656 | tf_op jit(solution)/shard_map/ppermute | solution.py:99
  174.9 14.9 %collective-permute-start.35 = (bf16[48,3072]{1,0:T(8,128)(2,1)S(1)}, bf16[48,3072]{1,0:T(8,128)(2,1)S(1)}, u32[]{:S(2)}, u32[]{:S(2)}) collective-permute-start(bf16[48,3072]{1,0:T(8,128)(2,1)S(1)} %get-tuple-element.207), channel_id=1, source_target_pairs={{0,16},{2,18},{4,20},{6,22},{8,24},{10,26},{12,28},{14,30},{16,0},... | collective-permute-start | bytes 884744 | tf_op jit(solution)/shard_map/ppermute | solution.py:99
  175.9 12.2 %collective-permute-start.38 = (bf16[96,1024]{1,0:T(8,128)(2,1)S(1)}, bf16[96,1024]{1,0:T(8,128)(2,1)S(1)}, u32[]{:S(2)}, u32[]{:S(2)}) collective-permute-start(bf16[96,1024]{1,0:T(8,128)(2,1)S(1)} %get-tuple-element.213), channel_id=1, source_target_pairs={{0,8},{2,10},{4,12},{6,14},{8,0},{10,2},{12,4},{14,6},{16,24},{18,... | collective-permute-start | bytes 589832 | tf_op jit(solution)/shard_map/ppermute | solution.py:99
  177.1 10.9 %collective-permute-start.36 = (bf16[96,384]{1,0:T(8,128)(2,1)S(1)}, bf16[96,384]{1,0:T(8,128)(2,1)S(1)}, u32[]{:S(2)}, u32[]{:S(2)}) collective-permute-start(bf16[96,384]{1,0:T(8,128)(2,1)S(1)} %get-tuple-element.211), channel_id=1, source_target_pairs={{0,2},{2,0},{4,6},{6,4},{8,10},{10,8},{12,14},{14,12},{16,18},{18,... | collective-permute-start | bytes 221192 | tf_op jit(solution)/shard_map/ppermute | solution.py:99
  177.7 10.3 %collective-permute-start.37 = (bf16[96,384]{1,0:T(8,128)(2,1)S(1)}, bf16[96,384]{1,0:T(8,128)(2,1)S(1)}, u32[]{:S(2)}, u32[]{:S(2)}) collective-permute-start(bf16[96,384]{1,0:T(8,128)(2,1)S(1)} %get-tuple-element.212), channel_id=1, source_target_pairs={{0,4},{2,6},{4,0},{6,2},{8,12},{10,14},{12,8},{14,10},{16,20},{18,... | collective-permute-start | bytes 221192 | tf_op jit(solution)/shard_map/ppermute | solution.py:99
  191.3 10.3 %collective-permute-start.39 = (bf16[48,1792]{1,0:T(8,128)(2,1)S(1)}, bf16[48,1792]{1,0:T(8,128)(2,1)S(1)}, u32[]{:S(2)}, u32[]{:S(2)}) collective-permute-start(bf16[48,1792]{1,0:T(8,128)(2,1)S(1)} %get-tuple-element.232), channel_id=1, source_target_pairs={{0,16},{2,18},{4,20},{6,22},{8,24},{10,26},{12,28},{14,30},{16,0},... | collective-permute-start | bytes 516104 | tf_op jit(solution)/shard_map/ppermute | solution.py:99
  (73 other events, 433.3 us)

commit v3 on v1

--- a/solution.py
+++ b/solution.py
@@ -10,6 +10,9 @@
 HHEADS = 4
 LANES = 128
 EXTRA = 256
+EARLY = 1024
+HBM = pltpu.HBM
+PART = 208
 
 highest = lax.Precision.HIGHEST
 norm_epsilon = 1e-06
@@ -48,8 +51,14 @@
 
 
 def exact(left, right, dims=((1,), (0,))):
-    return lax.dot_general(
-        left, right, (dims, ((), ())), precision=highest, preferred_element_type=f32
+    def product(a, b):
+        return lax.dot_general(a, b, (dims, ((), ())), preferred_element_type=f32)
+
+    left_high, right_high = left.astype(bf16), right.astype(bf16)
+    left_low = (left - left_high.astype(f32)).astype(bf16)
+    right_low = (right - right_high.astype(f32)).astype(bf16)
+    return product(left_high, right_high) + (
+        product(left_high, right_low) + product(left_low, right_high)
     )
 
 
@@ -67,9 +76,13 @@
     return ((row >> row_shift) & row_mask) == ((column >> column_shift) & column_mask)
 
 
-def onehot_of(wave_column, wave_count):
-    slots = wave_column.shape[0]
-    return wave_column == lax.broadcasted_iota(jnp.int32, (slots, wave_count), 1)
+def onehot_of(ids_ref, wave_count):
+    slots = ids_ref.shape[1]
+    row = lax.broadcasted_iota(jnp.int32, (slots, wave_count), 0)
+    waves = jnp.zeros((slots, wave_count), jnp.int32)
+    for s in range(slots):
+        waves = jnp.where(row == s, ids_ref[0, s], waves)
+    return waves == lax.broadcasted_iota(jnp.int32, (slots, wave_count), 1)
 
 
 def spread(mix, piece):
@@ -171,7 +184,10 @@
     return slice(c * LANES, (c + 1) * LANES)
 
 
-def local_call(kernel, where, tables, args, out_shape, scratch=(), name=None, flops=0):
+def local_call(
+    kernel, where, tables, args, out_shape, scratch=(), name=None, flops=0, mebibytes=24,
+    spaces=None,
+):
     vmem = pl.BlockSpec(memory_space=pltpu.VMEM)
     smem = pl.BlockSpec(memory_space=pltpu.SMEM)
     moved = sum(x.size * x.dtype.itemsize for x in args)
@@ -179,17 +195,20 @@
     return pl.pallas_call(
         kernel,
         in_specs=[smem] * (1 + len(tables)) + [vmem] * len(args),
-        out_specs=[vmem] * len(out_shape),
+        out_specs=[
+            pl.BlockSpec(memory_space=space or pltpu.VMEM)
+            for space in spaces or [None] * len(out_shape)
+        ],
         out_shape=list(out_shape),
         scratch_shapes=list(scratch),
         cost_estimate=pl.CostEstimate(flops=flops, bytes_accessed=moved, transcendentals=0),
-        compiler_params=pltpu.CompilerParams(vmem_limit_bytes=56 * 2**20),
+        compiler_params=pltpu.CompilerParams(vmem_limit_bytes=mebibytes * 2**20),
         name=name,
     )(where, *tables, *args)
 
 
 def hyper_forward(where, wave_ids, band_mask, table, weights, gains, gen_rows, bias_gen, count):
-    slots = wave_ids.shape[0]
+    slots = wave_ids.shape[1]
     wave_count, width = table.shape
     piece = gen_rows.shape[0] // width
     half_width = gen_rows.shape[1]
@@ -226,7 +245,7 @@
         normal_two_out[...] = normal_two
         scale_two_out[...] = scale_two
         mix_out[...] = mix
-        onehot = onehot_of(ids_ref[...], wave_count)
+        onehot = onehot_of(ids_ref, wave_count)
         slot_mix = low_dot(onehot.astype(bf16), mix).astype(bf16)
         piece_out[...] = low_dot(kron_identity(slot_mix, piece), gen_ref[...]).astype(bf16)
         image = lax.broadcasted_iota(jnp.int32, mask_ref.shape, 0) == where_ref[0]
@@ -240,8 +259,8 @@
     return local_call(
         kernel,
         where,
-        [],
-        [wave_ids, band_mask, table, *weights, *gains, gen_rows, bias_gen],
+        [wave_ids],
+        [band_mask, table, *weights, *gains, gen_rows, bias_gen],
         [
             jax.ShapeDtypeStruct((slots * piece, half_width), bf16),
             shape(1, half_width),
@@ -256,6 +275,7 @@
             shape(wave_count, 1),
         ],
         name="hyper_forward",
+        mebibytes=56,
         flops=8 * slots * piece * gen_rows.size,
     )
 
@@ -395,8 +415,10 @@
             active_out[:, columns] = (hidden * factor).astype(bf16)
             grad_active = contract_last(cotangent_ref[...], down_ref[columns, :])
             grad_hidden_out[:, columns] = (grad_active * slope).astype(bf16)
-        parts_out[0] = low_dot(active_out[...], down_ref[...]).astype(bf16)
-        parts_out[1] = contract_last(grad_hidden_out[...], up_ref[...]).astype(bf16)
+        parts_out[:patches, :] = low_dot(active_out[...], down_ref[...]).astype(bf16)
+        parts_out[PART : PART + patches, :] = contract_last(
+            grad_hidden_out[...], up_ref[...]
+        ).astype(bf16)
 
     return local_call(
         kernel,
@@ -408,7 +430,7 @@
             jax.ShapeDtypeStruct((patches, width), bf16),
             jax.ShapeDtypeStruct((patches, local), bf16),
             jax.ShapeDtypeStruct((patches, local), bf16),
-            jax.ShapeDtypeStruct((2, patches, width), bf16),
+            jax.ShapeDtypeStruct((PART + patches, width), bf16),
         ],
         name="feed_forward",
         flops=8 * patches * up.size,
@@ -428,9 +450,10 @@
         query_out, key_out, value_out, part_out,
     ):
         mid_values = mid_ref[...]
-        down = own_ref[0].astype(f32) + other_ref[0].astype(f32)
+        down = own_ref[:patches, :].astype(f32) + other_ref[:patches, :].astype(f32)
         layer_out[...] = (mid_values + down).astype(bf16)
-        grad_second = own_ref[1].astype(f32) + other_ref[1].astype(f32)
+        back = slice(PART, PART + patches)
+        grad_second = own_ref[back, :].astype(f32) + other_ref[back, :].astype(f32)
         normal, scale = norm_parts(mid_values)
         gain_out[...] = jnp.sum(grad_second * normal, axis=0, keepdims=True)
         grad_mid = cotangent_ref[...].astype(f32) + norm_grad(
@@ -522,11 +545,11 @@
     )
 
 
-def wave_grads(wave_column, blocks_ref, rows_ref, wave_count, piece):
-    slots = wave_column.shape[0]
+def wave_grads(ids_ref, blocks_ref, rows_ref, wave_count, piece):
+    slots = ids_ref.shape[1]
     for s in range(slots):
         rows_ref[s * piece : (s + 1) * piece, :] = blocks_ref[s, :piece, :]
-    onehot = onehot_of(wave_column, wave_count)
+    onehot = onehot_of(ids_ref, wave_count)
     bits = 2**30 - 1
     shift = piece.bit_length() - 1
     tall = low_dot(
@@ -556,7 +579,7 @@
     def kernel(
         where_ref, ids_ref, blocks_ref, gen_ref, bias_ref, mix_out, kernels_out, biases_out, rows_ref
     ):
-        kernels, biases = wave_grads(ids_ref[...], blocks_ref, rows_ref, wave_count, piece)
+        kernels, biases = wave_grads(ids_ref, blocks_ref, rows_ref, wave_count, piece)
         kernels_out[...] = kernels
         biases_out[...] = biases
         products = contract_last(kernels, gen_ref[...])
@@ -573,14 +596,14 @@
     return local_call(
         kernel,
         where,
-        [],
-        [wave_ids, blocks, gen_rows, bias_gen],
+        [wave_ids],
+        [blocks, gen_rows, bias_gen],
         [
             jax.ShapeDtypeStruct((wave_count, width), f32),
             jax.ShapeDtypeStruct((wave_count * piece, half_width), bf16),
             jax.ShapeDtypeStruct((wave_count, half_width), f32),
         ],
-        scratch=[pltpu.VMEM((wave_ids.shape[0] * piece, half_width), bf16)],
+        scratch=[pltpu.VMEM((wave_ids.shape[1] * piece, half_width), bf16)],
         name="mix_grad",
         flops=2 * wave_count * piece * gen_rows.size,
     )
@@ -757,9 +780,10 @@
     def kernel(where_ref, *refs):
         left_refs = refs[: len(lefts)]
         right_refs = refs[len(lefts) : len(lefts) + len(rights)]
-        outs = refs[len(lefts) + len(rights) : len(lefts) + len(rights) + 2 * len(portions)]
-        turned_refs = refs[-len(uses) - len(lefts) : -len(uses)]
-        ordered = dict(zip(uses, refs[-len(uses) :]))
+        outs = refs[len(lefts) + len(rights) : len(lefts) + len(rights) + 6]
+        turned_refs = refs[len(lefts) + len(rights) + 6 : -len(uses) - 7]
+        ordered = dict(zip(uses, refs[-len(uses) - 7 : -7]))
+        made, sems = refs[-7:-1], refs[-1]
         band = where_ref[0]
         for left_ref, turned_ref in zip(left_refs, turned_refs):
             turned_ref[...] = left_ref[...].T
@@ -769,23 +793,27 @@
                 ordered_ref[p * rows : (p + 1) * rows, :] = turned_refs[i][
                     pl.ds(pl.multiple_of(block, 16), rows), :
                 ]
+        copies = []
         for side in (1, 0):
             for c, portion in enumerate(portions):
                 place = 0
+                slot = 3 - 3 * side + c
                 for i, j, start, width in portion:
                     left = ordered[i, c][side * half : (side + 1) * half, :]
                     for column in range(0, width, 256):
                         wide = min(256, width - column)
-                        outs[2 * c + side][:, place : place + wide] = jnp.dot(
+                        made[slot][:, place : place + wide] = jnp.dot(
                             left,
                             right_refs[j][:, start + column : start + column + wide],
                             preferred_element_type=f32,
                         ).astype(bf16)
                         place += wide
-
-    shapes = []
-    for width in widths:
-        shapes += [jax.ShapeDtypeStruct((half, width), bf16)] * 2
+                copies.append(pltpu.make_async_copy(made[slot], outs[slot], sems.at[slot]))
+                copies[-1].start()
+        for copy in copies:
+            copy.wait()
+
+    shapes = [jax.ShapeDtypeStruct((half, width), bf16) for width in widths] * 2
     turned = [pltpu.VMEM((left.shape[1], left.shape[0]), bf16) for left in lefts]
     ordered = [pltpu.VMEM((lefts[i].shape[1], lefts[i].shape[0]), bf16) for i, _ in uses]
     outs = local_call(
@@ -794,11 +822,422 @@
         [],
         [*lefts, *rights],
         shapes,
-        scratch=turned + ordered,
+        scratch=turned
+        + ordered
+        + [pltpu.VMEM(shape.shape, bf16) for shape in shapes]
+        + [pltpu.SemaphoreType.DMA((6,))],
+        spaces=[HBM] * 6,
         name=name,
         flops=2 * lefts[0].size * sum(widths),
-    )
-    return outs[0::2], outs[1::2]
+        mebibytes=32,
+    )
+    return outs[3:], outs[:3]
+
+
+def half_sum(where, keeps, arriving, last):
+    half = keeps[0].shape[0] // 2
+    widths = [keep.shape[1] for keep in keeps]
+
+    def kernel(where_ref, *refs):
+        keep_refs, arriving_refs = refs[:3], refs[3:6]
+        sends, kept = (refs[6:7], refs[7:8]) if last else (refs[6:9], refs[9:12])
+        place = 0
+        for c in range(3):
+            total = keep_refs[c][...].astype(f32) + arriving_refs[c][...].astype(f32)
+            at = slice(place, place + widths[c]) if last else slice(None)
+            out = 0 if last else c
+            kept[out][:, at] = total[:half]
+            sends[out][:, at] = total[half:].astype(bf16)
+            place += widths[c]
+
+    shapes = [(half, sum(widths))] if last else [(half, width) for width in widths]
+    outs = local_call(
+        kernel,
+        where,
+        [],
+        [*keeps, *arriving],
+        [jax.ShapeDtypeStruct(shape, bf16) for shape in shapes]
+        + [jax.ShapeDtypeStruct(shape, f32) for shape in shapes],
+        name="half_sum",
+    )
+    return outs[: len(shapes)], outs[len(shapes) :]
+
+
+def final_sum(where, kept, arriving, ff_local, half_width, patches):
+    rows = kept.shape[0]
+
+    def kernel(
+        where_ref, kept_ref, arriving_ref, up_out, down_out, in_out, out_out, pos_out, one_out,
+        two_out,
+    ):
+        total = kept_ref[...] + arriving_ref[...].astype(f32)
+        side = ff_local + EXTRA // 2
+        up_out[...] = total[:, :ff_local]
+        down_out[...] = total[:, side : side + ff_local]
+        for k in range(3):
+            in_out[k] = total[:, 2 * side + k * half_width : 2 * side + (k + 1) * half_width]
+        out_out[...] = total[:, 2 * side + 3 * half_width :]
+        extra = jnp.concatenate(
+            [total[:, ff_local:side], total[:, side + ff_local : 2 * side]], axis=1
+        )
+        pos_out[...] = extra[:, :patches]
+        extra = extra.T
+        one_out[...] = extra[patches : patches + 1]
+        two_out[...] = extra[patches + 1 : patches + 2]
+
+    def shape(*dims):
+        return jax.ShapeDtypeStruct(dims, f32)
+
+    return local_call(
+        kernel,
+        where,
+        [],
+        [kept, arriving],
+        [
+            shape(rows, ff_local),
+            shape(rows, ff_local),
+            shape(3, rows, half_width),
+            shape(rows, half_width),
+            shape(rows, patches),
+            shape(1, rows),
+            shape(1, rows),
+        ],
+        name="final_sum",
+    )
+
+
+STEPS = (1, 2, 4, 8)
+XY, YX, ZX, ZY = (8, 4, 2, 1), (8, 4, 1, 2), (8, 2, 1, 4), (8, 1, 2, 4)
+
+
+def product_scratch(lefts, uses):
+    return [pltpu.VMEM((left.shape[1], left.shape[0]), bf16) for left in lefts] + [
+        pltpu.VMEM((lefts[i].shape[1], lefts[i].shape[0]), bf16) for i, _ in uses
+    ]
+
+
+def order_rows(band, left_refs, turned_refs, ordered, positions):
+    rows = left_refs[0].shape[1] // 16
+    for left_ref, turned_ref in zip(left_refs, turned_refs):
+        turned_ref[...] = left_ref[...].T
+    for (i, order), ordered_ref in ordered.items():
+        for p in positions:
+            block = (band ^ relative_index(p, order)) * rows
+            ordered_ref[p * rows : (p + 1) * rows, :] = turned_refs[i][
+                pl.ds(pl.multiple_of(block, 16), rows), :
+            ]
+
+
+def product_tiles(left, right_refs, portion, ordered, order, rows):
+    place = 0
+    for i, j, start, width in portion:
+        for column in range(0, width, 256):
+            wide = min(256, width - column)
+            yield (
+                place,
+                wide,
+                jnp.dot(
+                    ordered[i, order][rows, :],
+                    right_refs[j][:, start + column : start + column + wide],
+                    preferred_element_type=f32,
+                ).astype(bf16),
+            )
+            place += wide
+
+
+def early_products(where, lefts, rights, portions, orders):
+    uses = sorted({(piece[0], order) for portion, order in zip(portions, orders) for piece in portion})
+    half = lefts[0].shape[1] // 2
+    widths = [sum(piece[3] for piece in portion) for portion in portions]
+    n = len(lefts) + len(rights)
+
+    def kernel(where_ref, *refs):
+        left_refs, right_refs = refs[: len(lefts)], refs[len(lefts) : n]
+        outs, scratch = refs[n : n + len(portions)], refs[n + len(portions) :]
+        ordered = dict(zip(uses, scratch[len(lefts) :]))
+        order_rows(where_ref[0], left_refs, scratch[: len(lefts)], ordered, range(8, 16))
+        for out, portion, order in zip(outs, portions, orders):
+            tiles = product_tiles(
+                None, right_refs, portion, ordered, order, slice(half, 2 * half)
+            )
+            for place, wide, product in tiles:
+                out[:, place : place + wide] = product
+
+    return local_call(
+        kernel,
+        where,
+        [],
+        [*lefts, *rights],
+        [jax.ShapeDtypeStruct((half, width), bf16) for width in widths],
+        scratch=product_scratch(lefts, uses),
+        name="early_products",
+        flops=lefts[0].size * sum(widths),
+    )
+
+
+def round_products(where, lefts, rights, early, early_orders, portions, orders):
+    early_of = {0: 1, 1: 0}
+    groups = [(0,), (1,), (2, 3)]
+    uses = sorted(
+        {
+            (piece[0], order)
+            for portion, order in zip([*early, *portions], [*early_orders, *orders])
+            for piece in portion
+        }
+    )
+    quarter = lefts[0].shape[1] // 4
+    early_width = sum(piece[3] for piece in early[0])
+    widths = [sum(piece[3] for piece in portion) for portion in portions]
+    shapes = []
+    for g, group in enumerate(groups):
+        width = 2 * sum(widths[c] for c in group) + (early_width if g in early_of else 0)
+        shapes.append(jax.ShapeDtypeStruct((quarter, width), bf16))
+    n = len(lefts) + len(rights)
+
+    def kernel(where_ref, *refs):
+        left_refs, right_refs = refs[: len(lefts)], refs[len(lefts) : n]
+        outs, made, sems = refs[n : n + 6], refs[-7:-1], refs[-1]
+        scratch = refs[n + 6 : -7]
+        ordered = dict(zip(uses, scratch[len(lefts) :]))
+        order_rows(where_ref[0], left_refs, scratch[: len(lefts)], ordered, range(16))
+        copies = []
+        for side in (1, 0):
+            for g, group in enumerate(groups):
+                slot = 3 * (1 - side) + g
+                base = 0
+                if g in early_of:
+                    e = early_of[g]
+                    rows = slice(side * quarter, (side + 1) * quarter)
+                    tiles = product_tiles(
+                        None, right_refs, early[e], ordered, early_orders[e], rows
+                    )
+                    for place, wide, product in tiles:
+                        made[slot][:, place : place + wide] = product
+                    base = early_width
+                for c in group:
+                    rows = slice(side * 2 * quarter, (side + 1) * 2 * quarter)
+                    tiles = product_tiles(None, right_refs, portions[c], ordered, orders[c], rows)
+                    for place, wide, product in tiles:
+                        for k in range(2):
+                            at = base + k * widths[c] + place
+                            made[slot][:, at : at + wide] = product[k * quarter : (k + 1) * quarter]
+                    base += 2 * widths[c]
+                copies.append(pltpu.make_async_copy(made[slot], outs[slot], sems.at[slot]))
+                copies[-1].start()
+        for copy in copies:
+            copy.wait()
+
+    outs = local_call(
+        kernel,
+        where,
+        [],
+        [*lefts, *rights],
+        shapes * 2,
+        scratch=product_scratch(lefts, uses)
+        + [pltpu.VMEM(shape.shape, bf16) for shape in shapes * 2]
+        + [pltpu.SemaphoreType.DMA((6,))],
+        spaces=[HBM] * 6,
+        name="round_products",
+        flops=2 * lefts[0].size * sum(widths) + lefts[0].size * early_width,
+        mebibytes=32,
+    )
+    return outs[:3], outs[3:]
+
+
+def early_sum(where, sends, keeps, arriving):
+    quarter = sends[0].shape[0]
+    width = arriving[0].shape[1]
+    buffers = [sends[0], keeps[0], sends[1], keeps[1]]
+
+    def kernel(where_ref, *refs):
+        arriving_refs, outs, parts, sems = refs[4:6], refs[6:10], refs[10], refs[11]
+        loads = []
+        for k in range(4):
+            loads.append(
+                pltpu.make_async_copy(refs[k].at[:, pl.ds(0, width)], parts.at[k], sems.at[k])
+            )
+            loads[-1].start()
+        stores = []
+        for k in range(4):
+            loads[k].wait()
+            rows = slice(quarter, 2 * quarter) if k % 2 == 0 else slice(0, quarter)
+            added = arriving_refs[1 - k // 2][rows, :].astype(f32)
+            parts[k] = (parts[k].astype(f32) + added).astype(bf16)
+            stores.append(
+                pltpu.make_async_copy(parts.at[k], outs[k].at[:, pl.ds(0, width)], sems.at[4 + k])
+            )
+            stores[-1].start()
+        for store in stores:
+            store.wait()
+
+    smem = pl.BlockSpec(memory_space=pltpu.SMEM)
+    outs = pl.pallas_call(
+        kernel,
+        in_specs=[smem]
+        + [pl.BlockSpec(memory_space=HBM)] * 4
+        + [pl.BlockSpec(memory_space=pltpu.VMEM)] * 2,
+        out_specs=[pl.BlockSpec(memory_space=HBM)] * 4,
+        out_shape=[jax.ShapeDtypeStruct(b.shape, bf16) for b in buffers],
+        input_output_aliases={1: 0, 2: 1, 3: 2, 4: 3},
+        scratch_shapes=[
+            pltpu.VMEM((4, quarter, width), bf16),
+            pltpu.SemaphoreType.DMA((8,)),
+        ],
+        compiler_params=pltpu.CompilerParams(vmem_limit_bytes=24 * 2**20),
+        name="early_sum",
+    )(where, *buffers, *arriving)
+    return [outs[0], outs[2], sends[2]], [outs[1], outs[3], keeps[2]]
+
+
+def second_sum(where, keeps, arriving, early_width, widths):
+    quarter = keeps[0].shape[0]
+    pair = quarter // 2
+    wa, wb, wc, wd = widths
+
+    def kernel(where_ref, *refs):
+        keep_refs, arriving_refs = refs[:3], refs[3:6]
+        send_y, send_x, send_z, keep_y, keep_x, keep_z = refs[6:]
+        totals = [k[...].astype(f32) + a[...].astype(f32) for k, a in zip(keep_refs, arriving_refs)]
+        for e, g in ((0, 1), (1, 0)):
+            at = slice(e * early_width, (e + 1) * early_width)
+            keep_z[:, at] = totals[g][:pair, :early_width]
+            send_z[:, at] = totals[g][pair:, :early_width].astype(bf16)
+        for total, start, width, keep, send, place in (
+            (totals[0], early_width, wa, keep_y, send_y, 0),
+            (totals[2], 2 * wc, wd, keep_y, send_y, 2 * wa),
+            (totals[1], early_width, wb, keep_x, send_x, 0),
+            (totals[2], 0, wc, keep_x, send_x, 2 * wb),
+        ):
+            for k in range(2):
+                rows = slice(k * pair, (k + 1) * pair)
+                at = slice(place + k * width, place + (k + 1) * width)
+                keep[:, at] = total[rows, start : start + width]
+                send[:, at] = total[rows, start + width : start + 2 * width].astype(bf16)
+
+    shapes = [(pair, 2 * (wa + wd)), (pair, 2 * (wb + wc)), (pair, 2 * early_width)]
+    outs = local_call(
+        kernel,
+        where,
+        [],
+        [*keeps, *arriving],
+        [jax.ShapeDtypeStruct(shape, bf16) for shape in shapes]
+        + [jax.ShapeDtypeStruct(shape, f32) for shape in shapes],
+        name="second_sum",
+    )
+    return outs[:3], outs[3:]
+
+
+def third_sum(where, keeps, arriving, early_width, widths):
+    pair = keeps[0].shape[0]
+    rows = pair // 2
+    wa, wb, wc, wd = widths
+
+    def kernel(where_ref, *refs):
+        keep_refs, arriving_refs = refs[:3], refs[3:6]
+        send_e, send_ab, send_c, send_d, keep_e, keep_ab, keep_c, keep_d = refs[6:]
+        y, x, z = (k[...] + a[...].astype(f32) for k, a in zip(keep_refs, arriving_refs))
+        keep_e[...] = z[:rows]
+        send_e[...] = z[rows:].astype(bf16)
+        for total, start, width, keep, send, place in (
+            (y, 0, wa, keep_ab, send_ab, 0),
+            (x, 0, wb, keep_ab, send_ab, wa),
+            (x, 2 * wb, wc, keep_c, send_c, 0),
+            (y, 2 * wa, wd, keep_d, send_d, 0),
+        ):
+            keep[:, place : place + width] = total[:, start : start + width]
+            send[:, place : place + width] = total[:, start + width : start + 2 * width].astype(bf16)
+
+    shapes = [(rows, 2 * early_width), (pair, wa + wb), (pair, wc), (pair, wd)]
+    outs = local_call(
+        kernel,
+        where,
+        [],
+        [*keeps, *arriving],
+        [jax.ShapeDtypeStruct(shape, bf16) for shape in shapes]
+        + [jax.ShapeDtypeStruct(shape, f32) for shape in shapes],
+        name="third_sum",
+    )
+    return outs[:4], outs[4:]
+
+
+def fourth_sum(where, keeps, arriving):
+    rows = keeps[0].shape[0] // 2
+    widths = [keep.shape[1] for keep in keeps]
+
+    def kernel(where_ref, *refs):
+        send, kept = refs[6:]
+        place = 0
+        for keep, arrived, width in zip(refs[:3], refs[3:6], widths):
+            total = keep[...] + arrived[...].astype(f32)
+            kept[:, place : place + width] = total[:rows]
+            send[:, place : place + width] = total[rows:].astype(bf16)
+            place += width
+
+    return local_call(
+        kernel,
+        where,
+        [],
+        [*keeps, *arriving],
+        [
+            jax.ShapeDtypeStruct((rows, sum(widths)), bf16),
+            jax.ShapeDtypeStruct((rows, sum(widths)), f32),
+        ],
+        name="fourth_sum",
+    )
+
+
+def last_sum(where, early, early_arriving, kept, arriving, ff_local, half_width, patches):
+    rows = kept.shape[0]
+    early_width = early.shape[1] // 2
+    rest = ff_local - early_width
+
+    def kernel(
+        where_ref, early_ref, early_arriving_ref, kept_ref, arriving_ref, up_out, down_out, in_out,
+        out_out, pos_out, one_out, two_out,
+    ):
+        first = early_ref[...] + early_arriving_ref[...].astype(f32)
+        total = kept_ref[...] + arriving_ref[...].astype(f32)
+        up_out[:, :early_width] = first[:, :early_width]
+        down_out[:, :early_width] = first[:, early_width:]
+        up_out[:, early_width:] = total[:, :rest]
+        b = rest + 256
+        down_out[:, early_width:] = total[:, b : b + rest]
+        in_out[0, :, :256] = total[:, rest:b]
+        at = b + rest
+        in_out[0, :, 256:] = total[:, at : at + half_width - 256]
+        at += half_width - 256
+        in_out[1] = total[:, at : at + half_width]
+        in_out[2] = total[:, at + half_width : at + 2 * half_width]
+        at += 2 * half_width
+        out_out[...] = total[:, at : at + half_width]
+        extra = total[:, at + half_width :].T
+        pos_out[...] = total[:, at + half_width : at + half_width + patches]
+        one_out[...] = extra[patches : patches + 1]
+        two_out[...] = extra[patches + 1 : patches + 2]
+
+    def shape(*dims):
+        return jax.ShapeDtypeStruct(dims, f32)
+
+    return local_call(
+        kernel,
+        where,
+        [],
+        [early, early_arriving, kept, arriving],
+        [
+            shape(rows, ff_local),
+            shape(rows, ff_local),
+            shape(3, rows, half_width),
+            shape(rows, half_width),
+            shape(rows, patches),
+            shape(1, rows),
+            shape(1, rows),
+        ],
+        name="last_sum",
+    )
+
+
+def after(values, *others):
+    return lax.optimization_barrier((values, others))[0]
 
 
 def shards(
@@ -834,6 +1273,7 @@
     orders = gather_orders(count)
     where = jnp.stack([band_index, head_index]).astype(jnp.int32)
     pixels = pixels.reshape(images, patches, pixel_count)
+    wave_ids = wave_ids.reshape(1, -1)
 
     gen_rows = kernel_gen.reshape(-1, half_width)
     hyper_weights = [hyper_in, hyper_out, hyper_up, hyper_down]
@@ -871,22 +1311,15 @@
     ff_other = swap(ff_parts)
 
     ff_local = up_proj.shape[1]
-    third = ff_local * 2 // 3
-    ff_keeps, ff_sends = row_products(
-        orders,
-        count,
-        where,
-        [second_low, grad_low],
-        [grad_hidden, active_low],
-        [
-            [(0, 0, 0, third)],
-            [(0, 0, third, ff_local - third), (1, 1, 0, 2 * third - ff_local)],
-            [(1, 1, 2 * third - ff_local, third)],
-        ],
-        "ff_grads",
-    )
-    ff_sends, ff_other = lax.optimization_barrier((ff_sends, ff_other))
-    ff_arriving = [hop(send, order[-1]) for send, order in zip(ff_sends, orders)]
+    staged = count == 16
+    if staged:
+        early_width = EARLY
+        ff_early = [[(0, 0, 0, early_width)], [(1, 1, 0, early_width)]]
+        early_sends = early_products(
+            where, [second_low, grad_low], [grad_hidden, active_low], ff_early, [XY, YX]
+        )
+        early_sends, ff_other = lax.optimization_barrier((early_sends, ff_other))
+        early_arriving = [hop(send, step) for send, step in zip(early_sends, STEPS)]
 
     layer_out, gain_two_grad, grad_mid, grad_mid_low, *grad_projected, normed_part = (
         attention_backward(
@@ -909,6 +1342,30 @@
     )
 
     first = hop(grad_embed_half, orders[0][0])
+    lefts = [second_low, grad_low, normed_low, grad_mid_low, small]
+    rights = [grad_hidden, active_low, *grad_projected, attended, jnp.eye(EXTRA, dtype=bf16)]
+    side = EXTRA // 2
+    if staged:
+        portions = [
+            [(0, 0, early_width, ff_local - early_width), (2, 2, 0, 256)],
+            [(1, 1, early_width, ff_local - early_width)]
+            + [(2, 2, 256, half_width - 256), (2, 3, 0, half_width - 256)],
+            [(2, 3, half_width - 256, 256), (2, 4, 0, half_width)],
+            [(3, 5, 0, half_width), (4, 6, 0, EXTRA)],
+        ]
+        widths = [sum(piece[3] for piece in portion) for portion in portions]
+        sends, keeps = round_products(
+            where, lefts, rights, ff_early, [XY, YX], portions, [XY, YX, ZX, ZY]
+        )
+        first = after(first, (sends, early_arriving))
+    else:
+        portions = [
+            [(0, 0, 0, ff_local), (4, 6, 0, side)],
+            [(1, 1, 0, ff_local), (4, 6, side, side)],
+            [(2, 2 + k, 0, half_width) for k in range(3)] + [(3, 5, 0, half_width)],
+        ]
+        keeps, sends = row_products(orders, count, where, lefts, rights, portions, "weight_grads")
+        first = after(first, sends)
     early, late = [], []
     for c, order in enumerate(orders):
         block = jnp.stack([grad_embed_half[:, span(c)], first[:, span(c)]])
@@ -917,65 +1374,73 @@
         early.append(block)
         late.append(hop(block, order[-1]))
     total, bias = kernel_grad(0, orders, where, band_mask, pixels, early, None, None)
+    if staged:
+        sends, keeps = early_sum(where, sends, keeps, after(early_arriving, early))
+    sends, late, total = lax.optimization_barrier((sends, late, total))
+    if staged:
+        arriving = [hop(send, step) for send, step in zip(sends, STEPS)]
+    else:
+        arriving = [hop(send, order[-1]) for send, order in zip(sends, orders)]
     blocks = kernel_grad(1, orders, where, band_mask, pixels, late, total, bias)
+    spread_blocks = lax.all_to_all(blocks, "band", 0, 0, tiled=True)
+    early, late = after((early, late), blocks)
     own_pixels, other_pixels = pixel_grad(orders, where, band_mask, early, late, kernels)
     grad_pixels = (own_pixels.astype(f32) + swap(other_pixels).astype(f32)).astype(bf16)
     grad_pixels = grad_pixels[:, None]
-
-    blocks = lax.all_to_all(blocks, "band", 0, 0, tiled=True)
-    grad_mix, wave_kernels, wave_biases = mix_grad(
-        where, wave_ids, blocks, gen_rows, bias_gen, wave_count, count
-    )
-    grad_kernel_gen, grad_bias_gen = generator_grads(where, mix_low, wave_kernels, wave_biases)
-    grad_mix = grad_mix + swap(grad_mix)
-    step = 1
-    while step < count:
-        if step * 4 <= count:
-            grad_mix = (grad_mix + hop(grad_mix, step)) + (
-                hop(grad_mix, 2 * step) + hop(grad_mix, 3 * step)
+    steps = len(orders[0])
+    mixing = count // 2
+    arriving = after(arriving, (spread_blocks, own_pixels))
+    for t in range(steps - 1):
+        last = t == steps - 2
+        if not staged:
+            sends, keeps = half_sum(where, keeps, arriving, last)
+            if last:
+                arriving = hop(sends[0], orders[0][0])
+            else:
+                arriving = [hop(send, order[-2 - t]) for send, order in zip(sends, orders)]
+        elif t == 0:
+            sends, keeps = second_sum(where, keeps, arriving, early_width, widths)
+            arriving = [hop(send, step) for send, step in zip(sends, (2, 1, 4))]
+        elif t == 1:
+            sends, keeps = third_sum(where, keeps, arriving, early_width, widths)
+            early_last, *arriving = [hop(send, step) for send, step in zip(sends, (8, 4, 2, 1))]
+            early_kept, *keeps = keeps
+        else:
+            sends, keeps = fourth_sum(where, keeps, arriving)
+            arriving = hop(sends, 8)
+        if t == 0:
+            grad_mix, wave_kernels, wave_biases = mix_grad(
+                where, wave_ids, after(spread_blocks, sends), gen_rows, bias_gen, wave_count, count
             )
-            step *= 4
+            grad_mix = grad_mix + swap(grad_mix)
         else:
-            grad_mix = grad_mix + hop(grad_mix, step)
-            step *= 2
+            grad_mix = after(grad_mix, sends)
+        while mixing and (t >= 2 or mixing > count // 8):
+            grad_mix = grad_mix + hop(grad_mix, mixing)
+            mixing //= 2
+        if not last:
+            arriving = after(arriving, grad_mix)
     hyper_grads = hyper_backward(
         where, grad_mix, wave_table, hyper_weights, hyper_gains, hyper_kept
     )
-
-    at_keeps, at_sends = row_products(
-        orders,
-        count,
-        where,
-        [normed_low, grad_mid_low, small],
-        [*grad_projected, attended, jnp.eye(EXTRA, dtype=bf16)],
-        [
-            [(0, 0, 0, half_width), (0, 1, 0, 256)],
-            [(0, 1, 256, half_width - 256), (0, 2, 0, half_width), (1, 3, 0, 128)],
-            [(1, 3, 128, half_width - 128), (2, 4, 0, EXTRA)],
-        ],
-        "attention_grads",
-    )
-    ff_keeps, ff_arriving, at_sends, _ = lax.optimization_barrier(
-        (ff_keeps, ff_arriving, at_sends, late)
-    )
-    ff_sums = jnp.concatenate(scatter_sum(ff_keeps, None, orders, ff_arriving), axis=1)
-    at_sums = jnp.concatenate(scatter_sum(at_keeps, at_sends, orders), axis=1)
-    grad_up, grad_down = ff_sums[:, :ff_local], ff_sums[:, ff_local:]
-    grad_in_proj = jnp.stack(
-        [at_sums[:, i * half_width : (i + 1) * half_width] for i in range(3)]
-    )
-    grad_out_proj = at_sums[:, 3 * half_width : 4 * half_width].T
-    tail = at_sums[:, 4 * half_width :].T
+    grad_kernel_gen, grad_bias_gen = generator_grads(where, mix_low, wave_kernels, wave_biases)
+    if staged:
+        sums = last_sum(
+            where, early_kept, early_last, keeps, arriving, ff_local, half_width, patches
+        )
+    else:
+        sums = final_sum(where, keeps[0], arriving, ff_local, half_width, patches)
+    grad_up, grad_down, grad_in_proj, grad_out_proj, grad_pos, *grad_gains = sums
     return (
         layer_out[None],
         grad_pixels,
-        tail[:patches],
+        grad_pos.T,
         grad_in_proj,
-        grad_out_proj,
+        grad_out_proj.T,
         grad_up,
         grad_down.T,
-        tail[patches],
-        tail[patches + 1],
+        grad_gains[0][0],
+        grad_gains[1][0],
         grad_kernel_gen.reshape(kernel_gen.shape),
         grad_bias_gen,
         *hyper_grads[:5],

time: 251 us -> 197 us (0.78)
  waiting for transfers between devices: 84.7 us -> 61.1 us
  Pallas kernels: 70.7 us -> 52.6 us
  other arithmetic: 14.4 us -> 3.53 us
    ppermute x46 -> x37, waiting for transfers between devices: 74.7 us -> 44.1 us  [hop(): return lax.ppermute(values, 'band', [(i, i ^ step) for i in range(count)])]
    pallas_call x15 -> x19, Pallas kernels: 70.7 us -> 49.8 us  [local_call(): pl.pallas_call(kernel, in_specs=[smem] * (1 + len(tables)) + [vmem] * len...]
    convert_element_type x27 -> x9, other arithmetic: 9.44 us -> 0.48 us  [scatter_sum(): sends.append((k[half:].astype(f32) + a[half:].astype(f32)).astype(bf16))]
    unnamed x63 -> x112, local copies, waits for them, and re-layouts: 8.63 us -> 16.3 us
    ppermute x46 -> x37, starting transfers between devices: 47.8 us -> 44.9 us  [hop(): return lax.ppermute(values, 'band', [(i, i ^ step) for i in range(count)])]
    all_to_all x1, waiting for transfers between devices: 0.01 us -> 2.87 us  [shards(): spread_blocks = lax.all_to_all(blocks, 'band', 0, 0, tiled=True)]
    pallas_call x0 -> x1, Pallas kernels: none -> 2.77 us  [early_sum(): pl.pallas_call(kernel, in_specs=[smem] + [pl.BlockSpec(memory_space=HBM)]...]
    ppermute x6, waiting for transfers between devices: 3.29 us -> 6.02 us  [swap(): return lax.ppermute(values, 'head', [(0, 1), (1, 0)])]
  transfers between devices with their start and end apart: 54 -> 45, of which waited for: 29 -> 31; matrix products, arithmetic and copies ran while one was open for 7% -> 1% of each run, Pallas kernels for 16% -> 18%
where the time goes in v3:
time: 197 us
  starting transfers between devices  61.5 us (31%)
  waiting for transfers between devices  61.1 us (31%)
  Pallas kernels  52.6 us (27%)
  local copies, waits for them, and re-layouts  16.6 us (8%)
  other arithmetic  3.53 us (2%)
    pallas_call x19, Pallas kernels, local_call(): pl.pallas_call(kernel, in_specs=[smem] * (1 + len(tables)) + [vmem] * len...  49.8 us
    ppermute x37, starting transfers between devices, hop(): return lax.ppermute(values, 'band', [(i, i ^ step) for i in range(count)])  44.9 us
    ppermute x37, waiting for transfers between devices, hop(): return lax.ppermute(values, 'band', [(i, i ^ step) for i in range(count)])  44.1 us
    unnamed x112, local copies, waits for them, and re-layouts  16.3 us
    all_to_all x1, starting transfers between devices, shards(): lax.all_to_all(slot_piece, 'band', 0, 0, tiled=True)  8.33 us
    all_to_all x1, waiting for transfers between devices, shards(): lax.all_to_all(slot_piece, 'band', 0, 0, tiled=True)  8.03 us
    all_to_all x1, starting transfers between devices, shards(): spread_blocks = lax.all_to_all(blocks, 'band', 0, 0, tiled=True)  7.53 us
    ppermute x6, waiting for transfers between devices, swap(): return lax.ppermute(values, 'head', [(0, 1), (1, 0)])  6.02 us
  transfers between devices with their start and end apart: 45, of which 31 were waited for; matrix products, arithmetic and copies ran while one was open for 1% of the time, Pallas kernels for 18%

profile of v3, /device:TPU:0, one launch (start us, length us, event | category | flops | bytes accessed | tf_op | source)
XLA Modules:
  0.0 196.7 jit_solution(5383551912967521044)
XLA Ops:
  1.2 6.3 %hyper_forward.1 = (bf16[256,384]{1,0:T(8,128)(2,1)}, f32[1,384]{1,0:T(1,128)}, bf16[16,128]{1,0:T(8,128)(2,1)}, f32[16,384]{1,0:T(8,128)}, f32[4,16,16]{2,1,0:T...) custom-call(s32[2]{0:T(128)} %pad_add_fusion.where_ref, ...), custom_call_target="tpu_custom_call" | custom-call | flops 1610612736 | bytes 4427392 | tf_op jit(solution)/shard_map/hyper_forward/pallas_call | solution.py:195
  7.5 8.3 %all-to-all-start = ((bf16[16,16,384]{2,1,0:T(8,128)(2,1)}), bf16[16,16,384]{2,1,0:T(8,128)(2,1)S(1)}, u32[]{:S(2)}, u32[]{:S(2)}) async-start(bf16[16,16,384]{2,1,0:T(8,128)(2,1)} %bitcast.60), calls=%async_computation | async-start | bytes 393216 | tf_op jit(solution)/shard_map/all_to_all | solution.py:1293
  16.5 8.0 %all-to-all-done = bf16[16,16,384]{2,1,0:T(8,128)(2,1)S(1)} async-done(((bf16[16,16,384]{2,1,0:T(8,128)(2,1)}), bf16[16,16,384]{2,1,0:T(8,128)(2,1)S(1)}, u32[]{:S(2)}, u32[]{:S(2)}) %all-to-all-start) | async-done | bytes 196640 | tf_op jit(solution)/shard_map/all_to_all | solution.py:1293
  29.8 5.6 %collective-permute-done.6 = bf16[8,196,128]{2,1,0:T(8,128)(2,1)S(1)} collective-permute-done((bf16[8,196,128]{2,1,0:T(8,128)(2,1)S(1)}, bf16[8,196,128]{2,1,0:T(8,128)(2,1)S(1)}, u32[]{:S(2)}, u32[]{:S(2)}) %collective-permute-start.6) | collective-permute-done | bytes 401440 | tf_op jit(solution)/shard_map/ppermute | solution.py:111
  50.6 2.8 %collective-permute-start.9 = (bf16[1,196,384]{2,1,0:T(8,128)(2,1)}, bf16[1,196,384]{2,1,0:T(8,128)(2,1)}, u32[]{:S(2)}, u32[]{:S(2)}) collective-permute-start(bf16[1,196,384]{2,1,0:T(8,128)(2,1)} %pad_maximum_fusion.6), channel_id=1, source_target_pairs={{0,16},{2,18},{4,20},{6,22},{8,24},{10,26},{12,28},{14,30},{16,0},... | collective-permute-start | bytes 451592 | tf_op jit(solution)/shard_map/ppermute | solution.py:111
  53.4 5.2 %collective-permute-done.9 = bf16[1,196,384]{2,1,0:T(8,128)(2,1)} collective-permute-done((bf16[1,196,384]{2,1,0:T(8,128)(2,1)}, bf16[1,196,384]{2,1,0:T(8,128)(2,1)}, u32[]{:S(2)}, u32[]{:S(2)}) %collective-permute-start.9) | collective-permute-done | bytes 150560 | tf_op jit(solution)/shard_map/ppermute | solution.py:111
  62.3 2.5 %attention_forward.1 = (f32[196,768]{1,0:T(8,128)S(1)}, bf16[196,768]{1,0:T(8,128)(2,1)S(1)}, bf16[196,384]{1,0:T(8,128)(2,1)S(1)}, bf16[196,384]{1,0:T(8,128)(2...) custom-call(s32[2]{0:T(128)S(1)} %copy-done.29, ...), custom_call_target="tpu_custom_call" | custom-call | flops 580435968 | bytes 5691264 | tf_op jit(solution)/shard_map/attention_forward/pallas_call | solution.py:195
  68.2 3.4 %feed_forward.1 = (f32[196,768]{1,0:T(8,128)S(1)}, bf16[196,768]{1,0:T(8,128)(2,1)S(1)}, bf16[196,1536]{1,0:T(8,128)(2,1)S(1)}, bf16[196,1536]{1,0:T(8,128)(2,1)S(1)}, bf16[404,768]{1,0:T(8,128)(2,1)S(1)}) custom-call(s32[2]{0:T(128)S(1)} %copy-done.29, f32[196,768]{1,0:T(8,128)S(1)} %get-tuple-element.148.tokens_ref, ...), custom_call_target="tpu_custom_call" | custom-call | flops 1849688064 | bytes 8953344 | tf_op jit(solution)/shard_map/feed_forward/pallas_call | solution.py:195
  75.7 4.2 %attention_backward.1 = (bf16[196,768]{1,0:T(8,128)(2,1)}, f32[1,768]{1,0:T(1,128)S(1)}, f32[196,768]{1,0:T(8,128)S(1)}, bf16[196,768]{1,0:T(8,128)(2,1)S(1)}, b...) custom-call(s32[2]{0:T(128)S(1)} %copy-done.29, ...), custom_call_target="tpu_custom_call" | custom-call | flops 698449920 | bytes 7838592 | tf_op jit(solution)/shard_map/attention_backward/pallas_call | solution.py:195
  84.0 4.4 %round_products.1 = (bf16[192,2560]{1,0:T(8,128)(2,1)}, bf16[192,2560]{1,0:T(8,128)(2,1)}, bf16[192,2560]{1,0:T(8,128)(2,1)}, bf16[192,2560]{1,0:T(8,128)(2,1)S(...) custom-call(s32[2]{0:T(128)S(1)} %copy-done.29, bf16[196,768]{1,0:T(8,128)(2,1)S(1)} %get-tuple-element.152.refs_0_, ...), custom_call_target="tpu_custom_call" | custom-call | flops 1001914368 | bytes 9433088 | tf_op jit(solution)/shard_map/round_products/pallas_call | solution.py:195
  88.4 4.5 %collective-permute-done.14 = bf16[196,384]{1,0:T(8,128)(2,1)S(1)} collective-permute-done((bf16[196,384]{1,0:T(8,128)(2,1)S(1)}, bf16[196,384]{1,0:T(8,128)(2,1)S(1)}, u32[]{:S(2)}, u32[]{:S(2)}) %collective-permute-start.14) | collective-permute-done | bytes 150560 | tf_op jit(solution)/shard_map/ppermute | solution.py:111
  107.0 2.5 %collective-permute-done.20 = bf16[4,196,128]{2,1,0:T(8,128)(2,1)S(1)} collective-permute-done((bf16[4,196,128]{2,1,0:T(8,128)(2,1)S(1)}, bf16[4,196,128]{2,1,0:T(8,128)(2,1)S(1)}, u32[]{:S(2)}, u32[]{:S(2)}) %collective-permute-start.20) | collective-permute-done | bytes 200736 | tf_op jit(solution)/shard_map/ppermute | solution.py:111
  111.2 2.8 %early_sum.1 = (bf16[192,2560]{1,0:T(8,128)(2,1)}, bf16[192,2560]{1,0:T(8,128)(2,1)S(1)}, bf16[192,2560]{1,0:T(8,128)(2,1)}, bf16[192,2560]{1,0:T(8,128)(2,1)S(1)}) custom-call(s32[2]{0:T(128)S(1)} %copy-done.29, bf16[192,2560]{1,0:T(8,128)(2,1)} %get-tuple-element.174.refs_0_, ...), custom_call_target="tpu_custom_call", output_to_operand_aliasing={{0}: (1, {}), {1}: (2, {}), {2}: (3, {}), {3}: (4, {})} | custom-call | tf_op jit(solution)/shard_map/early_sum/pallas_call | solution.py:1074
  115.0 2.4 %kernel_grad.1 = (f32[384,256]{1,0:T(8,128)S(1)}, f32[1,384]{1,0:T(1,128)S(1)}) custom-call(s32[2]{0:T(128)S(1)} %copy-done.29, s32[16,16]{1,0:T(8,128)S(1)} %copy-done.26, bf16[16,196,256]{2,1,0:T(8,128)(2,1)S(1)} %bitcast.43, bf16[8,196,128]{2,1,0:T(8,128)(2,1)S(1)} %pad_maximum_fusion.refs_0_, bf16[8,196,128]{2,1,0:T(8,128)(2,1)S(1)} %pad_maximum_fusion.1.refs_1_, ...), custom_call_target="tpu_custom_call" | custom-call | flops 308281344 | bytes 3204608 | tf_op jit(solution)/shard_map/kernel_grad/pallas_call | solution.py:195
  120.2 2.7 %collective-permute-start.28 = (bf16[192,2560]{1,0:T(8,128)(2,1)}, bf16[192,2560]{1,0:T(8,128)(2,1)}, u32[]{:S(2)}, u32[]{:S(2)}) collective-permute-start(bf16[192,2560]{1,0:T(8,128)(2,1)} %get-tuple-element.204), channel_id=1, source_target_pairs={{0,4},{2,6},{4,0},{6,2},{8,12},{10,14},{12,8},{14,10},{16,20},{18,... | collective-permute-start | bytes 2949128 | tf_op jit(solution)/shard_map/ppermute | solution.py:111
  128.5 7.5 %all-to-all-start.1 = ((bf16[16,18,384]{2,1,0:T(8,128)(2,1)}), bf16[16,18,384]{2,1,0:T(8,128)(2,1)}, u32[]{:S(2)}, u32[]{:S(2)}) async-start(bf16[16,18,384]{2,1,0:T(8,128)(2,1)} %copy-done.16), calls=%async_computation.1 | async-start | bytes 589824 | tf_op jit(solution)/shard_map/all_to_all | solution.py:1385
  145.0 2.9 %all-to-all-done.1.blocks_ref = bf16[16,18,384]{2,1,0:T(8,128)(2,1)} async-done(((bf16[16,18,384]{2,1,0:T(8,128)(2,1)}), bf16[16,18,384]{2,1,0:T(8,128)(2,1)}, u32[]{:S(2)}, u32[]{:S(2)}) %all-to-all-start.1) | async-done | bytes 221216 | tf_op jit(solution)/shard_map/all_to_all | solution.py:1385
  149.1 2.5 %second_sum.1 = (bf16[96,2816]{1,0:T(8,128)(2,1)S(1)}, bf16[96,2816]{1,0:T(8,128)(2,1)S(1)}, bf16[96,2048]{1,0:T(8,128)(2,1)S(1)}, f32[96,2816]{1,0:T(8,128)S(1)...) custom-call(s32[2]{0:T(128)S(1)} %copy-done.29, bf16[192,2560]{1,0:T(8,128)(2,1)S(1)} %get-tuple-element.200.refs_0_, ...), custom_call_target="tpu_custom_call" | custom-call | bytes 10321920 | tf_op jit(solution)/shard_map/second_sum/pallas_call | solution.py:195
  153.9 3.1 %mix_grad.1 = (f32[16,128]{1,0:T(8,128)S(1)}, bf16[256,384]{1,0:T(8,128)(2,1)S(1)}, f32[16,384]{1,0:T(8,128)S(1)}) custom-call(s32[2]{0:T(128)S(1)} %copy-done.29, s32[1,16]{1,0:T(1,128)S(1)} %bitcast.55, bf16[16,18,384]{2,1,0:T(8,128)(2,1)} %all-to-all-done.1.blocks_ref, bf16[2048,384]{1,0:T(8,128)(2,1)S(1)} %bitcast.49, bf16[128,384]{1,0:T(8,128)(2,1)S(1)} %copy-done.30), custom_call_target="tpu_custom_call" | custom-call | flops 402653184 | bytes 2121728 | tf_op jit(solution)/shard_map/mix_grad/pallas_call | solution.py:195
  160.5 2.6 %collective-permute-done.34 = f32[16,128]{1,0:T(8,128)S(1)} collective-permute-done((f32[16,128]{1,0:T(8,128)S(1)}, f32[16,128]{1,0:T(8,128)S(1)}, u32[]{:S(2)}, u32[]{:S(2)}) %collective-permute-start.34) | collective-permute-done | bytes 8224 | tf_op jit(solution)/shard_map/ppermute | solution.py:111
  163.1 3.3 %collective-permute-start.35 = (f32[16,128]{1,0:T(8,128)S(1)}, f32[16,128]{1,0:T(8,128)S(1)}, u32[]{:S(2)}, u32[]{:S(2)}) collective-permute-start(f32[16,128]{1,0:T(8,128)S(1)} %add.117), channel_id=1, source_target_pairs={{0,8},{2,10},{4,12},{6,14},{8,0},{10,2},{12,4},{14,6},{16,24},{18,... | collective-permute-start | bytes 24584 | tf_op jit(solution)/shard_map/ppermute | solution.py:111
  176.8 2.4 %collective-permute-done.37.refs_3_ = bf16[96,1536]{1,0:T(8,128)(2,1)S(1)} collective-permute-done((bf16[96,1536]{1,0:T(8,128)(2,1)S(1)}, bf16[96,1536]{1,0:T(8,128)(2,1)S(1)}, u32[]{:S(2)}, u32[]{:S(2)}) %collective-permute-start.37) | collective-permute-done | bytes 294944 | tf_op jit(solution)/shard_map/ppermute | solution.py:111
  186.7 3.3 %generator_grads.1 = (f32[2048,384]{1,0:T(8,128)}, f32[128,384]{1,0:T(8,128)}) custom-call(s32[2]{0:T(128)S(1)} %copy-done.29, bf16[16,128]{1,0:T(8,128)(2,1)S(1)} %copy-done.45, bf16[256,384]{1,0:T(8,128)(2,1)S(1)} %get-tuple-element.242.kernels_ref, f32[16,384]{1,0:T(8,128)S(1)} %get-tuple-element.243.biases_ref), custom_call_target="tpu_custom_call" | custom-call | flops 402653184 | bytes 3567616 | tf_op jit(solution)/shard_map/generator_grads/pallas_call | solution.py:195
  190.2 5.0 %hyper_backward.1 = (f32[16,128]{1,0:T(8,128)}, f32[128,384]{1,0:T(8,128)}, f32[128,128]{1,0:T(8,128)}, f32[128,2048]{1,0:T(8,128)}, f32[2048,128]{1,0:T(8,128)}, /*index=5*/f32[1,128]{1,0:T(1,128)}, f32[1,128]{1,0:T(1,128)}) custom-call(s32[2]{0:T(128)S(1)} %copy-done.29, f32[16,128]{1,0:T(8,128)S(1)} %add.120.grad_ref, f32[16,128]{1,0:T(8,128)S(1)} %copy-done.34, ...), custom_call_target="tpu_custom_call" | custom-call | flops 335544320 | bytes 4929664 | tf_op jit(solution)/shard_map/hyper_backward/pallas_call | solution.py:195
  (233 shorter events, 97.0 us)
Async XLA Ops:
  7.5 17.0 %all-to-all-start = ((bf16[16,16,384]{2,1,0:T(8,128)(2,1)}), bf16[16,16,384]{2,1,0:T(8,128)(2,1)S(1)}, u32[]{:S(2)}, u32[]{:S(2)}) async-start(bf16[16,16,384]{2,1,0:T(8,128)(2,1)} %bitcast.60), calls=%async_computation | async-start | bytes 393216 | tf_op jit(solution)/shard_map/all_to_all | solution.py:1293
  26.0 9.3 %collective-permute-start.6 = (bf16[8,196,128]{2,1,0:T(8,128)(2,1)S(1)}, bf16[8,196,128]{2,1,0:T(8,128)(2,1)S(1)}, u32[]{:S(2)}, u32[]{:S(2)}) collective-permute-start(bf16[8,196,128]{2,1,0:T(8,128)(2,1)S(1)} %get-tuple-element.146), channel_id=1, source_target_pairs={{0,8},{2,10},{4,12},{6,14},{8,0},{10,2},{12,4},{14,6},{16,24},{18,... | collective-permute-start | bytes 1204232 | tf_op jit(solution)/shard_map/ppermute | solution.py:111
  27.0 10.1 %collective-permute-start.3 = (bf16[8,196,128]{2,1,0:T(8,128)(2,1)S(1)}, bf16[8,196,128]{2,1,0:T(8,128)(2,1)S(1)}, u32[]{:S(2)}, u32[]{:S(2)}) collective-permute-start(bf16[8,196,128]{2,1,0:T(8,128)(2,1)S(1)} %get-tuple-element.144), channel_id=1, source_target_pairs={{0,4},{2,6},{4,0},{6,2},{8,12},{10,14},{12,8},{14,10},{16,20},{18,... | collective-permute-start | bytes 1204232 | tf_op jit(solution)/shard_map/ppermute | solution.py:111
  27.7 9.8 %collective-permute-start = (bf16[8,196,128]{2,1,0:T(8,128)(2,1)S(1)}, bf16[8,196,128]{2,1,0:T(8,128)(2,1)S(1)}, u32[]{:S(2)}, u32[]{:S(2)}) collective-permute-start(bf16[8,196,128]{2,1,0:T(8,128)(2,1)S(1)} %get-tuple-element.142), channel_id=1, source_target_pairs={{0,2},{2,0},{4,6},{6,4},{8,10},{10,8},{12,14},{14,12},{16,18},{18,... | collective-permute-start | bytes 1204232 | tf_op jit(solution)/shard_map/ppermute | solution.py:111
  50.6 8.1 %collective-permute-start.9 = (bf16[1,196,384]{2,1,0:T(8,128)(2,1)}, bf16[1,196,384]{2,1,0:T(8,128)(2,1)}, u32[]{:S(2)}, u32[]{:S(2)}) collective-permute-start(bf16[1,196,384]{2,1,0:T(8,128)(2,1)} %pad_maximum_fusion.6), channel_id=1, source_target_pairs={{0,16},{2,18},{4,20},{6,22},{8,24},{10,26},{12,28},{14,30},{16,0},... | collective-permute-start | bytes 451592 | tf_op jit(solution)/shard_map/ppermute | solution.py:111
  73.7 19.6 %collective-permute-start.15 = (bf16[384,1024]{1,0:T(8,128)(2,1)S(1)}, bf16[384,1024]{1,0:T(8,128)(2,1)S(1)}, u32[]{:S(2)}, u32[]{:S(2)}) collective-permute-start(bf16[384,1024]{1,0:T(8,128)(2,1)S(1)} %get-tuple-element.177), channel_id=1, source_target_pairs={{0,2},{2,0},{4,6},{6,4},{8,10},{10,8},{12,14},{14,12},{16,18},{18,... | collective-permute-start | bytes 2359304 | tf_op jit(solution)/shard_map/ppermute | solution.py:111
  74.8 19.3 %collective-permute-start.16 = (bf16[384,1024]{1,0:T(8,128)(2,1)S(1)}, bf16[384,1024]{1,0:T(8,128)(2,1)S(1)}, u32[]{:S(2)}, u32[]{:S(2)}) collective-permute-start(bf16[384,1024]{1,0:T(8,128)(2,1)S(1)} %get-tuple-element.178), channel_id=1, source_target_pairs={{0,4},{2,6},{4,0},{6,2},{8,12},{10,14},{12,8},{14,10},{16,20},{18,... | collective-permute-start | bytes 2359304 | tf_op jit(solution)/shard_map/ppermute | solution.py:111
  82.6 10.3 %collective-permute-start.14 = (bf16[196,384]{1,0:T(8,128)(2,1)S(1)}, bf16[196,384]{1,0:T(8,128)(2,1)S(1)}, u32[]{:S(2)}, u32[]{:S(2)}) collective-permute-start(bf16[196,384]{1,0:T(8,128)(2,1)S(1)} %get-tuple-element.166), channel_id=1, source_target_pairs={{0,16},{2,18},{4,20},{6,22},{8,24},{10,26},{12,28},{14,30},{16,0},... | collective-permute-start | bytes 451592 | tf_op jit(solution)/shard_map/ppermute | solution.py:111
  94.2 8.4 %collective-permute-start.17 = (bf16[2,196,128]{2,1,0:T(8,128)(2,1)S(1)}, bf16[2,196,128]{2,1,0:T(8,128)(2,1)S(1)}, u32[]{:S(2)}, u32[]{:S(2)}) collective-permute-start(bf16[2,196,128]{2,1,0:T(8,128)(2,1)S(1)} %pad_maximum_fusion.7), channel_id=1, source_target_pairs={{0,8},{2,10},{4,12},{6,14},{8,0},{10,2},{12,4},{14,6},{16,24},{18,... | collective-permute-start | bytes 301064 | tf_op jit(solution)/shard_map/ppermute | solution.py:111
  101.6 7.9 %collective-permute-start.20 = (bf16[4,196,128]{2,1,0:T(8,128)(2,1)S(1)}, bf16[4,196,128]{2,1,0:T(8,128)(2,1)S(1)}, u32[]{:S(2)}, u32[]{:S(2)}) collective-permute-start(bf16[4,196,128]{2,1,0:T(8,128)(2,1)S(1)} %pad_maximum_fusion.4), channel_id=1, source_target_pairs={{0,8},{2,10},{4,12},{6,14},{8,0},{10,2},{12,4},{14,6},{16,24},{18,... | collective-permute-start | bytes 602120 | tf_op jit(solution)/shard_map/ppermute | solution.py:111
  105.0 12.4 %collective-permute-start.25 = (bf16[8,196,128]{2,1,0:T(8,128)(2,1)S(1)}, bf16[8,196,128]{2,1,0:T(8,128)(2,1)S(1)}, u32[]{:S(2)}, u32[]{:S(2)}) collective-permute-start(bf16[8,196,128]{2,1,0:T(8,128)(2,1)S(1)} %pad_maximum_fusion.2.refs_2_), channel_id=1, source_target_pairs={{0,8},{2,10},{4,12},{6,14},{8,0},{10,2},{12,4},{14,6},{16,24},{18,... | collective-permute-start | bytes 1204232 | tf_op jit(solution)/shard_map/ppermute | solution.py:111
  109.6 8.0 %collective-permute-start.24 = (bf16[8,196,128]{2,1,0:T(8,128)(2,1)S(1)}, bf16[8,196,128]{2,1,0:T(8,128)(2,1)S(1)}, u32[]{:S(2)}, u32[]{:S(2)}) collective-permute-start(bf16[8,196,128]{2,1,0:T(8,128)(2,1)S(1)} %pad_maximum_fusion.1.refs_1_), channel_id=1, source_target_pairs={{0,4},{2,6},{4,0},{6,2},{8,12},{10,14},{12,8},{14,10},{16,20},{18,... | collective-permute-start | bytes 1204232 | tf_op jit(solution)/shard_map/ppermute | solution.py:111
  110.4 9.4 %collective-permute-start.23 = (bf16[8,196,128]{2,1,0:T(8,128)(2,1)S(1)}, bf16[8,196,128]{2,1,0:T(8,128)(2,1)S(1)}, u32[]{:S(2)}, u32[]{:S(2)}) collective-permute-start(bf16[8,196,128]{2,1,0:T(8,128)(2,1)S(1)} %pad_maximum_fusion.refs_0_), channel_id=1, source_target_pairs={{0,2},{2,0},{4,6},{6,4},{8,10},{10,8},{12,14},{14,12},{16,18},{18,... | collective-permute-start | bytes 1204232 | tf_op jit(solution)/shard_map/ppermute | solution.py:111
  119.8 28.1 %collective-permute-start.27 = (bf16[192,2560]{1,0:T(8,128)(2,1)}, bf16[192,2560]{1,0:T(8,128)(2,1)}, u32[]{:S(2)}, u32[]{:S(2)}) collective-permute-start(bf16[192,2560]{1,0:T(8,128)(2,1)} %get-tuple-element.203), channel_id=1, source_target_pairs={{0,2},{2,0},{4,6},{6,4},{8,10},{10,8},{12,14},{14,12},{16,18},{18,... | collective-permute-start | bytes 2949128 | tf_op jit(solution)/shard_map/ppermute | solution.py:111
  120.2 27.7 %collective-permute-start.28 = (bf16[192,2560]{1,0:T(8,128)(2,1)}, bf16[192,2560]{1,0:T(8,128)(2,1)}, u32[]{:S(2)}, u32[]{:S(2)}) collective-permute-start(bf16[192,2560]{1,0:T(8,128)(2,1)} %get-tuple-element.204), channel_id=1, source_target_pairs={{0,4},{2,6},{4,0},{6,2},{8,12},{10,14},{12,8},{14,10},{16,20},{18,... | collective-permute-start | bytes 2949128 | tf_op jit(solution)/shard_map/ppermute | solution.py:111
  122.9 24.9 %collective-permute-start.29 = (bf16[192,2560]{1,0:T(8,128)(2,1)}, bf16[192,2560]{1,0:T(8,128)(2,1)}, u32[]{:S(2)}, u32[]{:S(2)}) collective-permute-start(bf16[192,2560]{1,0:T(8,128)(2,1)} %get-tuple-element.205), channel_id=1, source_target_pairs={{0,8},{2,10},{4,12},{6,14},{8,0},{10,2},{12,4},{14,6},{16,24},{18,... | collective-permute-start | bytes 2949128 | tf_op jit(solution)/shard_map/ppermute | solution.py:111
  128.5 19.3 %all-to-all-start.1 = ((bf16[16,18,384]{2,1,0:T(8,128)(2,1)}), bf16[16,18,384]{2,1,0:T(8,128)(2,1)}, u32[]{:S(2)}, u32[]{:S(2)}) async-start(bf16[16,18,384]{2,1,0:T(8,128)(2,1)} %copy-done.16), calls=%async_computation.1 | async-start | bytes 589824 | tf_op jit(solution)/shard_map/all_to_all | solution.py:1385
  151.6 16.4 %collective-permute-start.30 = (bf16[96,2816]{1,0:T(8,128)(2,1)S(1)}, bf16[96,2816]{1,0:T(8,128)(2,1)S(1)}, u32[]{:S(2)}, u32[]{:S(2)}) collective-permute-start(bf16[96,2816]{1,0:T(8,128)(2,1)S(1)} %get-tuple-element.212), channel_id=1, source_target_pairs={{0,4},{2,6},{4,0},{6,2},{8,12},{10,14},{12,8},{14,10},{16,20},{18,... | collective-permute-start | bytes 1622024 | tf_op jit(solution)/shard_map/ppermute | solution.py:111
  152.0 16.0 %collective-permute-start.31 = (bf16[96,2816]{1,0:T(8,128)(2,1)S(1)}, bf16[96,2816]{1,0:T(8,128)(2,1)S(1)}, u32[]{:S(2)}, u32[]{:S(2)}) collective-permute-start(bf16[96,2816]{1,0:T(8,128)(2,1)S(1)} %get-tuple-element.213), channel_id=1, source_target_pairs={{0,2},{2,0},{4,6},{6,4},{8,10},{10,8},{12,14},{14,12},{16,18},{18,... | collective-permute-start | bytes 1622024 | tf_op jit(solution)/shard_map/ppermute | solution.py:111
  153.3 30.1 %collective-permute-start.26 = (bf16[8,196,256]{2,0,1:T(8,128)(2,1)S(1)}, bf16[8,196,256]{2,0,1:T(8,128)(2,1)S(1)}, u32[]{:S(2)}, u32[]{:S(2)}) collective-permute-start(bf16[8,196,256]{2,0,1:T(8,128)(2,1)S(1)} %copy.45), channel_id=1, source_target_pairs={{0,1},{1,0},{2,3},{3,2},{4,5},{5,4},{6,7},{7,6},{8,9},{9,8},{10,11... | collective-permute-start | bytes 2408456 | tf_op jit(solution)/shard_map/ppermute | solution.py:115
  153.4 14.6 %collective-permute-start.32 = (bf16[96,2048]{1,0:T(8,128)(2,1)S(1)}, bf16[96,2048]{1,0:T(8,128)(2,1)S(1)}, u32[]{:S(2)}, u32[]{:S(2)}) collective-permute-start(bf16[96,2048]{1,0:T(8,128)(2,1)S(1)} %get-tuple-element.214), channel_id=1, source_target_pairs={{0,8},{2,10},{4,12},{6,14},{8,0},{10,2},{12,4},{14,6},{16,24},{18,... | collective-permute-start | bytes 1179656 | tf_op jit(solution)/shard_map/ppermute | solution.py:111
  168.8 10.4 %collective-permute-start.37 = (bf16[96,1536]{1,0:T(8,128)(2,1)S(1)}, bf16[96,1536]{1,0:T(8,128)(2,1)S(1)}, u32[]{:S(2)}, u32[]{:S(2)}) collective-permute-start(bf16[96,1536]{1,0:T(8,128)(2,1)S(1)} %get-tuple-element.225), channel_id=1, source_target_pairs={{0,8},{2,10},{4,12},{6,14},{8,0},{10,2},{12,4},{14,6},{16,24},{18,... | collective-permute-start | bytes 884744 | tf_op jit(solution)/shard_map/ppermute | solution.py:111
  173.2 21.9 %collective-permute-start.36 = (bf16[48,2048]{1,0:T(8,128)(2,1)S(1)}, bf16[48,2048]{1,0:T(8,128)(2,1)S(1)}, u32[]{:S(2)}, u32[]{:S(2)}) collective-permute-start(bf16[48,2048]{1,0:T(8,128)(2,1)S(1)} %get-tuple-element.221), channel_id=1, source_target_pairs={{0,16},{2,18},{4,20},{6,22},{8,24},{10,26},{12,28},{14,30},{16,0},... | collective-permute-start | bytes 589832 | tf_op jit(solution)/shard_map/ppermute | solution.py:111
  179.8 15.3 %collective-permute-start.40 = (bf16[48,2816]{1,0:T(8,128)(2,1)S(1)}, bf16[48,2816]{1,0:T(8,128)(2,1)S(1)}, u32[]{:S(2)}, u32[]{:S(2)}) collective-permute-start(bf16[48,2816]{1,0:T(8,128)(2,1)S(1)} %get-tuple-element.233), channel_id=1, source_target_pairs={{0,16},{2,18},{4,20},{6,22},{8,24},{10,26},{12,28},{14,30},{16,0},... | collective-permute-start | bytes 811016 | tf_op jit(solution)/shard_map/ppermute | solution.py:111
  (76 other events, 413.9 us)

commit v4 on v3

--- a/solution.py
+++ b/solution.py
@@ -10,7 +10,7 @@
 HHEADS = 4
 LANES = 128
 EXTRA = 256
-EARLY = 1024
+EARLY = 896
 HBM = pltpu.HBM
 PART = 208
 
@@ -1236,6 +1236,10 @@
     )
 
 
+def in_hbm(arrays):
+    return [pltpu.with_memory_space_constraint(array, pltpu.HBM) for array in arrays]
+
+
 def after(values, *others):
     return lax.optimization_barrier((values, others))[0]
 
@@ -1302,11 +1306,24 @@
     gain_one = gain_one[None]
     gain_two = gain_two[None]
     tokens, normed_low, query, key, value, probs, attended, attn_part = attention_forward(
-        where, embed_low, swap(embed_low), pos_embed, gain_one, in_proj, out_proj
+        where,
+        embed_low,
+        swap(embed_low),
+        pltpu.with_memory_space_constraint(pos_embed, pltpu.HBM),
+        gain_one,
+        in_proj,
+        out_proj,
     )
     grad_low = cotangent[0]
     mid_stream, second_low, active_low, grad_hidden, ff_parts = feed_forward(
-        where, tokens, attn_part, swap(attn_part), gain_two, up_proj, down_proj, grad_low
+        where,
+        tokens,
+        attn_part,
+        swap(attn_part),
+        gain_two,
+        up_proj,
+        pltpu.with_memory_space_constraint(down_proj, pltpu.HBM),
+        grad_low,
     )
     ff_other = swap(ff_parts)
 
@@ -1357,7 +1374,8 @@
         sends, keeps = round_products(
             where, lefts, rights, ff_early, [XY, YX], portions, [XY, YX, ZX, ZY]
         )
-        first = after(first, (sends, early_arriving))
+        sends, keeps = early_sum(where, sends, keeps, early_arriving)
+        first = after(first, (sends, keeps))
     else:
         portions = [
             [(0, 0, 0, ff_local), (4, 6, 0, side)],
@@ -1374,17 +1392,15 @@
         early.append(block)
         late.append(hop(block, order[-1]))
     total, bias = kernel_grad(0, orders, where, band_mask, pixels, early, None, None)
-    if staged:
-        sends, keeps = early_sum(where, sends, keeps, after(early_arriving, early))
     sends, late, total = lax.optimization_barrier((sends, late, total))
     if staged:
         arriving = [hop(send, step) for send, step in zip(sends, STEPS)]
     else:
         arriving = [hop(send, order[-1]) for send, order in zip(sends, orders)]
+    own_pixels, other_pixels = pixel_grad(orders, where, band_mask, early, late, kernels)
     blocks = kernel_grad(1, orders, where, band_mask, pixels, late, total, bias)
+    blocks = after(blocks, own_pixels)
     spread_blocks = lax.all_to_all(blocks, "band", 0, 0, tiled=True)
-    early, late = after((early, late), blocks)
-    own_pixels, other_pixels = pixel_grad(orders, where, band_mask, early, late, kernels)
     grad_pixels = (own_pixels.astype(f32) + swap(other_pixels).astype(f32)).astype(bf16)
     grad_pixels = grad_pixels[:, None]
     steps = len(orders[0])

time: 197 us -> 190 us (0.964)
  starting transfers between devices: 61.5 us -> 42.2 us
  blocking collectives: 0 us -> 17.3 us
  local copies, waits for them, and re-layouts: 16.6 us -> 3.42 us
  waiting for transfers between devices: 61.1 us -> 65.5 us
  Pallas kernels: 52.6 us -> 56 us
    all_to_all x0 -> x1, blocking collectives: none -> 17.3 us  [shards(): spread_blocks = lax.all_to_all(blocks, 'band', 0, 0, tiled=True)]
    unnamed x112 -> x72, local copies, waits for them, and re-layouts: 16.3 us -> 3.2 us
    ppermute x37, starting transfers between devices: 44.9 us -> 33.1 us  [hop(): return lax.ppermute(values, 'band', [(i, i ^ step) for i in range(count)])]
    ppermute x37, waiting for transfers between devices: 44.1 us -> 52.9 us  [hop(): return lax.ppermute(values, 'band', [(i, i ^ step) for i in range(count)])]
    all_to_all x1 -> x0, starting transfers between devices: 7.53 us -> none  [shards(): spread_blocks = lax.all_to_all(blocks, 'band', 0, 0, tiled=True)]
    pallas_call x19, Pallas kernels: 49.8 us -> 54.8 us  [local_call(): pl.pallas_call(kernel, in_specs=[smem] * (1 + len(tables)) + [vmem] * len...]
    all_to_all x1 -> x0, waiting for transfers between devices: 2.87 us -> none  [shards(): spread_blocks = lax.all_to_all(blocks, 'band', 0, 0, tiled=True)]
  transfers between devices with their start and end apart: 45 -> 44, of which waited for: 31 -> 29; matrix products, arithmetic and copies ran while one was open for 1% -> 2% of each run, Pallas kernels for 18% -> 20%
where the time goes in v4:
time: 190 us; the launch traced here: 189 us
  waiting for transfers between devices  65.5 us (34%)
  Pallas kernels  56 us (29%)
  starting transfers between devices  42.2 us (22%)
  blocking collectives  17.3 us (9%)
  other arithmetic  3.5 us (2%)
  local copies, waits for them, and re-layouts  3.42 us (2%)
    pallas_call x19, Pallas kernels, local_call(): pl.pallas_call(kernel, in_specs=[smem] * (1 + len(tables)) + [vmem] * len...  54.8 us
    ppermute x37, waiting for transfers between devices, hop(): return lax.ppermute(values, 'band', [(i, i ^ step) for i in range(count)])  52.9 us
    ppermute x37, starting transfers between devices, hop(): return lax.ppermute(values, 'band', [(i, i ^ step) for i in range(count)])  33.1 us
    all_to_all x1, blocking collectives, shards(): spread_blocks = lax.all_to_all(blocks, 'band', 0, 0, tiled=True)  17.3 us
    all_to_all x1, starting transfers between devices, shards(): lax.all_to_all(slot_piece, 'band', 0, 0, tiled=True)  8.33 us
    all_to_all x1, waiting for transfers between devices, shards(): lax.all_to_all(slot_piece, 'band', 0, 0, tiled=True)  6.65 us
    ppermute x6, waiting for transfers between devices, swap(): return lax.ppermute(values, 'head', [(0, 1), (1, 0)])  6.01 us
  transfers between devices with their start and end apart: 44, of which 29 were waited for; matrix products, arithmetic and copies ran while one was open for 2% of the time, Pallas kernels for 20%

profile of v4, /device:TPU:0, one launch (start us, length us, event | category | flops | bytes accessed | tf_op | source)
XLA Modules:
  0.0 189.3 jit_solution(4264036635046270202)
XLA Ops:
  1.2 6.2 %hyper_forward.1 = (bf16[256,384]{1,0:T(8,128)(2,1)}, f32[1,384]{1,0:T(1,128)}, bf16[16,128]{1,0:T(8,128)(2,1)}, f32[16,384]{1,0:T(8,128)}, f32[4,16,16]{2,1,0:T...) custom-call(s32[2]{0:T(128)} %pad_add_fusion.where_ref, ...), custom_call_target="tpu_custom_call" | custom-call | flops 1610612736 | bytes 4427392 | tf_op jit(solution)/shard_map/hyper_forward/pallas_call | solution.py:195
  7.4 8.3 %all-to-all-start = ((bf16[16,16,384]{2,1,0:T(8,128)(2,1)}), bf16[16,16,384]{2,1,0:T(8,128)(2,1)S(1)}, u32[]{:S(2)}, u32[]{:S(2)}) async-start(bf16[16,16,384]{2,1,0:T(8,128)(2,1)} %bitcast.60), calls=%async_computation | async-start | bytes 393216 | tf_op jit(solution)/shard_map/all_to_all | solution.py:1297
  17.7 6.7 %all-to-all-done = bf16[16,16,384]{2,1,0:T(8,128)(2,1)S(1)} async-done(((bf16[16,16,384]{2,1,0:T(8,128)(2,1)}), bf16[16,16,384]{2,1,0:T(8,128)(2,1)S(1)}, u32[]{:S(2)}, u32[]{:S(2)}) %all-to-all-start) | async-done | bytes 196640 | tf_op jit(solution)/shard_map/all_to_all | solution.py:1297
  29.7 5.6 %collective-permute-done = bf16[8,196,128]{2,1,0:T(8,128)(2,1)S(1)} collective-permute-done((bf16[8,196,128]{2,1,0:T(8,128)(2,1)S(1)}, bf16[8,196,128]{2,1,0:T(8,128)(2,1)S(1)}, u32[]{:S(2)}, u32[]{:S(2)}) %collective-permute-start) | collective-permute-done | bytes 401440 | tf_op jit(solution)/shard_map/ppermute | solution.py:111
  42.1 2.5 %collective-permute-done.4 = bf16[4,196,128]{2,1,0:T(8,128)(2,1)S(1)} collective-permute-done((bf16[4,196,128]{2,1,0:T(8,128)(2,1)S(1)}, bf16[4,196,128]{2,1,0:T(8,128)(2,1)S(1)}, u32[]{:S(2)}, u32[]{:S(2)}) %collective-permute-start.4) | collective-permute-done | bytes 200736 | tf_op jit(solution)/shard_map/ppermute | solution.py:111
  46.8 2.6 %collective-permute-done.5 = bf16[2,196,128]{2,1,0:T(8,128)(2,1)S(1)} collective-permute-done((bf16[2,196,128]{2,1,0:T(8,128)(2,1)S(1)}, bf16[2,196,128]{2,1,0:T(8,128)(2,1)S(1)}, u32[]{:S(2)}, u32[]{:S(2)}) %collective-permute-start.5) | collective-permute-done | bytes 100384 | tf_op jit(solution)/shard_map/ppermute | solution.py:111
  52.6 5.8 %collective-permute-done.9 = bf16[1,196,384]{2,1,0:T(8,128)(2,1)} collective-permute-done((bf16[1,196,384]{2,1,0:T(8,128)(2,1)}, bf16[1,196,384]{2,1,0:T(8,128)(2,1)}, u32[]{:S(2)}, u32[]{:S(2)}) %collective-permute-start.9) | collective-permute-done | bytes 150560 | tf_op jit(solution)/shard_map/ppermute | solution.py:111
  61.0 2.9 %attention_forward.1 = (f32[196,768]{1,0:T(8,128)S(1)}, bf16[196,768]{1,0:T(8,128)(2,1)S(1)}, bf16[196,384]{1,0:T(8,128)(2,1)S(1)}, bf16[196,384]{1,0:T(8,128)(2...) custom-call(s32[2]{0:T(128)S(1)} %copy-done.11, ...), custom_call_target="tpu_custom_call" | custom-call | flops 580435968 | bytes 5691264 | tf_op jit(solution)/shard_map/attention_forward/pallas_call | solution.py:195
  65.7 4.7 %feed_forward.1 = (f32[196,768]{1,0:T(8,128)S(1)}, bf16[196,768]{1,0:T(8,128)(2,1)S(1)}, bf16[196,1536]{1,0:T(8,128)(2,1)S(1)}, bf16[196,1536]{1,0:T(8,128)(2,1)S(1)}, bf16[404,768]{1,0:T(8,128)(2,1)S(1)}) custom-call(s32[2]{0:T(128)S(1)} %copy-done.11, f32[196,768]{1,0:T(8,128)S(1)} %get-tuple-element.141.tokens_ref, ...), custom_call_target="tpu_custom_call" | custom-call | flops 1849688064 | bytes 8953344 | tf_op jit(solution)/shard_map/feed_forward/pallas_call | solution.py:195
  74.9 4.2 %attention_backward.1 = (bf16[196,768]{1,0:T(8,128)(2,1)}, f32[1,768]{1,0:T(1,128)S(1)}, f32[196,768]{1,0:T(8,128)S(1)}, bf16[196,768]{1,0:T(8,128)(2,1)S(1)}, b...) custom-call(s32[2]{0:T(128)S(1)} %copy-done.11, ...), custom_call_target="tpu_custom_call" | custom-call | flops 698449920 | bytes 7838592 | tf_op jit(solution)/shard_map/attention_backward/pallas_call | solution.py:195
  81.9 6.6 %round_products.1 = (bf16[192,2688]{1,0:T(8,128)(2,1)S(1)}, bf16[192,2688]{1,0:T(8,128)(2,1)S(1)}, bf16[192,2560]{1,0:T(8,128)(2,1)S(1)}, bf16[192,2688]{1,0:T(8...) custom-call(s32[2]{0:T(128)S(1)} %copy-done.11, ...), custom_call_target="tpu_custom_call" | custom-call | flops 1059717120 | bytes 9629696 | tf_op jit(solution)/shard_map/round_products/pallas_call | solution.py:195
  94.7 2.7 %collective-permute-done.21 = bf16[2,196,128]{2,1,0:T(8,128)(2,1)S(1)} collective-permute-done((bf16[2,196,128]{2,1,0:T(8,128)(2,1)S(1)}, bf16[2,196,128]{2,1,0:T(8,128)(2,1)S(1)}, u32[]{:S(2)}, u32[]{:S(2)}) %collective-permute-start.21) | collective-permute-done | bytes 100384 | tf_op jit(solution)/shard_map/ppermute | solution.py:111
  100.4 2.9 %collective-permute-done.22 = bf16[4,196,128]{2,1,0:T(8,128)(2,1)S(1)} collective-permute-done((bf16[4,196,128]{2,1,0:T(8,128)(2,1)S(1)}, bf16[4,196,128]{2,1,0:T(8,128)(2,1)S(1)}, u32[]{:S(2)}, u32[]{:S(2)}) %collective-permute-start.22) | collective-permute-done | bytes 200736 | tf_op jit(solution)/shard_map/ppermute | solution.py:111
  108.0 3.8 %kernel_grad.1 = (f32[384,256]{1,0:T(8,128)S(1)}, f32[1,384]{1,0:T(1,128)S(1)}) custom-call(s32[2]{0:T(128)S(1)} %copy-done.11, s32[16,16]{1,0:T(8,128)S(1)} %copy-done.8, bf16[16,196,256]{2,1,0:T(8,128)(2,1)S(1)} %bitcast.43, bf16[8,196,128]{2,1,0:T(8,128)(2,1)S(1)} %pad_maximum_fusion.refs_0_, bf16[8,196,128]{2,1,0:T(8,128)(2,1)S(1)} %pad_maximum_fusion.1.refs_1_, ...), custom_call_target="tpu_custom_call" | custom-call | flops 308281344 | bytes 3204608 | tf_op jit(solution)/shard_map/kernel_grad/pallas_call | solution.py:195
  114.6 3.2 %collective-permute-done.23.refs_3_.refs_0_ = bf16[8,196,128]{2,1,0:T(8,128)(2,1)S(1)} collective-permute-done((bf16[8,196,128]{2,1,0:T(8,128)(2,1)S(1)}, bf16[8,196,128]{2,1,0:T(8,128)(2,1)S(1)}, u32[]{:S(2)}, u32[]{:S(2)}) %collective-permute-start.23) | collective-permute-done | bytes 401440 | tf_op jit(solution)/shard_map/ppermute | solution.py:111
  119.8 3.9 %kernel_grad_end.1 = bf16[16,18,384]{2,1,0:T(8,128)(2,1)S(1)} custom-call(s32[2]{0:T(128)S(1)} %copy-done.11, s32[16,16]{1,0:T(8,128)S(1)} %copy-done.8, bf16[16,196,256]{2,1,0:T(8,128)(2,1)S(1)} %bitcast.44, bf16[8,196,128]{2,1,0:T(8,128)(2,1)S(1)} %collective-permute-done.23.refs_3_.refs_0_, ...), custom_call_target="tpu_custom_call" | custom-call | flops 308281344 | bytes 3425792 | tf_op jit(solution)/shard_map/kernel_grad_end/pallas_call | solution.py:195
  125.7 17.3 %all_to_all.10.blocks_ref = bf16[16,18,384]{2,1,0:T(8,128)(2,1)S(1)} all-to-all(bf16[16,18,384]{2,1,0:T(8,128)(2,1)S(1)} %kernel_grad_end.1), channel_id=1, replica_groups=mesh['band'=16,'head'=2] {'band'}, dimensions={0} | all-to-all | bytes 442368 | tf_op jit(solution)/shard_map/all_to_all | solution.py:1403
  147.6 2.6 %mix_grad.1 = (f32[16,128]{1,0:T(8,128)S(1)}, bf16[256,384]{1,0:T(8,128)(2,1)S(1)}, f32[16,384]{1,0:T(8,128)S(1)}) custom-call(s32[2]{0:T(128)S(1)} %copy-done.11, s32[1,16]{1,0:T(1,128)S(1)} %bitcast.55, bf16[16,18,384]{2,1,0:T(8,128)(2,1)S(1)} %all_to_all.10.blocks_ref, bf16[2048,384]{1,0:T(8,128)(2,1)S(1)} %bitcast.49, bf16[128,384]{1,0:T(8,128)(2,1)S(1)} %copy-done.12), custom_call_target="tpu_custom_call" | custom-call | flops 402653184 | bytes 2121728 | tf_op jit(solution)/shard_map/mix_grad/pallas_call | solution.py:195
  153.1 3.0 %collective-permute-done.34 = f32[16,128]{1,0:T(8,128)S(1)} collective-permute-done((f32[16,128]{1,0:T(8,128)S(1)}, f32[16,128]{1,0:T(8,128)S(1)}, u32[]{:S(2)}, u32[]{:S(2)}) %collective-permute-start.34) | collective-permute-done | bytes 8224 | tf_op jit(solution)/shard_map/ppermute | solution.py:111
  156.1 2.3 %collective-permute-start.35 = (f32[16,128]{1,0:T(8,128)S(1)}, f32[16,128]{1,0:T(8,128)S(1)}, u32[]{:S(2)}, u32[]{:S(2)}) collective-permute-start(f32[16,128]{1,0:T(8,128)S(1)} %add.117), channel_id=1, source_target_pairs={{0,8},{2,10},{4,12},{6,14},{8,0},{10,2},{12,4},{14,6},{16,24},{18,... | collective-permute-start | bytes 24584 | tf_op jit(solution)/shard_map/ppermute | solution.py:111
  165.4 2.5 %collective-permute-done.38.refs_4_ = bf16[96,640]{1,0:T(8,128)(2,1)S(1)} collective-permute-done((bf16[96,640]{1,0:T(8,128)(2,1)S(1)}, bf16[96,640]{1,0:T(8,128)(2,1)S(1)}, u32[]{:S(2)}, u32[]{:S(2)}) %collective-permute-start.38) | collective-permute-done | bytes 122912 | tf_op jit(solution)/shard_map/ppermute | solution.py:111
  168.8 4.4 %collective-permute-done.37.refs_3_ = bf16[96,1792]{1,0:T(8,128)(2,1)S(1)} collective-permute-done((bf16[96,1792]{1,0:T(8,128)(2,1)S(1)}, bf16[96,1792]{1,0:T(8,128)(2,1)S(1)}, u32[]{:S(2)}, u32[]{:S(2)}) %collective-permute-start.37) | collective-permute-done | bytes 344096 | tf_op jit(solution)/shard_map/ppermute | solution.py:111
  179.3 3.3 %generator_grads.1 = (f32[2048,384]{1,0:T(8,128)}, f32[128,384]{1,0:T(8,128)}) custom-call(s32[2]{0:T(128)S(1)} %copy-done.11, bf16[16,128]{1,0:T(8,128)(2,1)S(1)} %copy-done.26, bf16[256,384]{1,0:T(8,128)(2,1)S(1)} %get-tuple-element.228.kernels_ref, f32[16,384]{1,0:T(8,128)S(1)} %get-tuple-element.229.biases_ref), custom_call_target="tpu_custom_call" | custom-call | flops 402653184 | bytes 3567616 | tf_op jit(solution)/shard_map/generator_grads/pallas_call | solution.py:195
  182.8 5.0 %hyper_backward.1 = (f32[16,128]{1,0:T(8,128)}, f32[128,384]{1,0:T(8,128)}, f32[128,128]{1,0:T(8,128)}, f32[128,2048]{1,0:T(8,128)}, f32[2048,128]{1,0:T(8,128)}, /*index=5*/f32[1,128]{1,0:T(1,128)}, f32[1,128]{1,0:T(1,128)}) custom-call(s32[2]{0:T(128)S(1)} %copy-done.11, f32[16,128]{1,0:T(8,128)S(1)} %add.120.grad_ref, f32[16,128]{1,0:T(8,128)S(1)} %copy-done.16, ...), custom_call_target="tpu_custom_call" | custom-call | flops 335544320 | bytes 4929664 | tf_op jit(solution)/shard_map/hyper_backward/pallas_call | solution.py:195
  (192 shorter events, 74.9 us)
Async XLA Ops:
  7.4 17.0 %all-to-all-start = ((bf16[16,16,384]{2,1,0:T(8,128)(2,1)}), bf16[16,16,384]{2,1,0:T(8,128)(2,1)S(1)}, u32[]{:S(2)}, u32[]{:S(2)}) async-start(bf16[16,16,384]{2,1,0:T(8,128)(2,1)} %bitcast.60), calls=%async_computation | async-start | bytes 393216 | tf_op jit(solution)/shard_map/all_to_all | solution.py:1297
  25.9 9.3 %collective-permute-start = (bf16[8,196,128]{2,1,0:T(8,128)(2,1)S(1)}, bf16[8,196,128]{2,1,0:T(8,128)(2,1)S(1)}, u32[]{:S(2)}, u32[]{:S(2)}) collective-permute-start(bf16[8,196,128]{2,1,0:T(8,128)(2,1)S(1)} %get-tuple-element.135), channel_id=1, source_target_pairs={{0,2},{2,0},{4,6},{6,4},{8,10},{10,8},{12,14},{14,12},{16,18},{18,... | collective-permute-start | bytes 1204232 | tf_op jit(solution)/shard_map/ppermute | solution.py:111
  26.9 11.2 %collective-permute-start.3 = (bf16[8,196,128]{2,1,0:T(8,128)(2,1)S(1)}, bf16[8,196,128]{2,1,0:T(8,128)(2,1)S(1)}, u32[]{:S(2)}, u32[]{:S(2)}) collective-permute-start(bf16[8,196,128]{2,1,0:T(8,128)(2,1)S(1)} %get-tuple-element.137), channel_id=1, source_target_pairs={{0,4},{2,6},{4,0},{6,2},{8,12},{10,14},{12,8},{14,10},{16,20},{18,... | collective-permute-start | bytes 1204232 | tf_op jit(solution)/shard_map/ppermute | solution.py:111
  27.4 10.9 %collective-permute-start.6 = (bf16[8,196,128]{2,1,0:T(8,128)(2,1)S(1)}, bf16[8,196,128]{2,1,0:T(8,128)(2,1)S(1)}, u32[]{:S(2)}, u32[]{:S(2)}) collective-permute-start(bf16[8,196,128]{2,1,0:T(8,128)(2,1)S(1)} %get-tuple-element.139), channel_id=1, source_target_pairs={{0,8},{2,10},{4,12},{6,14},{8,0},{10,2},{12,4},{14,6},{16,24},{18,... | collective-permute-start | bytes 1204232 | tf_op jit(solution)/shard_map/ppermute | solution.py:111
  38.2 6.4 %collective-permute-start.4 = (bf16[4,196,128]{2,1,0:T(8,128)(2,1)S(1)}, bf16[4,196,128]{2,1,0:T(8,128)(2,1)S(1)}, u32[]{:S(2)}, u32[]{:S(2)}) collective-permute-start(bf16[4,196,128]{2,1,0:T(8,128)(2,1)S(1)} %get-tuple-element.286), channel_id=1, source_target_pairs={{0,8},{2,10},{4,12},{6,14},{8,0},{10,2},{12,4},{14,6},{16,24},{18,... | collective-permute-start | bytes 602120 | tf_op jit(solution)/shard_map/ppermute | solution.py:111
  50.3 8.1 %collective-permute-start.9 = (bf16[1,196,384]{2,1,0:T(8,128)(2,1)}, bf16[1,196,384]{2,1,0:T(8,128)(2,1)}, u32[]{:S(2)}, u32[]{:S(2)}) collective-permute-start(bf16[1,196,384]{2,1,0:T(8,128)(2,1)} %pad_maximum_fusion.6), channel_id=1, source_target_pairs={{0,16},{2,18},{4,20},{6,22},{8,24},{10,26},{12,28},{14,30},{16,0},... | collective-permute-start | bytes 451592 | tf_op jit(solution)/shard_map/ppermute | solution.py:111
  72.4 17.6 %collective-permute-start.15 = (bf16[384,896]{1,0:T(8,128)(2,1)S(1)}, bf16[384,896]{1,0:T(8,128)(2,1)S(1)}, u32[]{:S(2)}, u32[]{:S(2)}) collective-permute-start(bf16[384,896]{1,0:T(8,128)(2,1)S(1)} %get-tuple-element.171), channel_id=1, source_target_pairs={{0,2},{2,0},{4,6},{6,4},{8,10},{10,8},{12,14},{14,12},{16,18},{18,... | collective-permute-start | bytes 2064392 | tf_op jit(solution)/shard_map/ppermute | solution.py:111
  74.3 17.2 %collective-permute-start.16 = (bf16[384,896]{1,0:T(8,128)(2,1)S(1)}, bf16[384,896]{1,0:T(8,128)(2,1)S(1)}, u32[]{:S(2)}, u32[]{:S(2)}) collective-permute-start(bf16[384,896]{1,0:T(8,128)(2,1)S(1)} %get-tuple-element.172), channel_id=1, source_target_pairs={{0,4},{2,6},{4,0},{6,2},{8,12},{10,14},{12,8},{14,10},{16,20},{18,... | collective-permute-start | bytes 2064392 | tf_op jit(solution)/shard_map/ppermute | solution.py:111
  81.8 10.8 %collective-permute-start.14 = (bf16[196,384]{1,0:T(8,128)(2,1)S(1)}, bf16[196,384]{1,0:T(8,128)(2,1)S(1)}, u32[]{:S(2)}, u32[]{:S(2)}) collective-permute-start(bf16[196,384]{1,0:T(8,128)(2,1)S(1)} %get-tuple-element.159), channel_id=1, source_target_pairs={{0,16},{2,18},{4,20},{6,22},{8,24},{10,26},{12,28},{14,30},{16,0},... | collective-permute-start | bytes 451592 | tf_op jit(solution)/shard_map/ppermute | solution.py:111
  98.5 7.2 %collective-permute-start.20 = (bf16[4,196,128]{2,1,0:T(8,128)(2,1)S(1)}, bf16[4,196,128]{2,1,0:T(8,128)(2,1)S(1)}, u32[]{:S(2)}, u32[]{:S(2)}) collective-permute-start(bf16[4,196,128]{2,1,0:T(8,128)(2,1)S(1)} %pad_maximum_fusion.4), channel_id=1, source_target_pairs={{0,8},{2,10},{4,12},{6,14},{8,0},{10,2},{12,4},{14,6},{16,24},{18,... | collective-permute-start | bytes 602120 | tf_op jit(solution)/shard_map/ppermute | solution.py:111
  100.0 7.9 %collective-permute-start.18 = (bf16[4,196,128]{2,1,0:T(8,128)(2,1)S(1)}, bf16[4,196,128]{2,1,0:T(8,128)(2,1)S(1)}, u32[]{:S(2)}, u32[]{:S(2)}) collective-permute-start(bf16[4,196,128]{2,1,0:T(8,128)(2,1)S(1)} %pad_maximum_fusion.3), channel_id=1, source_target_pairs={{0,4},{2,6},{4,0},{6,2},{8,12},{10,14},{12,8},{14,10},{16,20},{18,... | collective-permute-start | bytes 602120 | tf_op jit(solution)/shard_map/ppermute | solution.py:111
  103.4 9.7 %collective-permute-start.25 = (bf16[8,196,128]{2,1,0:T(8,128)(2,1)S(1)}, bf16[8,196,128]{2,1,0:T(8,128)(2,1)S(1)}, u32[]{:S(2)}, u32[]{:S(2)}) collective-permute-start(bf16[8,196,128]{2,1,0:T(8,128)(2,1)S(1)} %pad_maximum_fusion.2.refs_2_), channel_id=1, source_target_pairs={{0,8},{2,10},{4,12},{6,14},{8,0},{10,2},{12,4},{14,6},{16,24},{18,... | collective-permute-start | bytes 1204232 | tf_op jit(solution)/shard_map/ppermute | solution.py:111
  105.7 8.9 %collective-permute-start.24 = (bf16[8,196,128]{2,1,0:T(8,128)(2,1)S(1)}, bf16[8,196,128]{2,1,0:T(8,128)(2,1)S(1)}, u32[]{:S(2)}, u32[]{:S(2)}) collective-permute-start(bf16[8,196,128]{2,1,0:T(8,128)(2,1)S(1)} %pad_maximum_fusion.1.refs_1_), channel_id=1, source_target_pairs={{0,4},{2,6},{4,0},{6,2},{8,12},{10,14},{12,8},{14,10},{16,20},{18,... | collective-permute-start | bytes 1204232 | tf_op jit(solution)/shard_map/ppermute | solution.py:111
  108.0 9.9 %collective-permute-start.23 = (bf16[8,196,128]{2,1,0:T(8,128)(2,1)S(1)}, bf16[8,196,128]{2,1,0:T(8,128)(2,1)S(1)}, u32[]{:S(2)}, u32[]{:S(2)}) collective-permute-start(bf16[8,196,128]{2,1,0:T(8,128)(2,1)S(1)} %pad_maximum_fusion.refs_0_), channel_id=1, source_target_pairs={{0,2},{2,0},{4,6},{6,4},{8,10},{10,8},{12,14},{14,12},{16,18},{18,... | collective-permute-start | bytes 1204232 | tf_op jit(solution)/shard_map/ppermute | solution.py:111
  117.8 25.1 %collective-permute-start.27 = (bf16[192,2688]{1,0:T(8,128)(2,1)S(1)}, bf16[192,2688]{1,0:T(8,128)(2,1)S(1)}, u32[]{:S(2)}, u32[]{:S(2)}) collective-permute-start(bf16[192,2688]{1,0:T(8,128)(2,1)S(1)} %get-tuple-element.186), channel_id=1, source_target_pairs={{0,2},{2,0},{4,6},{6,4},{8,10},{10,8},{12,14},{14,12},{16,18},{18,... | collective-permute-start | bytes 3096584 | tf_op jit(solution)/shard_map/ppermute | solution.py:111
  117.8 25.1 %collective-permute-start.28 = (bf16[192,2688]{1,0:T(8,128)(2,1)S(1)}, bf16[192,2688]{1,0:T(8,128)(2,1)S(1)}, u32[]{:S(2)}, u32[]{:S(2)}) collective-permute-start(bf16[192,2688]{1,0:T(8,128)(2,1)S(1)} %get-tuple-element.187), channel_id=1, source_target_pairs={{0,4},{2,6},{4,0},{6,2},{8,12},{10,14},{12,8},{14,10},{16,20},{18,... | collective-permute-start | bytes 3096584 | tf_op jit(solution)/shard_map/ppermute | solution.py:111
  119.3 23.7 %collective-permute-start.29 = (bf16[192,2560]{1,0:T(8,128)(2,1)S(1)}, bf16[192,2560]{1,0:T(8,128)(2,1)S(1)}, u32[]{:S(2)}, u32[]{:S(2)}) collective-permute-start(bf16[192,2560]{1,0:T(8,128)(2,1)S(1)} %get-tuple-element.188), channel_id=1, source_target_pairs={{0,8},{2,10},{4,12},{6,14},{8,0},{10,2},{12,4},{14,6},{16,24},{18,... | collective-permute-start | bytes 2949128 | tf_op jit(solution)/shard_map/ppermute | solution.py:111
  144.2 15.9 %collective-permute-start.30 = (bf16[96,3072]{1,0:T(8,128)(2,1)S(1)}, bf16[96,3072]{1,0:T(8,128)(2,1)S(1)}, u32[]{:S(2)}, u32[]{:S(2)}) collective-permute-start(bf16[96,3072]{1,0:T(8,128)(2,1)S(1)} %get-tuple-element.198), channel_id=1, source_target_pairs={{0,4},{2,6},{4,0},{6,2},{8,12},{10,14},{12,8},{14,10},{16,20},{18,... | collective-permute-start | bytes 1769480 | tf_op jit(solution)/shard_map/ppermute | solution.py:111
  145.3 14.8 %collective-permute-start.31 = (bf16[96,3072]{1,0:T(8,128)(2,1)S(1)}, bf16[96,3072]{1,0:T(8,128)(2,1)S(1)}, u32[]{:S(2)}, u32[]{:S(2)}) collective-permute-start(bf16[96,3072]{1,0:T(8,128)(2,1)S(1)} %get-tuple-element.199), channel_id=1, source_target_pairs={{0,2},{2,0},{4,6},{6,4},{8,10},{10,8},{12,14},{14,12},{16,18},{18,... | collective-permute-start | bytes 1769480 | tf_op jit(solution)/shard_map/ppermute | solution.py:111
  146.5 28.8 %collective-permute-start.26 = (bf16[8,196,256]{2,0,1:T(8,128)(2,1)S(1)}, bf16[8,196,256]{2,0,1:T(8,128)(2,1)S(1)}, u32[]{:S(2)}, u32[]{:S(2)}) collective-permute-start(bf16[8,196,256]{2,0,1:T(8,128)(2,1)S(1)} %copy.45), channel_id=1, source_target_pairs={{0,1},{1,0},{2,3},{3,2},{4,5},{5,4},{6,7},{7,6},{8,9},{9,8},{10,11... | collective-permute-start | bytes 2408456 | tf_op jit(solution)/shard_map/ppermute | solution.py:115
  146.6 13.5 %collective-permute-start.32 = (bf16[96,1792]{1,0:T(8,128)(2,1)S(1)}, bf16[96,1792]{1,0:T(8,128)(2,1)S(1)}, u32[]{:S(2)}, u32[]{:S(2)}) collective-permute-start(bf16[96,1792]{1,0:T(8,128)(2,1)S(1)} %get-tuple-element.200), channel_id=1, source_target_pairs={{0,8},{2,10},{4,12},{6,14},{8,0},{10,2},{12,4},{14,6},{16,24},{18,... | collective-permute-start | bytes 1032200 | tf_op jit(solution)/shard_map/ppermute | solution.py:111
  160.9 12.3 %collective-permute-start.37 = (bf16[96,1792]{1,0:T(8,128)(2,1)S(1)}, bf16[96,1792]{1,0:T(8,128)(2,1)S(1)}, u32[]{:S(2)}, u32[]{:S(2)}) collective-permute-start(bf16[96,1792]{1,0:T(8,128)(2,1)S(1)} %get-tuple-element.211), channel_id=1, source_target_pairs={{0,8},{2,10},{4,12},{6,14},{8,0},{10,2},{12,4},{14,6},{16,24},{18,... | collective-permute-start | bytes 1032200 | tf_op jit(solution)/shard_map/ppermute | solution.py:111
  164.8 23.0 %collective-permute-start.36 = (bf16[48,1792]{1,0:T(8,128)(2,1)S(1)}, bf16[48,1792]{1,0:T(8,128)(2,1)S(1)}, u32[]{:S(2)}, u32[]{:S(2)}) collective-permute-start(bf16[48,1792]{1,0:T(8,128)(2,1)S(1)} %get-tuple-element.207), channel_id=1, source_target_pairs={{0,16},{2,18},{4,20},{6,22},{8,24},{10,26},{12,28},{14,30},{16,0},... | collective-permute-start | bytes 516104 | tf_op jit(solution)/shard_map/ppermute | solution.py:111
  173.9 13.9 %collective-permute-start.40 = (bf16[48,3072]{1,0:T(8,128)(2,1)S(1)}, bf16[48,3072]{1,0:T(8,128)(2,1)S(1)}, u32[]{:S(2)}, u32[]{:S(2)}) collective-permute-start(bf16[48,3072]{1,0:T(8,128)(2,1)S(1)} %get-tuple-element.219), channel_id=1, source_target_pairs={{0,16},{2,18},{4,20},{6,22},{8,24},{10,26},{12,28},{14,30},{16,0},... | collective-permute-start | bytes 884744 | tf_op jit(solution)/shard_map/ppermute | solution.py:111
  (55 other events, 319.1 us)

commit v5 on v4

--- a/solution.py
+++ b/solution.py
@@ -908,6 +908,7 @@
 
 STEPS = (1, 2, 4, 8)
 XY, YX, ZX, ZY = (8, 4, 2, 1), (8, 4, 1, 2), (8, 2, 1, 4), (8, 1, 2, 4)
+XZ, YZ = (8, 2, 4, 1), (8, 1, 4, 2)
 
 
 def product_scratch(lefts, uses):
@@ -977,7 +978,7 @@
 
 def round_products(where, lefts, rights, early, early_orders, portions, orders):
     early_of = {0: 1, 1: 0}
-    groups = [(0,), (1,), (2, 3)]
+    groups = [(0, 1), (2, 3), (4, 5)]
     uses = sorted(
         {
             (piece[0], order)
@@ -1092,29 +1093,30 @@
 def second_sum(where, keeps, arriving, early_width, widths):
     quarter = keeps[0].shape[0]
     pair = quarter // 2
-    wa, wb, wc, wd = widths
+    starts = [early_width, early_width + 2 * widths[0]] + [0] * 4
+    starts[2:4] = [early_width, early_width + 2 * widths[2]]
+    starts[4:] = [0, 2 * widths[4]]
+    rounds = [(0, (0, 5)), (0, (2, 4)), (2 * early_width, (1, 3))]
 
     def kernel(where_ref, *refs):
         keep_refs, arriving_refs = refs[:3], refs[3:6]
-        send_y, send_x, send_z, keep_y, keep_x, keep_z = refs[6:]
+        sends, kept = refs[6:9], refs[9:]
         totals = [k[...].astype(f32) + a[...].astype(f32) for k, a in zip(keep_refs, arriving_refs)]
         for e, g in ((0, 1), (1, 0)):
             at = slice(e * early_width, (e + 1) * early_width)
-            keep_z[:, at] = totals[g][:pair, :early_width]
-            send_z[:, at] = totals[g][pair:, :early_width].astype(bf16)
-        for total, start, width, keep, send, place in (
-            (totals[0], early_width, wa, keep_y, send_y, 0),
-            (totals[2], 2 * wc, wd, keep_y, send_y, 2 * wa),
-            (totals[1], early_width, wb, keep_x, send_x, 0),
-            (totals[2], 0, wc, keep_x, send_x, 2 * wb),
-        ):
-            for k in range(2):
-                rows = slice(k * pair, (k + 1) * pair)
-                at = slice(place + k * width, place + (k + 1) * width)
-                keep[:, at] = total[rows, start : start + width]
-                send[:, at] = total[rows, start + width : start + 2 * width].astype(bf16)
-
-    shapes = [(pair, 2 * (wa + wd)), (pair, 2 * (wb + wc)), (pair, 2 * early_width)]
+            kept[2][:, at] = totals[g][:pair, :early_width]
+            sends[2][:, at] = totals[g][pair:, :early_width].astype(bf16)
+        for (place, group), keep, send in zip(rounds, kept, sends):
+            for c in group:
+                total, start, width = totals[c // 2], starts[c], widths[c]
+                for k in range(2):
+                    rows = slice(k * pair, (k + 1) * pair)
+                    at = slice(place + k * width, place + (k + 1) * width)
+                    keep[:, at] = total[rows, start : start + width]
+                    send[:, at] = total[rows, start + width : start + 2 * width].astype(bf16)
+                place += 2 * width
+
+    shapes = [(pair, place + 2 * sum(widths[c] for c in group)) for place, group in rounds]
     outs = local_call(
         kernel,
         where,
@@ -1130,24 +1132,29 @@
 def third_sum(where, keeps, arriving, early_width, widths):
     pair = keeps[0].shape[0]
     rows = pair // 2
-    wa, wb, wc, wd = widths
+    place_in = {0: (0, 0), 5: (0, 2 * widths[0]), 2: (1, 0), 4: (1, 2 * widths[2])}
+    place_in[1] = (2, 2 * early_width)
+    place_in[3] = (2, 2 * early_width + 2 * widths[1])
+    rounds = [(0, 2), (4, 1), (5, 3)]
 
     def kernel(where_ref, *refs):
         keep_refs, arriving_refs = refs[:3], refs[3:6]
-        send_e, send_ab, send_c, send_d, keep_e, keep_ab, keep_c, keep_d = refs[6:]
-        y, x, z = (k[...] + a[...].astype(f32) for k, a in zip(keep_refs, arriving_refs))
-        keep_e[...] = z[:rows]
-        send_e[...] = z[rows:].astype(bf16)
-        for total, start, width, keep, send, place in (
-            (y, 0, wa, keep_ab, send_ab, 0),
-            (x, 0, wb, keep_ab, send_ab, wa),
-            (x, 2 * wb, wc, keep_c, send_c, 0),
-            (y, 2 * wa, wd, keep_d, send_d, 0),
-        ):
-            keep[:, place : place + width] = total[:, start : start + width]
-            send[:, place : place + width] = total[:, start + width : start + 2 * width].astype(bf16)
-
-    shapes = [(rows, 2 * early_width), (pair, wa + wb), (pair, wc), (pair, wd)]
+        sends, kept = refs[6:10], refs[10:]
+        totals = [k[...] + a[...].astype(f32) for k, a in zip(keep_refs, arriving_refs)]
+        kept[0][...] = totals[2][:rows, : 2 * early_width]
+        sends[0][...] = totals[2][rows:, : 2 * early_width].astype(bf16)
+        for group, keep, send in zip(rounds, kept[1:], sends[1:]):
+            place = 0
+            for c in group:
+                (g, start), width = place_in[c], widths[c]
+                at = slice(place, place + width)
+                keep[:, at] = totals[g][:, start : start + width]
+                send[:, at] = totals[g][:, start + width : start + 2 * width].astype(bf16)
+                place += width
+
+    shapes = [(rows, 2 * early_width)] + [
+        (pair, sum(widths[c] for c in group)) for group in rounds
+    ]
     outs = local_call(
         kernel,
         where,
@@ -1200,17 +1207,18 @@
         up_out[:, :early_width] = first[:, :early_width]
         down_out[:, :early_width] = first[:, early_width:]
         up_out[:, early_width:] = total[:, :rest]
-        b = rest + 256
-        down_out[:, early_width:] = total[:, b : b + rest]
-        in_out[0, :, :256] = total[:, rest:b]
-        at = b + rest
-        in_out[0, :, 256:] = total[:, at : at + half_width - 256]
-        at += half_width - 256
-        in_out[1] = total[:, at : at + half_width]
-        in_out[2] = total[:, at + half_width : at + 2 * half_width]
-        at += 2 * half_width
+        down_out[:, early_width:] = total[:, rest : 2 * rest]
+        at = 2 * rest
+        in_out[1, :, half_width - 256 :] = total[:, at : at + 256]
+        in_out[2] = total[:, at + 256 : at + 256 + half_width]
+        at += 256 + half_width
+        in_out[0, :, :256] = total[:, at : at + 256]
+        at += 256
         out_out[...] = total[:, at : at + half_width]
-        extra = total[:, at + half_width :].T
+        extra = total[:, at + half_width : at + half_width + EXTRA].T
+        b = at + half_width + EXTRA
+        in_out[0, :, 256:] = total[:, b : b + half_width - 256]
+        in_out[1, :, : half_width - 256] = total[:, b + half_width - 256 :]
         pos_out[...] = total[:, at + half_width : at + half_width + patches]
         one_out[...] = extra[patches : patches + 1]
         two_out[...] = extra[patches + 1 : patches + 2]
@@ -1364,18 +1372,18 @@
     side = EXTRA // 2
     if staged:
         portions = [
-            [(0, 0, early_width, ff_local - early_width), (2, 2, 0, 256)],
-            [(1, 1, early_width, ff_local - early_width)]
-            + [(2, 2, 256, half_width - 256), (2, 3, 0, half_width - 256)],
+            [(0, 0, early_width, ff_local - early_width)],
+            [(2, 2, 0, 256)],
+            [(1, 1, early_width, ff_local - early_width)],
+            [(2, 2, 256, half_width - 256), (2, 3, 0, half_width - 256)],
             [(2, 3, half_width - 256, 256), (2, 4, 0, half_width)],
             [(3, 5, 0, half_width), (4, 6, 0, EXTRA)],
         ]
         widths = [sum(piece[3] for piece in portion) for portion in portions]
         sends, keeps = round_products(
-            where, lefts, rights, ff_early, [XY, YX], portions, [XY, YX, ZX, ZY]
+            where, lefts, rights, ff_early, [XY, YX], portions, [XY, XZ, YX, YZ, ZX, ZY]
         )
-        sends, keeps = early_sum(where, sends, keeps, early_arriving)
-        first = after(first, (sends, keeps))
+        first = after(first, (sends, early_arriving))
     else:
         portions = [
             [(0, 0, 0, ff_local), (4, 6, 0, side)],
@@ -1392,6 +1400,8 @@
         early.append(block)
         late.append(hop(block, order[-1]))
     total, bias = kernel_grad(0, orders, where, band_mask, pixels, early, None, None)
+    if staged:
+        sends, keeps = early_sum(where, sends, keeps, after(early_arriving, early))
     sends, late, total = lax.optimization_barrier((sends, late, total))
     if staged:
         arriving = [hop(send, step) for send, step in zip(sends, STEPS)]
@@ -1415,7 +1425,7 @@
             else:
                 arriving = [hop(send, order[-2 - t]) for send, order in zip(sends, orders)]
         elif t == 0:
-            sends, keeps = second_sum(where, keeps, arriving, early_width, widths)
+            sends, keeps = second_sum(where, in_hbm(keeps), arriving, early_width, widths)
             arriving = [hop(send, step) for send, step in zip(sends, (2, 1, 4))]
         elif t == 1:
             sends, keeps = third_sum(where, keeps, arriving, early_width, widths)

time: 190 us -> 189 us (level)
  starting transfers between devices: 42.2 us -> 60.2 us
  blocking collectives: 17.3 us -> 0 us
  waiting for transfers between devices: 65.5 us -> 61.5 us
  Pallas kernels: 56 us -> 59.8 us
    all_to_all x1 -> x0, blocking collectives: 17.3 us -> none  [shards(): spread_blocks = lax.all_to_all(blocks, 'band', 0, 0, tiled=True)]
    ppermute x37, waiting for transfers between devices: 52.9 us -> 37.2 us  [hop(): return lax.ppermute(values, 'band', [(i, i ^ step) for i in range(count)])]
    ppermute x37, starting transfers between devices: 33.1 us -> 47.6 us  [hop(): return lax.ppermute(values, 'band', [(i, i ^ step) for i in range(count)])]
    all_to_all x0 -> x1, waiting for transfers between devices: none -> 10.1 us  [shards(): spread_blocks = lax.all_to_all(blocks, 'band', 0, 0, tiled=True)]
    all_to_all x0 -> x1, starting transfers between devices: none -> 3.77 us  [shards(): spread_blocks = lax.all_to_all(blocks, 'band', 0, 0, tiled=True)]
    pallas_call x19, Pallas kernels: 54.8 us -> 57.1 us  [local_call(): pl.pallas_call(kernel, in_specs=[smem] * (1 + len(tables)) + [vmem] * len...]
  transfers between devices with their start and end apart: 44 -> 45, of which waited for: 29 -> 25; matrix products, arithmetic and copies ran while one was open for 2% -> 1% of each run, Pallas kernels for 20% -> 23%
where the time goes in v5:
time: 189 us; the launch traced here: 188 us
  waiting for transfers between devices  61.5 us (33%)
  starting transfers between devices  60.2 us (32%)
  Pallas kernels  59.8 us (32%)
  other arithmetic  3.52 us (2%)
  local copies, waits for them, and re-layouts  2.04 us (1%)
    pallas_call x19, Pallas kernels, local_call(): pl.pallas_call(kernel, in_specs=[smem] * (1 + len(tables)) + [vmem] * len...  57.1 us
    ppermute x37, starting transfers between devices, hop(): return lax.ppermute(values, 'band', [(i, i ^ step) for i in range(count)])  47.6 us
    ppermute x37, waiting for transfers between devices, hop(): return lax.ppermute(values, 'band', [(i, i ^ step) for i in range(count)])  37.2 us
    all_to_all x1, waiting for transfers between devices, shards(): spread_blocks = lax.all_to_all(blocks, 'band', 0, 0, tiled=True)  10.1 us
    all_to_all x1, starting transfers between devices, shards(): lax.all_to_all(slot_piece, 'band', 0, 0, tiled=True)  8.33 us
    all_to_all x1, waiting for transfers between devices, shards(): lax.all_to_all(slot_piece, 'band', 0, 0, tiled=True)  8.03 us
    ppermute x6, waiting for transfers between devices, swap(): return lax.ppermute(values, 'head', [(0, 1), (1, 0)])  6.22 us
  transfers between devices with their start and end apart: 45, of which 25 were waited for; matrix products, arithmetic and copies ran while one was open for 1% of the time, Pallas kernels for 23%

profile of v5, /device:TPU:0, one launch (start us, length us, event | category | flops | bytes accessed | tf_op | source)
XLA Modules:
  0.0 188.5 jit_solution(15328656862561382688)
XLA Ops:
  1.2 6.3 %hyper_forward.1 = (bf16[256,384]{1,0:T(8,128)(2,1)}, f32[1,384]{1,0:T(1,128)}, bf16[16,128]{1,0:T(8,128)(2,1)}, f32[16,384]{1,0:T(8,128)}, f32[4,16,16]{2,1,0:T...) custom-call(s32[2]{0:T(128)} %pad_add_fusion.where_ref, ...), custom_call_target="tpu_custom_call" | custom-call | flops 1610612736 | bytes 4427392 | tf_op jit(solution)/shard_map/hyper_forward/pallas_call | solution.py:195
  7.5 8.3 %all-to-all-start = ((bf16[16,16,384]{2,1,0:T(8,128)(2,1)}), bf16[16,16,384]{2,1,0:T(8,128)(2,1)S(1)}, u32[]{:S(2)}, u32[]{:S(2)}) async-start(bf16[16,16,384]{2,1,0:T(8,128)(2,1)} %bitcast.60), calls=%async_computation | async-start | bytes 393216 | tf_op jit(solution)/shard_map/all_to_all | solution.py:1305
  16.5 8.0 %all-to-all-done = bf16[16,16,384]{2,1,0:T(8,128)(2,1)S(1)} async-done(((bf16[16,16,384]{2,1,0:T(8,128)(2,1)}), bf16[16,16,384]{2,1,0:T(8,128)(2,1)S(1)}, u32[]{:S(2)}, u32[]{:S(2)}) %all-to-all-start) | async-done | bytes 196640 | tf_op jit(solution)/shard_map/all_to_all | solution.py:1305
  29.8 5.5 %collective-permute-done.6 = bf16[8,196,128]{2,1,0:T(8,128)(2,1)S(1)} collective-permute-done((bf16[8,196,128]{2,1,0:T(8,128)(2,1)S(1)}, bf16[8,196,128]{2,1,0:T(8,128)(2,1)S(1)}, u32[]{:S(2)}, u32[]{:S(2)}) %collective-permute-start.6) | collective-permute-done | bytes 401440 | tf_op jit(solution)/shard_map/ppermute | solution.py:111
  50.6 2.8 %collective-permute-start.9 = (bf16[1,196,384]{2,1,0:T(8,128)(2,1)}, bf16[1,196,384]{2,1,0:T(8,128)(2,1)}, u32[]{:S(2)}, u32[]{:S(2)}) collective-permute-start(bf16[1,196,384]{2,1,0:T(8,128)(2,1)} %pad_maximum_fusion.6), channel_id=1, source_target_pairs={{0,16},{2,18},{4,20},{6,22},{8,24},{10,26},{12,28},{14,30},{16,0},... | collective-permute-start | bytes 451592 | tf_op jit(solution)/shard_map/ppermute | solution.py:111
  53.4 5.2 %collective-permute-done.9 = bf16[1,196,384]{2,1,0:T(8,128)(2,1)} collective-permute-done((bf16[1,196,384]{2,1,0:T(8,128)(2,1)}, bf16[1,196,384]{2,1,0:T(8,128)(2,1)}, u32[]{:S(2)}, u32[]{:S(2)}) %collective-permute-start.9) | collective-permute-done | bytes 150560 | tf_op jit(solution)/shard_map/ppermute | solution.py:111
  61.3 2.9 %attention_forward.1 = (f32[196,768]{1,0:T(8,128)S(1)}, bf16[196,768]{1,0:T(8,128)(2,1)S(1)}, bf16[196,384]{1,0:T(8,128)(2,1)S(1)}, bf16[196,384]{1,0:T(8,128)(2...) custom-call(s32[2]{0:T(128)S(1)} %copy-done.14, ...), custom_call_target="tpu_custom_call" | custom-call | flops 580435968 | bytes 5691264 | tf_op jit(solution)/shard_map/attention_forward/pallas_call | solution.py:195
  66.0 4.6 %feed_forward.1 = (f32[196,768]{1,0:T(8,128)S(1)}, bf16[196,768]{1,0:T(8,128)(2,1)S(1)}, bf16[196,1536]{1,0:T(8,128)(2,1)S(1)}, bf16[196,1536]{1,0:T(8,128)(2,1)S(1)}, bf16[404,768]{1,0:T(8,128)(2,1)S(1)}) custom-call(s32[2]{0:T(128)S(1)} %copy-done.14, f32[196,768]{1,0:T(8,128)S(1)} %get-tuple-element.143.tokens_ref, ...), custom_call_target="tpu_custom_call" | custom-call | flops 1849688064 | bytes 8953344 | tf_op jit(solution)/shard_map/feed_forward/pallas_call | solution.py:195
  74.7 4.2 %attention_backward.1 = (bf16[196,768]{1,0:T(8,128)(2,1)}, f32[1,768]{1,0:T(1,128)S(1)}, f32[196,768]{1,0:T(8,128)S(1)}, bf16[196,768]{1,0:T(8,128)(2,1)S(1)}, b...) custom-call(s32[2]{0:T(128)S(1)} %copy-done.14, ...), custom_call_target="tpu_custom_call" | custom-call | flops 698449920 | bytes 7838592 | tf_op jit(solution)/shard_map/attention_backward/pallas_call | solution.py:195
  82.9 4.8 %round_products.1 = (bf16[192,2688]{1,0:T(8,128)(2,1)}, bf16[192,2688]{1,0:T(8,128)(2,1)}, bf16[192,2560]{1,0:T(8,128)(2,1)}, bf16[192,2688]{1,0:T(8,128)(2,1)S(...) custom-call(s32[2]{0:T(128)S(1)} %copy-done.14, bf16[196,768]{1,0:T(8,128)(2,1)S(1)} %get-tuple-element.147.refs_0_, ...), custom_call_target="tpu_custom_call" | custom-call | flops 1059717120 | bytes 9629696 | tf_op jit(solution)/shard_map/round_products/pallas_call | solution.py:195
  87.7 4.1 %collective-permute-done.14 = bf16[196,384]{1,0:T(8,128)(2,1)S(1)} collective-permute-done((bf16[196,384]{1,0:T(8,128)(2,1)S(1)}, bf16[196,384]{1,0:T(8,128)(2,1)S(1)}, u32[]{:S(2)}, u32[]{:S(2)}) %collective-permute-start.14) | collective-permute-done | bytes 150560 | tf_op jit(solution)/shard_map/ppermute | solution.py:111
  107.1 2.6 %collective-permute-start.23 = (bf16[8,196,128]{2,1,0:T(8,128)(2,1)S(1)}, bf16[8,196,128]{2,1,0:T(8,128)(2,1)S(1)}, u32[]{:S(2)}, u32[]{:S(2)}) collective-permute-start(bf16[8,196,128]{2,1,0:T(8,128)(2,1)S(1)} %pad_maximum_fusion.refs_0_), channel_id=1, source_target_pairs={{0,2},{2,0},{4,6},{6,4},{8,10},{10,8},{12,14},{14,12},{16,18},{18,... | collective-permute-start | bytes 1204232 | tf_op jit(solution)/shard_map/ppermute | solution.py:111
  109.7 2.6 %early_sum.1 = (bf16[192,2688]{1,0:T(8,128)(2,1)}, bf16[192,2688]{1,0:T(8,128)(2,1)S(1)}, bf16[192,2688]{1,0:T(8,128)(2,1)}, bf16[192,2688]{1,0:T(8,128)(2,1)S(1)}) custom-call(s32[2]{0:T(128)S(1)} %copy-done.14, bf16[192,2688]{1,0:T(8,128)(2,1)} %get-tuple-element.169.refs_0_, ...), custom_call_target="tpu_custom_call", output_to_operand_aliasing={{0}: (1, {}), {1}: (2, {}), {2}: (3, {}), {3}: (4, {})} | custom-call | tf_op jit(solution)/shard_map/early_sum/pallas_call | solution.py:1075
  112.4 4.5 %kernel_grad.1 = (f32[384,256]{1,0:T(8,128)S(1)}, f32[1,384]{1,0:T(1,128)S(1)}) custom-call(s32[2]{0:T(128)S(1)} %copy-done.14, s32[16,16]{1,0:T(8,128)S(1)} %copy-done.11, bf16[16,196,256]{2,1,0:T(8,128)(2,1)S(1)} %bitcast.43, bf16[8,196,128]{2,1,0:T(8,128)(2,1)S(1)} %pad_maximum_fusion.refs_0_, bf16[8,196,128]{2,1,0:T(8,128)(2,1)S(1)} %pad_maximum_fusion.1.refs_1_, ...), custom_call_target="tpu_custom_call" | custom-call | flops 308281344 | bytes 3204608 | tf_op jit(solution)/shard_map/kernel_grad/pallas_call | solution.py:195
  119.3 3.0 %collective-permute-start.29 = (bf16[192,2560]{1,0:T(8,128)(2,1)}, bf16[192,2560]{1,0:T(8,128)(2,1)}, u32[]{:S(2)}, u32[]{:S(2)}) collective-permute-start(bf16[192,2560]{1,0:T(8,128)(2,1)} %get-tuple-element.192), channel_id=1, source_target_pairs={{0,8},{2,10},{4,12},{6,14},{8,0},{10,2},{12,4},{14,6},{16,24},{18,... | collective-permute-start | bytes 2949128 | tf_op jit(solution)/shard_map/ppermute | solution.py:111
  122.3 5.0 %kernel_grad_end.1 = bf16[16,18,384]{2,1,0:T(8,128)(2,1)} custom-call(s32[2]{0:T(128)S(1)} %copy-done.14, s32[16,16]{1,0:T(8,128)S(1)} %copy-done.11, bf16[16,196,256]{2,1,0:T(8,128)(2,1)S(1)} %bitcast.44, bf16[8,196,128]{2,1,0:T(8,128)(2,1)S(1)} %collective-permute-done.23.refs_3_.refs_0_, bf16[8,196,128]{2,1,0:T(8,128)(2,1)S(1)} %collective-permute-done.24.refs_4_.refs_1_, ...), custom_call_target="tpu_custom_call" | custom-call | flops 308281344 | bytes 3425792 | tf_op jit(solution)/shard_map/kernel_grad_end/pallas_call | solution.py:195
  129.4 3.8 %all-to-all-start.1 = ((bf16[16,18,384]{2,1,0:T(8,128)(2,1)}), bf16[16,18,384]{2,1,0:T(8,128)(2,1)S(1)}, u32[]{:S(2)}, u32[]{:S(2)}) async-start(bf16[16,18,384]{2,1,0:T(8,128)(2,1)} %kernel_grad_end.1), calls=%async_computation.1 | async-start | bytes 589824 | tf_op jit(solution)/shard_map/all_to_all | solution.py:1413
  133.5 10.1 %all-to-all-done.1.blocks_ref = bf16[16,18,384]{2,1,0:T(8,128)(2,1)S(1)} async-done(((bf16[16,18,384]{2,1,0:T(8,128)(2,1)}), bf16[16,18,384]{2,1,0:T(8,128)(2,1)S(1)}, u32[]{:S(2)}, u32[]{:S(2)}) %all-to-all-start.1) | async-done | bytes 221216 | tf_op jit(solution)/shard_map/all_to_all | solution.py:1413
  143.6 3.5 %second_sum.1 = (bf16[96,2560]{1,0:T(8,128)(2,1)S(1)}, bf16[96,2560]{1,0:T(8,128)(2,1)S(1)}, bf16[96,2816]{1,0:T(8,128)(2,1)S(1)}, f32[96,2560]{1,0:T(8,128)S(1)...) custom-call(s32[2]{0:T(128)S(1)} %copy-done.14, bf16[192,2688]{1,0:T(8,128)(2,1)} %copy-done.1, ...), custom_call_target="tpu_custom_call" | custom-call | bytes 10665984 | tf_op jit(solution)/shard_map/second_sum/pallas_call | solution.py:195
  149.4 2.6 %mix_grad.1 = (f32[16,128]{1,0:T(8,128)S(1)}, bf16[256,384]{1,0:T(8,128)(2,1)S(1)}, f32[16,384]{1,0:T(8,128)S(1)}) custom-call(s32[2]{0:T(128)S(1)} %copy-done.14, s32[1,16]{1,0:T(1,128)S(1)} %bitcast.55, bf16[16,18,384]{2,1,0:T(8,128)(2,1)S(1)} %all-to-all-done.1.blocks_ref, bf16[2048,384]{1,0:T(8,128)(2,1)S(1)} %bitcast.49, bf16[128,384]{1,0:T(8,128)(2,1)S(1)} %copy-done.15), custom_call_target="tpu_custom_call" | custom-call | flops 402653184 | bytes 2121728 | tf_op jit(solution)/shard_map/mix_grad/pallas_call | solution.py:195
  158.9 2.6 %collective-permute-done.35 = f32[16,128]{1,0:T(8,128)S(1)} collective-permute-done((f32[16,128]{1,0:T(8,128)S(1)}, f32[16,128]{1,0:T(8,128)S(1)}, u32[]{:S(2)}, u32[]{:S(2)}) %collective-permute-start.35) | collective-permute-done | bytes 8224 | tf_op jit(solution)/shard_map/ppermute | solution.py:111
  171.2 2.7 %collective-permute-start.40 = (bf16[48,3072]{1,0:T(8,128)(2,1)S(1)}, bf16[48,3072]{1,0:T(8,128)(2,1)S(1)}, u32[]{:S(2)}, u32[]{:S(2)}) collective-permute-start(bf16[48,3072]{1,0:T(8,128)(2,1)S(1)} %get-tuple-element.223), channel_id=1, source_target_pairs={{0,16},{2,18},{4,20},{6,22},{8,24},{10,26},{12,28},{14,30},{16,0},... | collective-permute-start | bytes 884744 | tf_op jit(solution)/shard_map/ppermute | solution.py:111
  177.9 3.3 %generator_grads.1 = (f32[2048,384]{1,0:T(8,128)}, f32[128,384]{1,0:T(8,128)}) custom-call(s32[2]{0:T(128)S(1)} %copy-done.14, bf16[16,128]{1,0:T(8,128)(2,1)S(1)} %copy-done.29, bf16[256,384]{1,0:T(8,128)(2,1)S(1)} %get-tuple-element.232.kernels_ref, f32[16,384]{1,0:T(8,128)S(1)} %get-tuple-element.233.biases_ref), custom_call_target="tpu_custom_call" | custom-call | flops 402653184 | bytes 3567616 | tf_op jit(solution)/shard_map/generator_grads/pallas_call | solution.py:195
  181.4 5.0 %hyper_backward.1 = (f32[16,128]{1,0:T(8,128)}, f32[128,384]{1,0:T(8,128)}, f32[128,128]{1,0:T(8,128)}, f32[128,2048]{1,0:T(8,128)}, f32[2048,128]{1,0:T(8,128)}, /*index=5*/f32[1,128]{1,0:T(1,128)}, f32[1,128]{1,0:T(1,128)}) custom-call(s32[2]{0:T(128)S(1)} %copy-done.14, f32[16,128]{1,0:T(8,128)S(1)} %add.120.grad_ref, f32[16,128]{1,0:T(8,128)S(1)} %copy-done.19, ...), custom_call_target="tpu_custom_call" | custom-call | flops 335544320 | bytes 4929664 | tf_op jit(solution)/shard_map/hyper_backward/pallas_call | solution.py:195
  (201 shorter events, 79.0 us)
Async XLA Ops:
  7.5 17.0 %all-to-all-start = ((bf16[16,16,384]{2,1,0:T(8,128)(2,1)}), bf16[16,16,384]{2,1,0:T(8,128)(2,1)S(1)}, u32[]{:S(2)}, u32[]{:S(2)}) async-start(bf16[16,16,384]{2,1,0:T(8,128)(2,1)} %bitcast.60), calls=%async_computation | async-start | bytes 393216 | tf_op jit(solution)/shard_map/all_to_all | solution.py:1305
  26.0 9.3 %collective-permute-start.6 = (bf16[8,196,128]{2,1,0:T(8,128)(2,1)S(1)}, bf16[8,196,128]{2,1,0:T(8,128)(2,1)S(1)}, u32[]{:S(2)}, u32[]{:S(2)}) collective-permute-start(bf16[8,196,128]{2,1,0:T(8,128)(2,1)S(1)} %get-tuple-element.141), channel_id=1, source_target_pairs={{0,8},{2,10},{4,12},{6,14},{8,0},{10,2},{12,4},{14,6},{16,24},{18,... | collective-permute-start | bytes 1204232 | tf_op jit(solution)/shard_map/ppermute | solution.py:111
  27.1 10.1 %collective-permute-start.3 = (bf16[8,196,128]{2,1,0:T(8,128)(2,1)S(1)}, bf16[8,196,128]{2,1,0:T(8,128)(2,1)S(1)}, u32[]{:S(2)}, u32[]{:S(2)}) collective-permute-start(bf16[8,196,128]{2,1,0:T(8,128)(2,1)S(1)} %get-tuple-element.139), channel_id=1, source_target_pairs={{0,4},{2,6},{4,0},{6,2},{8,12},{10,14},{12,8},{14,10},{16,20},{18,... | collective-permute-start | bytes 1204232 | tf_op jit(solution)/shard_map/ppermute | solution.py:111
  27.7 9.8 %collective-permute-start = (bf16[8,196,128]{2,1,0:T(8,128)(2,1)S(1)}, bf16[8,196,128]{2,1,0:T(8,128)(2,1)S(1)}, u32[]{:S(2)}, u32[]{:S(2)}) collective-permute-start(bf16[8,196,128]{2,1,0:T(8,128)(2,1)S(1)} %get-tuple-element.137), channel_id=1, source_target_pairs={{0,2},{2,0},{4,6},{6,4},{8,10},{10,8},{12,14},{14,12},{16,18},{18,... | collective-permute-start | bytes 1204232 | tf_op jit(solution)/shard_map/ppermute | solution.py:111
  50.6 8.1 %collective-permute-start.9 = (bf16[1,196,384]{2,1,0:T(8,128)(2,1)}, bf16[1,196,384]{2,1,0:T(8,128)(2,1)}, u32[]{:S(2)}, u32[]{:S(2)}) collective-permute-start(bf16[1,196,384]{2,1,0:T(8,128)(2,1)} %pad_maximum_fusion.6), channel_id=1, source_target_pairs={{0,16},{2,18},{4,20},{6,22},{8,24},{10,26},{12,28},{14,30},{16,0},... | collective-permute-start | bytes 451592 | tf_op jit(solution)/shard_map/ppermute | solution.py:111
  72.7 19.2 %collective-permute-start.15 = (bf16[384,896]{1,0:T(8,128)(2,1)S(1)}, bf16[384,896]{1,0:T(8,128)(2,1)S(1)}, u32[]{:S(2)}, u32[]{:S(2)}) collective-permute-start(bf16[384,896]{1,0:T(8,128)(2,1)S(1)} %get-tuple-element.172), channel_id=1, source_target_pairs={{0,2},{2,0},{4,6},{6,4},{8,10},{10,8},{12,14},{14,12},{16,18},{18,... | collective-permute-start | bytes 2064392 | tf_op jit(solution)/shard_map/ppermute | solution.py:111
  73.7 18.1 %collective-permute-start.16 = (bf16[384,896]{1,0:T(8,128)(2,1)S(1)}, bf16[384,896]{1,0:T(8,128)(2,1)S(1)}, u32[]{:S(2)}, u32[]{:S(2)}) collective-permute-start(bf16[384,896]{1,0:T(8,128)(2,1)S(1)} %get-tuple-element.173), channel_id=1, source_target_pairs={{0,4},{2,6},{4,0},{6,2},{8,12},{10,14},{12,8},{14,10},{16,20},{18,... | collective-permute-start | bytes 2064392 | tf_op jit(solution)/shard_map/ppermute | solution.py:111
  81.5 10.3 %collective-permute-start.14 = (bf16[196,384]{1,0:T(8,128)(2,1)S(1)}, bf16[196,384]{1,0:T(8,128)(2,1)S(1)}, u32[]{:S(2)}, u32[]{:S(2)}) collective-permute-start(bf16[196,384]{1,0:T(8,128)(2,1)S(1)} %get-tuple-element.161), channel_id=1, source_target_pairs={{0,16},{2,18},{4,20},{6,22},{8,24},{10,26},{12,28},{14,30},{16,0},... | collective-permute-start | bytes 451592 | tf_op jit(solution)/shard_map/ppermute | solution.py:111
  91.9 7.8 %collective-permute-start.17 = (bf16[2,196,128]{2,1,0:T(8,128)(2,1)S(1)}, bf16[2,196,128]{2,1,0:T(8,128)(2,1)S(1)}, u32[]{:S(2)}, u32[]{:S(2)}) collective-permute-start(bf16[2,196,128]{2,1,0:T(8,128)(2,1)S(1)} %pad_maximum_fusion.7), channel_id=1, source_target_pairs={{0,8},{2,10},{4,12},{6,14},{8,0},{10,2},{12,4},{14,6},{16,24},{18,... | collective-permute-start | bytes 301064 | tf_op jit(solution)/shard_map/ppermute | solution.py:111
  99.7 7.4 %collective-permute-start.18 = (bf16[4,196,128]{2,1,0:T(8,128)(2,1)S(1)}, bf16[4,196,128]{2,1,0:T(8,128)(2,1)S(1)}, u32[]{:S(2)}, u32[]{:S(2)}) collective-permute-start(bf16[4,196,128]{2,1,0:T(8,128)(2,1)S(1)} %pad_maximum_fusion.3), channel_id=1, source_target_pairs={{0,4},{2,6},{4,0},{6,2},{8,12},{10,14},{12,8},{14,10},{16,20},{18,... | collective-permute-start | bytes 602120 | tf_op jit(solution)/shard_map/ppermute | solution.py:111
  102.6 14.3 %collective-permute-start.25 = (bf16[8,196,128]{2,1,0:T(8,128)(2,1)S(1)}, bf16[8,196,128]{2,1,0:T(8,128)(2,1)S(1)}, u32[]{:S(2)}, u32[]{:S(2)}) collective-permute-start(bf16[8,196,128]{2,1,0:T(8,128)(2,1)S(1)} %pad_maximum_fusion.2.refs_2_), channel_id=1, source_target_pairs={{0,8},{2,10},{4,12},{6,14},{8,0},{10,2},{12,4},{14,6},{16,24},{18,... | collective-permute-start | bytes 1204232 | tf_op jit(solution)/shard_map/ppermute | solution.py:111
  104.7 12.1 %collective-permute-start.24 = (bf16[8,196,128]{2,1,0:T(8,128)(2,1)S(1)}, bf16[8,196,128]{2,1,0:T(8,128)(2,1)S(1)}, u32[]{:S(2)}, u32[]{:S(2)}) collective-permute-start(bf16[8,196,128]{2,1,0:T(8,128)(2,1)S(1)} %pad_maximum_fusion.1.refs_1_), channel_id=1, source_target_pairs={{0,4},{2,6},{4,0},{6,2},{8,12},{10,14},{12,8},{14,10},{16,20},{18,... | collective-permute-start | bytes 1204232 | tf_op jit(solution)/shard_map/ppermute | solution.py:111
  107.1 9.8 %collective-permute-start.23 = (bf16[8,196,128]{2,1,0:T(8,128)(2,1)S(1)}, bf16[8,196,128]{2,1,0:T(8,128)(2,1)S(1)}, u32[]{:S(2)}, u32[]{:S(2)}) collective-permute-start(bf16[8,196,128]{2,1,0:T(8,128)(2,1)S(1)} %pad_maximum_fusion.refs_0_), channel_id=1, source_target_pairs={{0,2},{2,0},{4,6},{6,4},{8,10},{10,8},{12,14},{14,12},{16,18},{18,... | collective-permute-start | bytes 1204232 | tf_op jit(solution)/shard_map/ppermute | solution.py:111
  116.9 26.7 %collective-permute-start.27 = (bf16[192,2688]{1,0:T(8,128)(2,1)}, bf16[192,2688]{1,0:T(8,128)(2,1)}, u32[]{:S(2)}, u32[]{:S(2)}) collective-permute-start(bf16[192,2688]{1,0:T(8,128)(2,1)} %get-tuple-element.190), channel_id=1, source_target_pairs={{0,2},{2,0},{4,6},{6,4},{8,10},{10,8},{12,14},{14,12},{16,18},{18,... | collective-permute-start | bytes 3096584 | tf_op jit(solution)/shard_map/ppermute | solution.py:111
  119.3 24.3 %collective-permute-start.28 = (bf16[192,2688]{1,0:T(8,128)(2,1)}, bf16[192,2688]{1,0:T(8,128)(2,1)}, u32[]{:S(2)}, u32[]{:S(2)}) collective-permute-start(bf16[192,2688]{1,0:T(8,128)(2,1)} %get-tuple-element.191), channel_id=1, source_target_pairs={{0,4},{2,6},{4,0},{6,2},{8,12},{10,14},{12,8},{14,10},{16,20},{18,... | collective-permute-start | bytes 3096584 | tf_op jit(solution)/shard_map/ppermute | solution.py:111
  119.3 24.3 %collective-permute-start.29 = (bf16[192,2560]{1,0:T(8,128)(2,1)}, bf16[192,2560]{1,0:T(8,128)(2,1)}, u32[]{:S(2)}, u32[]{:S(2)}) collective-permute-start(bf16[192,2560]{1,0:T(8,128)(2,1)} %get-tuple-element.192), channel_id=1, source_target_pairs={{0,8},{2,10},{4,12},{6,14},{8,0},{10,2},{12,4},{14,6},{16,24},{18,... | collective-permute-start | bytes 2949128 | tf_op jit(solution)/shard_map/ppermute | solution.py:111
  129.4 14.1 %all-to-all-start.1 = ((bf16[16,18,384]{2,1,0:T(8,128)(2,1)}), bf16[16,18,384]{2,1,0:T(8,128)(2,1)S(1)}, u32[]{:S(2)}, u32[]{:S(2)}) async-start(bf16[16,18,384]{2,1,0:T(8,128)(2,1)} %kernel_grad_end.1), calls=%async_computation.1 | async-start | bytes 589824 | tf_op jit(solution)/shard_map/all_to_all | solution.py:1413
  133.4 42.2 %collective-permute-start.26 = (bf16[8,196,256]{2,0,1:T(8,128)(2,1)S(1)}, bf16[8,196,256]{2,0,1:T(8,128)(2,1)S(1)}, u32[]{:S(2)}, u32[]{:S(2)}) collective-permute-start(bf16[8,196,256]{2,0,1:T(8,128)(2,1)S(1)} %copy.45), channel_id=1, source_target_pairs={{0,1},{1,0},{2,3},{3,2},{4,5},{5,4},{6,7},{7,6},{8,9},{9,8},{10,11... | collective-permute-start | bytes 2408456 | tf_op jit(solution)/shard_map/ppermute | solution.py:115
  147.1 14.3 %collective-permute-start.32 = (bf16[96,2816]{1,0:T(8,128)(2,1)S(1)}, bf16[96,2816]{1,0:T(8,128)(2,1)S(1)}, u32[]{:S(2)}, u32[]{:S(2)}) collective-permute-start(bf16[96,2816]{1,0:T(8,128)(2,1)S(1)} %get-tuple-element.204), channel_id=1, source_target_pairs={{0,8},{2,10},{4,12},{6,14},{8,0},{10,2},{12,4},{14,6},{16,24},{18,... | collective-permute-start | bytes 1622024 | tf_op jit(solution)/shard_map/ppermute | solution.py:111
  147.8 13.6 %collective-permute-start.30 = (bf16[96,2560]{1,0:T(8,128)(2,1)S(1)}, bf16[96,2560]{1,0:T(8,128)(2,1)S(1)}, u32[]{:S(2)}, u32[]{:S(2)}) collective-permute-start(bf16[96,2560]{1,0:T(8,128)(2,1)S(1)} %get-tuple-element.202), channel_id=1, source_target_pairs={{0,4},{2,6},{4,0},{6,2},{8,12},{10,14},{12,8},{14,10},{16,20},{18,... | collective-permute-start | bytes 1474568 | tf_op jit(solution)/shard_map/ppermute | solution.py:111
  148.4 13.1 %collective-permute-start.31 = (bf16[96,2560]{1,0:T(8,128)(2,1)S(1)}, bf16[96,2560]{1,0:T(8,128)(2,1)S(1)}, u32[]{:S(2)}, u32[]{:S(2)}) collective-permute-start(bf16[96,2560]{1,0:T(8,128)(2,1)S(1)} %get-tuple-element.203), channel_id=1, source_target_pairs={{0,2},{2,0},{4,6},{6,4},{8,10},{10,8},{12,14},{14,12},{16,18},{18,... | collective-permute-start | bytes 1474568 | tf_op jit(solution)/shard_map/ppermute | solution.py:111
  162.3 8.2 %collective-permute-start.37 = (bf16[96,1280]{1,0:T(8,128)(2,1)S(1)}, bf16[96,1280]{1,0:T(8,128)(2,1)S(1)}, u32[]{:S(2)}, u32[]{:S(2)}) collective-permute-start(bf16[96,1280]{1,0:T(8,128)(2,1)S(1)} %get-tuple-element.215), channel_id=1, source_target_pairs={{0,8},{2,10},{4,12},{6,14},{8,0},{10,2},{12,4},{14,6},{16,24},{18,... | collective-permute-start | bytes 737288 | tf_op jit(solution)/shard_map/ppermute | solution.py:111
  166.2 20.1 %collective-permute-start.36 = (bf16[48,1792]{1,0:T(8,128)(2,1)S(1)}, bf16[48,1792]{1,0:T(8,128)(2,1)S(1)}, u32[]{:S(2)}, u32[]{:S(2)}) collective-permute-start(bf16[48,1792]{1,0:T(8,128)(2,1)S(1)} %get-tuple-element.211), channel_id=1, source_target_pairs={{0,16},{2,18},{4,20},{6,22},{8,24},{10,26},{12,28},{14,30},{16,0},... | collective-permute-start | bytes 516104 | tf_op jit(solution)/shard_map/ppermute | solution.py:111
  171.2 15.8 %collective-permute-start.40 = (bf16[48,3072]{1,0:T(8,128)(2,1)S(1)}, bf16[48,3072]{1,0:T(8,128)(2,1)S(1)}, u32[]{:S(2)}, u32[]{:S(2)}) collective-permute-start(bf16[48,3072]{1,0:T(8,128)(2,1)S(1)} %get-tuple-element.223), channel_id=1, source_target_pairs={{0,16},{2,18},{4,20},{6,22},{8,24},{10,26},{12,28},{14,30},{16,0},... | collective-permute-start | bytes 884744 | tf_op jit(solution)/shard_map/ppermute | solution.py:111
  (60 other events, 376.1 us)

commit v6 on v5

--- a/solution.py
+++ b/solution.py
@@ -216,7 +216,7 @@
     head_size = width // HHEADS
 
     def kernel(
-        where_ref, ids_ref, mask_ref, table_ref, in_ref, out_ref, up_ref, down_ref, one_ref,
+        ids_ref, mask_ref, table_ref, in_ref, out_ref, up_ref, down_ref, one_ref,
         two_ref, gen_ref, bias_ref, piece_out, image_bias_out, mix_out, projected_out, probs_out,
         attended_out, normal_one_out, scale_one_out, hidden_out, normal_two_out, scale_two_out,
     ):
@@ -248,9 +248,7 @@
         onehot = onehot_of(ids_ref, wave_count)
         slot_mix = low_dot(onehot.astype(bf16), mix).astype(bf16)
         piece_out[...] = low_dot(kron_identity(slot_mix, piece), gen_ref[...]).astype(bf16)
-        image = lax.broadcasted_iota(jnp.int32, mask_ref.shape, 0) == where_ref[0]
-        bands = jnp.sum(jnp.where(image, mask_ref[...], 0).astype(f32), axis=0, keepdims=True)
-        waves = exact(bands, onehot.astype(f32))
+        waves = exact(mask_ref[...].astype(f32), onehot.astype(f32))
         image_bias_out[...] = exact(waves, low_dot(mix, bias_ref[...]))
 
     def shape(*dims):
@@ -258,12 +256,12 @@
 
     return local_call(
         kernel,
-        where,
-        [wave_ids],
+        wave_ids,
+        [],
         [band_mask, table, *weights, *gains, gen_rows, bias_gen],
         [
             jax.ShapeDtypeStruct((slots * piece, half_width), bf16),
-            shape(1, half_width),
+            shape(band_mask.shape[0], half_width),
             jax.ShapeDtypeStruct((wave_count, width), bf16),
             shape(wave_count, 3 * width),
             shape(HHEADS, wave_count, wave_count),
@@ -1310,7 +1308,8 @@
     embed_half = jnp.concatenate(
         [part[0] for part in scatter_sum(keeps, None, orders, arriving)], axis=1
     )
-    embed_low = (embed_half + image_bias).astype(bf16)
+    own_bias = lax.dynamic_slice_in_dim(image_bias, band_index, 1, 0)
+    embed_low = (embed_half + own_bias).astype(bf16)
     gain_one = gain_one[None]
     gain_two = gain_two[None]
     tokens, normed_low, query, key, value, probs, attended, attn_part = attention_forward(

time: 189 us -> 188 us (level)
  Pallas kernels: 59.8 us -> 56.9 us
  waiting for transfers between devices: 61.5 us -> 64.1 us
    pallas_call x19, Pallas kernels: 57.1 us -> 54.3 us  [local_call(): pl.pallas_call(kernel, in_specs=[smem] * (1 + len(tables)) + [vmem] * len...]
  transfers between devices with their start and end apart: 45 -> 45, of which waited for: 25 -> 27; matrix products, arithmetic and copies ran while one was open for 1% -> 2% of each run, Pallas kernels for 23% -> 21%
where the time goes in v6:
time: 188 us
  waiting for transfers between devices  64.1 us (34%)
  starting transfers between devices  59.7 us (32%)
  Pallas kernels  56.9 us (30%)
  other arithmetic  3 us (2%)
  local copies, waits for them, and re-layouts  2.82 us (2%)
    pallas_call x19, Pallas kernels, local_call(): pl.pallas_call(kernel, in_specs=[smem] * (1 + len(tables)) + [vmem] * len...  54.3 us
    ppermute x37, starting transfers between devices, hop(): return lax.ppermute(values, 'band', [(i, i ^ step) for i in range(count)])  47.1 us
    ppermute x37, waiting for transfers between devices, hop(): return lax.ppermute(values, 'band', [(i, i ^ step) for i in range(count)])  38.1 us
    all_to_all x1, waiting for transfers between devices, shards(): spread_blocks = lax.all_to_all(blocks, 'band', 0, 0, tiled=True)  11.8 us
    all_to_all x1, starting transfers between devices, shards(): lax.all_to_all(slot_piece, 'band', 0, 0, tiled=True)  8.33 us
    all_to_all x1, waiting for transfers between devices, shards(): lax.all_to_all(slot_piece, 'band', 0, 0, tiled=True)  7.96 us
    ppermute x6, waiting for transfers between devices, swap(): return lax.ppermute(values, 'head', [(0, 1), (1, 0)])  6.24 us
    all_to_all x1, starting transfers between devices, shards(): spread_blocks = lax.all_to_all(blocks, 'band', 0, 0, tiled=True)  3.77 us
  transfers between devices with their start and end apart: 45, of which 27 were waited for; matrix products, arithmetic and copies ran while one was open for 2% of the time, Pallas kernels for 21%

profile of v6, /device:TPU:0, one launch (start us, length us, event | category | flops | bytes accessed | tf_op | source)
XLA Modules:
  0.0 187.9 jit_solution(9414927237534213641)
XLA Ops:
  0.7 6.3 %hyper_forward.1 = (bf16[256,384]{1,0:T(8,128)(2,1)}, f32[16,384]{1,0:T(8,128)}, bf16[16,128]{1,0:T(8,128)(2,1)}, f32[16,384]{1,0:T(8,128)}, f32[4,16,16]{2,1,0:...) custom-call(s32[1,16]{1,0:T(1,128)} %bitcast.54, ...), custom_call_target="tpu_custom_call" | custom-call | flops 1610612736 | bytes 4450432 | tf_op jit(solution)/shard_map/hyper_forward/pallas_call | solution.py:195
  7.0 8.3 %all-to-all-start = ((bf16[16,16,384]{2,1,0:T(8,128)(2,1)}), bf16[16,16,384]{2,1,0:T(8,128)(2,1)S(1)}, u32[]{:S(2)}, u32[]{:S(2)}) async-start(bf16[16,16,384]{2,1,0:T(8,128)(2,1)} %bitcast.60), calls=%async_computation | async-start | bytes 393216 | tf_op jit(solution)/shard_map/all_to_all | solution.py:1303
  16.0 8.0 %all-to-all-done = bf16[16,16,384]{2,1,0:T(8,128)(2,1)S(1)} async-done(((bf16[16,16,384]{2,1,0:T(8,128)(2,1)}), bf16[16,16,384]{2,1,0:T(8,128)(2,1)S(1)}, u32[]{:S(2)}, u32[]{:S(2)}) %all-to-all-start) | async-done | bytes 196640 | tf_op jit(solution)/shard_map/all_to_all | solution.py:1303
  29.2 5.6 %collective-permute-done.6 = bf16[8,196,128]{2,1,0:T(8,128)(2,1)S(1)} collective-permute-done((bf16[8,196,128]{2,1,0:T(8,128)(2,1)S(1)}, bf16[8,196,128]{2,1,0:T(8,128)(2,1)S(1)}, u32[]{:S(2)}, u32[]{:S(2)}) %collective-permute-start.6) | collective-permute-done | bytes 401440 | tf_op jit(solution)/shard_map/ppermute | solution.py:111
  50.0 2.8 %collective-permute-start.9 = (bf16[1,196,384]{2,1,0:T(8,128)(2,1)}, bf16[1,196,384]{2,1,0:T(8,128)(2,1)}, u32[]{:S(2)}, u32[]{:S(2)}) collective-permute-start(bf16[1,196,384]{2,1,0:T(8,128)(2,1)} %pad_maximum_fusion.6), channel_id=1, source_target_pairs={{0,16},{2,18},{4,20},{6,22},{8,24},{10,26},{12,28},{14,30},{16,0},... | collective-permute-start | bytes 451592 | tf_op jit(solution)/shard_map/ppermute | solution.py:111
  53.6 4.4 %collective-permute-done.9 = bf16[1,196,384]{2,1,0:T(8,128)(2,1)} collective-permute-done((bf16[1,196,384]{2,1,0:T(8,128)(2,1)}, bf16[1,196,384]{2,1,0:T(8,128)(2,1)}, u32[]{:S(2)}, u32[]{:S(2)}) %collective-permute-start.9) | collective-permute-done | bytes 150560 | tf_op jit(solution)/shard_map/ppermute | solution.py:111
  60.8 2.9 %attention_forward.1 = (f32[196,768]{1,0:T(8,128)S(1)}, bf16[196,768]{1,0:T(8,128)(2,1)S(1)}, bf16[196,384]{1,0:T(8,128)(2,1)S(1)}, bf16[196,384]{1,0:T(8,128)(2...) custom-call(s32[2]{0:T(128)S(1)} %pad_add_fusion.where_ref, ...), custom_call_target="tpu_custom_call" | custom-call | flops 580435968 | bytes 5691264 | tf_op jit(solution)/shard_map/attention_forward/pallas_call | solution.py:195
  65.4 4.6 %feed_forward.1 = (f32[196,768]{1,0:T(8,128)S(1)}, bf16[196,768]{1,0:T(8,128)(2,1)S(1)}, bf16[196,1536]{1,0:T(8,128)(2,1)S(1)}, bf16[196,1536]{1,0:T(8,128)(2,1)S(1)}, bf16[404,768]{1,0:T(8,128)(2,1)S(1)}) custom-call(s32[2]{0:T(128)S(1)} %pad_add_fusion.where_ref, f32[196,768]{1,0:T(8,128)S(1)} %get-tuple-element.143.tokens_ref, ...), custom_call_target="tpu_custom_call" | custom-call | flops 1849688064 | bytes 8953344 | tf_op jit(solution)/shard_map/feed_forward/pallas_call | solution.py:195
  74.1 4.2 %attention_backward.1 = (bf16[196,768]{1,0:T(8,128)(2,1)}, f32[1,768]{1,0:T(1,128)S(1)}, f32[196,768]{1,0:T(8,128)S(1)}, bf16[196,768]{1,0:T(8,128)(2,1)S(1)}, b...) custom-call(s32[2]{0:T(128)S(1)} %pad_add_fusion.where_ref, ...), custom_call_target="tpu_custom_call" | custom-call | flops 698449920 | bytes 7838592 | tf_op jit(solution)/shard_map/attention_backward/pallas_call | solution.py:195
  82.4 4.8 %round_products.1 = (bf16[192,2688]{1,0:T(8,128)(2,1)}, bf16[192,2688]{1,0:T(8,128)(2,1)}, bf16[192,2560]{1,0:T(8,128)(2,1)}, bf16[192,2688]{1,0:T(8,128)(2,1)S(...) custom-call(s32[2]{0:T(128)S(1)} %pad_add_fusion.where_ref, ...), custom_call_target="tpu_custom_call" | custom-call | flops 1059717120 | bytes 9629696 | tf_op jit(solution)/shard_map/round_products/pallas_call | solution.py:195
  87.2 4.0 %collective-permute-done.14 = bf16[196,384]{1,0:T(8,128)(2,1)S(1)} collective-permute-done((bf16[196,384]{1,0:T(8,128)(2,1)S(1)}, bf16[196,384]{1,0:T(8,128)(2,1)S(1)}, u32[]{:S(2)}, u32[]{:S(2)}) %collective-permute-start.14) | collective-permute-done | bytes 150560 | tf_op jit(solution)/shard_map/ppermute | solution.py:111
  109.0 2.6 %early_sum.1 = (bf16[192,2688]{1,0:T(8,128)(2,1)}, bf16[192,2688]{1,0:T(8,128)(2,1)S(1)}, bf16[192,2688]{1,0:T(8,128)(2,1)}, bf16[192,2688]{1,0:T(8,128)(2,1)S(1)}) custom-call(s32[2]{0:T(128)S(1)} %pad_add_fusion.where_ref, bf16[192,2688]{1,0:T(8,128)(2,1)} %get-tuple-element.169.refs_0_, ...), custom_call_target="tpu_custom_call", output_to_operand_aliasing={{0}: (1, {}), {1}: (2, {}), {2}: (3, {}), {3}: (4, {})} | custom-call | tf_op jit(solution)/shard_map/early_sum/pallas_call | solution.py:1073
  111.6 3.2 %kernel_grad.1 = (f32[384,256]{1,0:T(8,128)S(1)}, f32[1,384]{1,0:T(1,128)S(1)}) custom-call(s32[2]{0:T(128)S(1)} %pad_add_fusion.where_ref, s32[16,16]{1,0:T(8,128)S(1)} %copy-done.11, bf16[16,196,256]{2,1,0:T(8,128)(2,1)S(1)} %bitcast.43, bf16[8,196,128]{2,1,0:T(8,128)(2,1)S(1)} %pad_maximum_fusion.refs_0_, ...), custom_call_target="tpu_custom_call" | custom-call | flops 308281344 | bytes 3204608 | tf_op jit(solution)/shard_map/kernel_grad/pallas_call | solution.py:195
  118.4 3.3 %collective-permute-start.29 = (bf16[192,2560]{1,0:T(8,128)(2,1)}, bf16[192,2560]{1,0:T(8,128)(2,1)}, u32[]{:S(2)}, u32[]{:S(2)}) collective-permute-start(bf16[192,2560]{1,0:T(8,128)(2,1)} %get-tuple-element.192), channel_id=1, source_target_pairs={{0,8},{2,10},{4,12},{6,14},{8,0},{10,2},{12,4},{14,6},{16,24},{18,... | collective-permute-start | bytes 2949128 | tf_op jit(solution)/shard_map/ppermute | solution.py:111
  121.6 3.5 %kernel_grad_end.1 = bf16[16,18,384]{2,1,0:T(8,128)(2,1)} custom-call(s32[2]{0:T(128)S(1)} %pad_add_fusion.where_ref, s32[16,16]{1,0:T(8,128)S(1)} %copy-done.11, bf16[16,196,256]{2,1,0:T(8,128)(2,1)S(1)} %bitcast.44, bf16[8,196,128]{2,1,0:T(8,128)(2,1)S(1)} %collective-permute-done.23.refs_3_.refs_0_, ...), custom_call_target="tpu_custom_call" | custom-call | flops 308281344 | bytes 3425792 | tf_op jit(solution)/shard_map/kernel_grad_end/pallas_call | solution.py:195
  127.2 3.8 %all-to-all-start.1 = ((bf16[16,18,384]{2,1,0:T(8,128)(2,1)}), bf16[16,18,384]{2,1,0:T(8,128)(2,1)S(1)}, u32[]{:S(2)}, u32[]{:S(2)}) async-start(bf16[16,18,384]{2,1,0:T(8,128)(2,1)} %kernel_grad_end.1), calls=%async_computation.1 | async-start | bytes 589824 | tf_op jit(solution)/shard_map/all_to_all | solution.py:1412
  131.2 11.8 %all-to-all-done.1.blocks_ref = bf16[16,18,384]{2,1,0:T(8,128)(2,1)S(1)} async-done(((bf16[16,18,384]{2,1,0:T(8,128)(2,1)}), bf16[16,18,384]{2,1,0:T(8,128)(2,1)S(1)}, u32[]{:S(2)}, u32[]{:S(2)}) %all-to-all-start.1) | async-done | bytes 221216 | tf_op jit(solution)/shard_map/all_to_all | solution.py:1412
  143.0 3.5 %second_sum.1 = (bf16[96,2560]{1,0:T(8,128)(2,1)S(1)}, bf16[96,2560]{1,0:T(8,128)(2,1)S(1)}, bf16[96,2816]{1,0:T(8,128)(2,1)S(1)}, f32[96,2560]{1,0:T(8,128)S(1)...) custom-call(s32[2]{0:T(128)S(1)} %pad_add_fusion.where_ref, bf16[192,2688]{1,0:T(8,128)(2,1)} %copy-done.1, ...), custom_call_target="tpu_custom_call" | custom-call | bytes 10665984 | tf_op jit(solution)/shard_map/second_sum/pallas_call | solution.py:195
  149.0 2.6 %mix_grad.1 = (f32[16,128]{1,0:T(8,128)S(1)}, bf16[256,384]{1,0:T(8,128)(2,1)S(1)}, f32[16,384]{1,0:T(8,128)S(1)}) custom-call(s32[2]{0:T(128)S(1)} %pad_add_fusion.where_ref, s32[1,16]{1,0:T(1,128)S(1)} %bitcast.55, bf16[16,18,384]{2,1,0:T(8,128)(2,1)S(1)} %all-to-all-done.1.blocks_ref, bf16[2048,384]{1,0:T(8,128)(2,1)S(1)} %bitcast.49, ...), custom_call_target="tpu_custom_call" | custom-call | flops 402653184 | bytes 2121728 | tf_op jit(solution)/shard_map/mix_grad/pallas_call | solution.py:195
  152.8 2.5 %collective-permute-start.34 = (f32[16,128]{1,0:T(8,128)S(1)}, f32[16,128]{1,0:T(8,128)S(1)}, u32[]{:S(2)}, u32[]{:S(2)}) collective-permute-start(f32[16,128]{1,0:T(8,128)S(1)} %add.120), channel_id=1, source_target_pairs={{0,16},{2,18},{4,20},{6,22},{8,24},{10,26},{12,28},{14,30},{16,0},... | collective-permute-start | bytes 24584 | tf_op jit(solution)/shard_map/ppermute | solution.py:111
  158.4 2.6 %collective-permute-done.35 = f32[16,128]{1,0:T(8,128)S(1)} collective-permute-done((f32[16,128]{1,0:T(8,128)S(1)}, f32[16,128]{1,0:T(8,128)S(1)}, u32[]{:S(2)}, u32[]{:S(2)}) %collective-permute-start.35) | collective-permute-done | bytes 8224 | tf_op jit(solution)/shard_map/ppermute | solution.py:111
  170.6 3.1 %collective-permute-start.40 = (bf16[48,3072]{1,0:T(8,128)(2,1)S(1)}, bf16[48,3072]{1,0:T(8,128)(2,1)S(1)}, u32[]{:S(2)}, u32[]{:S(2)}) collective-permute-start(bf16[48,3072]{1,0:T(8,128)(2,1)S(1)} %get-tuple-element.223), channel_id=1, source_target_pairs={{0,16},{2,18},{4,20},{6,22},{8,24},{10,26},{12,28},{14,30},{16,0},... | collective-permute-start | bytes 884744 | tf_op jit(solution)/shard_map/ppermute | solution.py:111
  177.4 3.3 %generator_grads.1 = (f32[2048,384]{1,0:T(8,128)}, f32[128,384]{1,0:T(8,128)}) custom-call(s32[2]{0:T(128)S(1)} %pad_add_fusion.where_ref, bf16[16,128]{1,0:T(8,128)(2,1)S(1)} %copy-done.28, bf16[256,384]{1,0:T(8,128)(2,1)S(1)} %get-tuple-element.232.kernels_ref, f32[16,384]{1,0:T(8,128)S(1)} %get-tuple-element.233.biases_ref), custom_call_target="tpu_custom_call" | custom-call | flops 402653184 | bytes 3567616 | tf_op jit(solution)/shard_map/generator_grads/pallas_call | solution.py:195
  181.1 5.0 %hyper_backward.1 = (f32[16,128]{1,0:T(8,128)}, f32[128,384]{1,0:T(8,128)}, f32[128,128]{1,0:T(8,128)}, f32[128,2048]{1,0:T(8,128)}, f32[2048,128]{1,0:T(8,128)}, /*index=5*/f32[1,128]{1,0:T(1,128)}, f32[1,128]{1,0:T(1,128)}) custom-call(s32[2]{0:T(128)S(1)} %pad_add_fusion.where_ref, f32[16,128]{1,0:T(8,128)S(1)} %add.124.grad_ref, ...), custom_call_target="tpu_custom_call" | custom-call | flops 335544320 | bytes 4929664 | tf_op jit(solution)/shard_map/hyper_backward/pallas_call | solution.py:195
  (197 shorter events, 79.9 us)
Async XLA Ops:
  7.0 17.0 %all-to-all-start = ((bf16[16,16,384]{2,1,0:T(8,128)(2,1)}), bf16[16,16,384]{2,1,0:T(8,128)(2,1)S(1)}, u32[]{:S(2)}, u32[]{:S(2)}) async-start(bf16[16,16,384]{2,1,0:T(8,128)(2,1)} %bitcast.60), calls=%async_computation | async-start | bytes 393216 | tf_op jit(solution)/shard_map/all_to_all | solution.py:1303
  25.5 9.3 %collective-permute-start.6 = (bf16[8,196,128]{2,1,0:T(8,128)(2,1)S(1)}, bf16[8,196,128]{2,1,0:T(8,128)(2,1)S(1)}, u32[]{:S(2)}, u32[]{:S(2)}) collective-permute-start(bf16[8,196,128]{2,1,0:T(8,128)(2,1)S(1)} %get-tuple-element.141), channel_id=1, source_target_pairs={{0,8},{2,10},{4,12},{6,14},{8,0},{10,2},{12,4},{14,6},{16,24},{18,... | collective-permute-start | bytes 1204232 | tf_op jit(solution)/shard_map/ppermute | solution.py:111
  26.5 10.1 %collective-permute-start.3 = (bf16[8,196,128]{2,1,0:T(8,128)(2,1)S(1)}, bf16[8,196,128]{2,1,0:T(8,128)(2,1)S(1)}, u32[]{:S(2)}, u32[]{:S(2)}) collective-permute-start(bf16[8,196,128]{2,1,0:T(8,128)(2,1)S(1)} %get-tuple-element.139), channel_id=1, source_target_pairs={{0,4},{2,6},{4,0},{6,2},{8,12},{10,14},{12,8},{14,10},{16,20},{18,... | collective-permute-start | bytes 1204232 | tf_op jit(solution)/shard_map/ppermute | solution.py:111
  27.2 9.8 %collective-permute-start = (bf16[8,196,128]{2,1,0:T(8,128)(2,1)S(1)}, bf16[8,196,128]{2,1,0:T(8,128)(2,1)S(1)}, u32[]{:S(2)}, u32[]{:S(2)}) collective-permute-start(bf16[8,196,128]{2,1,0:T(8,128)(2,1)S(1)} %get-tuple-element.137), channel_id=1, source_target_pairs={{0,2},{2,0},{4,6},{6,4},{8,10},{10,8},{12,14},{14,12},{16,18},{18,... | collective-permute-start | bytes 1204232 | tf_op jit(solution)/shard_map/ppermute | solution.py:111
  50.0 8.1 %collective-permute-start.9 = (bf16[1,196,384]{2,1,0:T(8,128)(2,1)}, bf16[1,196,384]{2,1,0:T(8,128)(2,1)}, u32[]{:S(2)}, u32[]{:S(2)}) collective-permute-start(bf16[1,196,384]{2,1,0:T(8,128)(2,1)} %pad_maximum_fusion.6), channel_id=1, source_target_pairs={{0,16},{2,18},{4,20},{6,22},{8,24},{10,26},{12,28},{14,30},{16,0},... | collective-permute-start | bytes 451592 | tf_op jit(solution)/shard_map/ppermute | solution.py:111
  72.1 19.1 %collective-permute-start.15 = (bf16[384,896]{1,0:T(8,128)(2,1)S(1)}, bf16[384,896]{1,0:T(8,128)(2,1)S(1)}, u32[]{:S(2)}, u32[]{:S(2)}) collective-permute-start(bf16[384,896]{1,0:T(8,128)(2,1)S(1)} %get-tuple-element.172), channel_id=1, source_target_pairs={{0,2},{2,0},{4,6},{6,4},{8,10},{10,8},{12,14},{14,12},{16,18},{18,... | collective-permute-start | bytes 2064392 | tf_op jit(solution)/shard_map/ppermute | solution.py:111
  73.2 18.1 %collective-permute-start.16 = (bf16[384,896]{1,0:T(8,128)(2,1)S(1)}, bf16[384,896]{1,0:T(8,128)(2,1)S(1)}, u32[]{:S(2)}, u32[]{:S(2)}) collective-permute-start(bf16[384,896]{1,0:T(8,128)(2,1)S(1)} %get-tuple-element.173), channel_id=1, source_target_pairs={{0,4},{2,6},{4,0},{6,2},{8,12},{10,14},{12,8},{14,10},{16,20},{18,... | collective-permute-start | bytes 2064392 | tf_op jit(solution)/shard_map/ppermute | solution.py:111
  80.9 10.3 %collective-permute-start.14 = (bf16[196,384]{1,0:T(8,128)(2,1)S(1)}, bf16[196,384]{1,0:T(8,128)(2,1)S(1)}, u32[]{:S(2)}, u32[]{:S(2)}) collective-permute-start(bf16[196,384]{1,0:T(8,128)(2,1)S(1)} %get-tuple-element.161), channel_id=1, source_target_pairs={{0,16},{2,18},{4,20},{6,22},{8,24},{10,26},{12,28},{14,30},{16,0},... | collective-permute-start | bytes 451592 | tf_op jit(solution)/shard_map/ppermute | solution.py:111
  91.3 7.9 %collective-permute-start.17 = (bf16[2,196,128]{2,1,0:T(8,128)(2,1)S(1)}, bf16[2,196,128]{2,1,0:T(8,128)(2,1)S(1)}, u32[]{:S(2)}, u32[]{:S(2)}) collective-permute-start(bf16[2,196,128]{2,1,0:T(8,128)(2,1)S(1)} %pad_maximum_fusion.7), channel_id=1, source_target_pairs={{0,8},{2,10},{4,12},{6,14},{8,0},{10,2},{12,4},{14,6},{16,24},{18,... | collective-permute-start | bytes 301064 | tf_op jit(solution)/shard_map/ppermute | solution.py:111
  99.2 7.4 %collective-permute-start.18 = (bf16[4,196,128]{2,1,0:T(8,128)(2,1)S(1)}, bf16[4,196,128]{2,1,0:T(8,128)(2,1)S(1)}, u32[]{:S(2)}, u32[]{:S(2)}) collective-permute-start(bf16[4,196,128]{2,1,0:T(8,128)(2,1)S(1)} %pad_maximum_fusion.3), channel_id=1, source_target_pairs={{0,4},{2,6},{4,0},{6,2},{8,12},{10,14},{12,8},{14,10},{16,20},{18,... | collective-permute-start | bytes 602120 | tf_op jit(solution)/shard_map/ppermute | solution.py:111
  102.0 12.8 %collective-permute-start.25 = (bf16[8,196,128]{2,1,0:T(8,128)(2,1)S(1)}, bf16[8,196,128]{2,1,0:T(8,128)(2,1)S(1)}, u32[]{:S(2)}, u32[]{:S(2)}) collective-permute-start(bf16[8,196,128]{2,1,0:T(8,128)(2,1)S(1)} %pad_maximum_fusion.2.refs_2_), channel_id=1, source_target_pairs={{0,8},{2,10},{4,12},{6,14},{8,0},{10,2},{12,4},{14,6},{16,24},{18,... | collective-permute-start | bytes 1204232 | tf_op jit(solution)/shard_map/ppermute | solution.py:111
  104.1 10.7 %collective-permute-start.24 = (bf16[8,196,128]{2,1,0:T(8,128)(2,1)S(1)}, bf16[8,196,128]{2,1,0:T(8,128)(2,1)S(1)}, u32[]{:S(2)}, u32[]{:S(2)}) collective-permute-start(bf16[8,196,128]{2,1,0:T(8,128)(2,1)S(1)} %pad_maximum_fusion.1.refs_1_), channel_id=1, source_target_pairs={{0,4},{2,6},{4,0},{6,2},{8,12},{10,14},{12,8},{14,10},{16,20},{18,... | collective-permute-start | bytes 1204232 | tf_op jit(solution)/shard_map/ppermute | solution.py:111
  106.7 9.2 %collective-permute-start.23 = (bf16[8,196,128]{2,1,0:T(8,128)(2,1)S(1)}, bf16[8,196,128]{2,1,0:T(8,128)(2,1)S(1)}, u32[]{:S(2)}, u32[]{:S(2)}) collective-permute-start(bf16[8,196,128]{2,1,0:T(8,128)(2,1)S(1)} %pad_maximum_fusion.refs_0_), channel_id=1, source_target_pairs={{0,2},{2,0},{4,6},{6,4},{8,10},{10,8},{12,14},{14,12},{16,18},{18,... | collective-permute-start | bytes 1204232 | tf_op jit(solution)/shard_map/ppermute | solution.py:111
  115.9 27.1 %collective-permute-start.27 = (bf16[192,2688]{1,0:T(8,128)(2,1)}, bf16[192,2688]{1,0:T(8,128)(2,1)}, u32[]{:S(2)}, u32[]{:S(2)}) collective-permute-start(bf16[192,2688]{1,0:T(8,128)(2,1)} %get-tuple-element.190), channel_id=1, source_target_pairs={{0,2},{2,0},{4,6},{6,4},{8,10},{10,8},{12,14},{14,12},{16,18},{18,... | collective-permute-start | bytes 3096584 | tf_op jit(solution)/shard_map/ppermute | solution.py:111
  118.4 24.6 %collective-permute-start.28 = (bf16[192,2688]{1,0:T(8,128)(2,1)}, bf16[192,2688]{1,0:T(8,128)(2,1)}, u32[]{:S(2)}, u32[]{:S(2)}) collective-permute-start(bf16[192,2688]{1,0:T(8,128)(2,1)} %get-tuple-element.191), channel_id=1, source_target_pairs={{0,4},{2,6},{4,0},{6,2},{8,12},{10,14},{12,8},{14,10},{16,20},{18,... | collective-permute-start | bytes 3096584 | tf_op jit(solution)/shard_map/ppermute | solution.py:111
  118.4 24.6 %collective-permute-start.29 = (bf16[192,2560]{1,0:T(8,128)(2,1)}, bf16[192,2560]{1,0:T(8,128)(2,1)}, u32[]{:S(2)}, u32[]{:S(2)}) collective-permute-start(bf16[192,2560]{1,0:T(8,128)(2,1)} %get-tuple-element.192), channel_id=1, source_target_pairs={{0,8},{2,10},{4,12},{6,14},{8,0},{10,2},{12,4},{14,6},{16,24},{18,... | collective-permute-start | bytes 2949128 | tf_op jit(solution)/shard_map/ppermute | solution.py:111
  127.2 15.8 %all-to-all-start.1 = ((bf16[16,18,384]{2,1,0:T(8,128)(2,1)}), bf16[16,18,384]{2,1,0:T(8,128)(2,1)S(1)}, u32[]{:S(2)}, u32[]{:S(2)}) async-start(bf16[16,18,384]{2,1,0:T(8,128)(2,1)} %kernel_grad_end.1), calls=%async_computation.1 | async-start | bytes 589824 | tf_op jit(solution)/shard_map/all_to_all | solution.py:1412
  131.1 43.8 %collective-permute-start.26 = (bf16[8,196,256]{2,0,1:T(8,128)(2,1)S(1)}, bf16[8,196,256]{2,0,1:T(8,128)(2,1)S(1)}, u32[]{:S(2)}, u32[]{:S(2)}) collective-permute-start(bf16[8,196,256]{2,0,1:T(8,128)(2,1)S(1)} %copy.45), channel_id=1, source_target_pairs={{0,1},{1,0},{2,3},{3,2},{4,5},{5,4},{6,7},{7,6},{8,9},{9,8},{10,11... | collective-permute-start | bytes 2408456 | tf_op jit(solution)/shard_map/ppermute | solution.py:115
  146.5 14.5 %collective-permute-start.32 = (bf16[96,2816]{1,0:T(8,128)(2,1)S(1)}, bf16[96,2816]{1,0:T(8,128)(2,1)S(1)}, u32[]{:S(2)}, u32[]{:S(2)}) collective-permute-start(bf16[96,2816]{1,0:T(8,128)(2,1)S(1)} %get-tuple-element.204), channel_id=1, source_target_pairs={{0,8},{2,10},{4,12},{6,14},{8,0},{10,2},{12,4},{14,6},{16,24},{18,... | collective-permute-start | bytes 1622024 | tf_op jit(solution)/shard_map/ppermute | solution.py:111
  147.5 13.5 %collective-permute-start.30 = (bf16[96,2560]{1,0:T(8,128)(2,1)S(1)}, bf16[96,2560]{1,0:T(8,128)(2,1)S(1)}, u32[]{:S(2)}, u32[]{:S(2)}) collective-permute-start(bf16[96,2560]{1,0:T(8,128)(2,1)S(1)} %get-tuple-element.202), channel_id=1, source_target_pairs={{0,4},{2,6},{4,0},{6,2},{8,12},{10,14},{12,8},{14,10},{16,20},{18,... | collective-permute-start | bytes 1474568 | tf_op jit(solution)/shard_map/ppermute | solution.py:111
  147.7 13.3 %collective-permute-start.31 = (bf16[96,2560]{1,0:T(8,128)(2,1)S(1)}, bf16[96,2560]{1,0:T(8,128)(2,1)S(1)}, u32[]{:S(2)}, u32[]{:S(2)}) collective-permute-start(bf16[96,2560]{1,0:T(8,128)(2,1)S(1)} %get-tuple-element.203), channel_id=1, source_target_pairs={{0,2},{2,0},{4,6},{6,4},{8,10},{10,8},{12,14},{14,12},{16,18},{18,... | collective-permute-start | bytes 1474568 | tf_op jit(solution)/shard_map/ppermute | solution.py:111
  161.8 8.1 %collective-permute-start.37 = (bf16[96,1280]{1,0:T(8,128)(2,1)S(1)}, bf16[96,1280]{1,0:T(8,128)(2,1)S(1)}, u32[]{:S(2)}, u32[]{:S(2)}) collective-permute-start(bf16[96,1280]{1,0:T(8,128)(2,1)S(1)} %get-tuple-element.215), channel_id=1, source_target_pairs={{0,8},{2,10},{4,12},{6,14},{8,0},{10,2},{12,4},{14,6},{16,24},{18,... | collective-permute-start | bytes 737288 | tf_op jit(solution)/shard_map/ppermute | solution.py:111
  165.6 20.5 %collective-permute-start.36 = (bf16[48,1792]{1,0:T(8,128)(2,1)S(1)}, bf16[48,1792]{1,0:T(8,128)(2,1)S(1)}, u32[]{:S(2)}, u32[]{:S(2)}) collective-permute-start(bf16[48,1792]{1,0:T(8,128)(2,1)S(1)} %get-tuple-element.211), channel_id=1, source_target_pairs={{0,16},{2,18},{4,20},{6,22},{8,24},{10,26},{12,28},{14,30},{16,0},... | collective-permute-start | bytes 516104 | tf_op jit(solution)/shard_map/ppermute | solution.py:111
  170.6 15.8 %collective-permute-start.40 = (bf16[48,3072]{1,0:T(8,128)(2,1)S(1)}, bf16[48,3072]{1,0:T(8,128)(2,1)S(1)}, u32[]{:S(2)}, u32[]{:S(2)}) collective-permute-start(bf16[48,3072]{1,0:T(8,128)(2,1)S(1)} %get-tuple-element.223), channel_id=1, source_target_pairs={{0,16},{2,18},{4,20},{6,22},{8,24},{10,26},{12,28},{14,30},{16,0},... | collective-permute-start | bytes 884744 | tf_op jit(solution)/shard_map/ppermute | solution.py:111
  (58 other events, 356.1 us)
